TPU v7x, 128 devices: a whole 4x4x4 slice. The times are simulated.
128 devices in a mesh: gx: 16 (over z, y), gy: 8 (over x, core).
Axes of the slice: x: 4, y: 4, z: 4, core: 2. Of those that a mesh axis runs over, the one named last changes fastest.
Arguments:
- state: float32 [512, 512, 128], P('gx', 'gy'), may hold values from -6 to 6
- syndromes: int32 [2, 512, 512], P(None, 'gx', 'gy'), may hold values from 0 to 1
- erased: int32 [2, 128, 128], P(None, 'gx', 'gy'), may hold values 0 or 1
- readers: int32 [16384, 1], P(('gx', 'gy')), may hold values from 0 to 127; in each aligned block of 128 rows (0 to 127, 128 to 255, ...) at most 2 rows name the same one
- conv_weight: float32 [9, 128, 128], replicated, may hold values from -0.1875 to 0.1875
- syndrome_table: float32 [2, 128], replicated, may hold values from -6 to 6
- erasure_vector: float32 [128], replicated, may hold values from -6 to 6
- read_weight: float32 [16384, 128], P(('gx', 'gy')), may hold values from -0.5 to 0.5
- erasure_offset: float32 [128], replicated, may hold values from -6 to 6
Outputs:
- final_state: float32 [512, 512, 128], P('gx', 'gy')
Inputs may be any that keep to these rules, and one draw needn't show every extreme that they name: `readers`: among the 128 blocks of one device no reader is named more than 2 times, a bound that some block reaches.
All inputs are finite; a program needn't handle non-finite values. No bound on the sum of `erased` on one device may be relied on, other than what follows from the above.
Results may differ from a plain program's by a relative error of at most 0.0003.
Values sent between devices are 32-bit elements; how exact they have to be, the bound alone decides.
No kernel may reach another device: no remote copies, remote signals or barrier semaphores. Data moves between devices by JAX's collectives and lax.ppermute only.
A program may use at most 64 MiB of HBM per device.

v0:
```python
import jax
import jax.numpy as jnp
from jax import lax
from jax.experimental import pallas as pl
from jax.experimental.pallas import tpu as pltpu
from jax.sharding import PartitionSpec as P


BS = 4
C = 128
TR = 32
TC = 64
HALO = 4
WIDE = TC + 2 * HALO
TALL = TR + 2 * HALO
BROWS = TALL // BS
BCOLS = WIDE // BS
GROUPS = WIDE // 8
CONV_ROWS = TR + 4
AX = ("gx", "gy")


def flat_id(z, y, x, c):
    return ((z % 4 * 4 + y % 4) * 4 + x % 4) * 2 + c


SITES = [
    (z, y, x, c) for z in range(4) for y in range(4) for x in range(4) for c in range(2)
]


def class_groups():
    groups = {}
    for z, y, x, c in SITES:
        groups.setdefault(((x + z) % 2, (y + z) % 2, c), []).append(flat_id(z, y, x, c))
    return [groups[k] for k in sorted(groups)]


def moved(dz, dy, dx):
    return [
        (flat_id(z, y, x, c), flat_id(z + dz, y + dy, x + dx, c)) for z, y, x, c in SITES
    ]


PARTNER = [(flat_id(z, y, x, c), flat_id(z, y, x, 1 - c)) for z, y, x, c in SITES]


def gather_weights(shard):
    copies = jnp.broadcast_to(shard[None], (16, C, C))
    own = lax.all_to_all(copies, AX, 0, 0, tiled=True, axis_index_groups=class_groups())
    low, high = own[:8], own[8:]
    pieces = [own]
    for step in ((0, 0, 1), (0, 1, 0), (1, 0, 0)):
        back = tuple(-s for s in step)
        pieces.append(lax.ppermute(low, AX, moved(*step)))
        pieces.append(lax.ppermute(high, AX, moved(*back)))
    pieces += [lax.ppermute(piece, AX, PARTNER) for piece in pieces]
    return pieces


def slots_of(ids):
    me = lax.axis_index("gx") * 8 + lax.axis_index("gy")

    def place(n):
        return n // 32, n // 8 % 4, n // 2 % 4, n % 2

    z, y, x, c = place(ids)
    mz, my, mx, mc = place(me)
    side = (x + z + mx + mz) % 2 + 2 * ((y + z + my + mz) % 2)
    return (((c + mc) % 2) * 4 + side) * 16 + z * 4 + y // 2 * 2 + x // 2


def split(value):
    high = value.astype(jnp.bfloat16)
    return high, (value - high.astype(jnp.float32)).astype(jnp.bfloat16)


def conv_chunk(read, weights, rows):
    highs, lows = [], []
    for a in range(3):
        high, low = split(read(a).reshape(rows * WIDE, C))
        highs.append(high)
        lows.append(low)
    left = jnp.concatenate(highs + highs + lows, axis=1)
    sums = jnp.dot(left, weights, preferred_element_type=jnp.float32)
    sums = sums.reshape(rows, WIDE, 3 * C)
    return (
        pltpu.roll(sums[:, :, :C], 1, 1)
        + sums[:, :, C : 2 * C]
        + pltpu.roll(sums[:, :, 2 * C :], WIDE - 1, 1)
    )


def first_kernel(
    state, top, bottom, right, left, taps, inputs, ext_out, pre_out, weights_out
):
    ext_out[HALO : HALO + TR, :TC] = state[...]
    ext_out[:HALO, :TC] = top[: HALO * TC].reshape(HALO, TC, C)
    ext_out[HALO + TR :, :TC] = bottom[: HALO * TC].reshape(HALO, TC, C)
    both = jnp.concatenate(
        [
            right[: TALL * HALO].reshape(TALL, HALO, C),
            left[: TALL * HALO].reshape(TALL, HALO, C),
        ],
        axis=1,
    )
    ext_out[:, TC:] = both
    for a in range(3):
        for b in range(3):
            high, low = split(taps[3 * a + b])
            cols = slice(b * C, (b + 1) * C)
            weights_out[a * C : (a + 1) * C, cols] = high
            weights_out[(3 + a) * C : (4 + a) * C, cols] = low
            weights_out[(6 + a) * C : (7 + a) * C, cols] = high
    rows = 12

    def step(i, carry):
        start = i * rows
        pre_out[pl.ds(start, rows)] = (
            conv_chunk(
                lambda a: ext_out[pl.ds(start + 1 + a, rows)], weights_out[...], rows
            )
            + inputs[pl.ds(start, rows)]
        )
        return carry

    lax.fori_loop(0, CONV_ROWS // rows, step, 0)


def group_sum(total, sub):
    near = jnp.where(sub % 2 == 0, pltpu.roll(total, 7, 0), pltpu.roll(total, 1, 0))
    total = total + near
    far = jnp.where(sub % 4 < 2, pltpu.roll(total, 6, 0), pltpu.roll(total, 2, 0))
    return total + far


def readout(sites, right, flag_a, flag_b, offset, sub):
    high, low = split(sites.reshape(32, C))
    left = jnp.concatenate(
        [jnp.concatenate([high, high], axis=1), jnp.concatenate([low, low], axis=1)],
        axis=0,
    )
    mixed = jnp.dot(left, right, preferred_element_type=jnp.float32)
    mixed = (mixed[:32] + mixed[32:]).reshape(4, 8, 2 * C)
    mixed = jnp.tanh(jnp.where(sub[None] < 4, mixed[:, :, :C], mixed[:, :, C:]))
    total = mixed[0] + mixed[1] + mixed[2] + mixed[3]
    flags = jnp.where(sub < 4, flag_a, flag_b)
    return jnp.tanh(group_sum(total, sub) * 0.0625 + flags * offset)


PIECES = (16, 8, 8, 8, 8, 8, 8) * 2


def second_kernel(
    slots, flags, inside, ext, pre, inputs, weights, offset, *rest
):
    pieces, (out, table, pairs, first, field, second, sems) = rest[:14], rest[14:]
    copies = []
    at = 0
    for i, (piece, count) in enumerate(zip(pieces, PIECES)):
        copies.append(
            pltpu.make_async_copy(piece, table.at[pl.ds(at, count)], sems.at[i])
        )
        at += count
    for copy in copies:
        copy.start()
    for copy in copies:
        copy.wait()
    sub = lax.broadcasted_iota(jnp.int32, (8, C), 0)
    shift = offset[...]

    def read_first(br, carry):
        for g in range(GROUPS):
            b = br * BCOLS + 2 * g
            high_a, low_a = split(table[slots[b]])
            high_b, low_b = split(table[slots[b + 1]])
            right = jnp.concatenate(
                [
                    jnp.concatenate([high_a, high_b], axis=1),
                    jnp.concatenate([low_a, low_b], axis=1),
                ],
                axis=0,
            )
            pairs[br * GROUPS + g] = right
            first[br, 8 * g : 8 * g + 8] = readout(
                ext[pl.ds(br * BS, BS), 8 * g : 8 * g + 8],
                right,
                flags[b].astype(jnp.float32),
                flags[b + 1].astype(jnp.float32),
                shift,
                sub,
            )
        return carry

    lax.fori_loop(0, BROWS, read_first, 0)

    def update(row, br):
        field[row + 1] = 0.5 * ext[row + HALO] + jnp.tanh(pre[row + 2] + first[br])

    column = lax.broadcasted_iota(jnp.int32, (WIDE, C), 0)

    update(-1, 0)
    update(TR, BROWS - 1)

    def update_block(br, carry):
        for r in range(BS):
            update(br * BS + r, br + 1)
        return carry

    lax.fori_loop(0, TR // BS, update_block, 0)
    field[0] = field[0] * inside[0].astype(jnp.float32)
    field[TR + 1] = field[TR + 1] * inside[1].astype(jnp.float32)
    edge = lax.broadcasted_iota(jnp.int32, (TR + 2, 8, C), 1)
    kept = jnp.where(edge < 4, inside[2].astype(jnp.float32), inside[3].astype(jnp.float32))
    field[:, TC:] = field[:, TC:] * kept

    def read_second(br, carry):
        for g in range(TC // 8):
            b = (br + 1) * BCOLS + 2 * g
            second[br, 8 * g : 8 * g + 8] = readout(
                field[pl.ds(br * BS + 1, BS), 8 * g : 8 * g + 8],
                pairs[(br + 1) * GROUPS + g],
                flags[BROWS * BCOLS + b].astype(jnp.float32),
                flags[BROWS * BCOLS + b + 1].astype(jnp.float32),
                shift,
                sub,
            )
        return carry

    lax.fori_loop(0, TR // BS, read_second, 0)
    rows = 8

    def finish(i, carry):
        start = i * rows
        sums = conv_chunk(
            lambda a: field[pl.ds(start + a, rows)], weights[...], rows
        )[:, :TC]
        for half in range(rows // BS):
            at = start + half * BS
            out[pl.ds(at, BS)] = 0.5 * field[pl.ds(at + 1, BS), :TC] + jnp.tanh(
                sums[half * BS : (half + 1) * BS]
                + inputs[pl.ds(at, BS)]
                + second[i * (rows // BS) + half][None]
            )
        return carry

    lax.fori_loop(0, TR // rows, finish, 0)


def meta_row(*parts):
    joined = jnp.concatenate([p.reshape(-1).astype(jnp.float32) for p in parts])
    return jnp.pad(joined[None], ((0, 7), (0, C - joined.shape[0])))


def decode(
    state,
    syndromes,
    erased,
    readers,
    conv_weight,
    syndrome_table,
    erasure_vector,
    read_weight,
    erasure_offset,
):
    f32 = jnp.float32
    pieces = gather_weights(read_weight)
    gx, gy = lax.axis_index("gx"), lax.axis_index("gy")
    gx_count, gy_count = lax.axis_size("gx"), lax.axis_size("gy")
    block_rows, block_cols = TR // BS, TC // BS
    ids = readers.reshape(block_rows, block_cols)
    bits, lost = syndromes[0], erased[0]

    def row_pay(row, block_row):
        cells = lax.slice_in_dim(state, row, row + HALO, axis=0).reshape(HALO * TC, C)
        edge = 0 if row == 0 else TR - 1
        return jnp.concatenate(
            [cells, meta_row(bits[edge], lost[block_row], ids[block_row])], axis=0
        )

    up = [(i, i - 1) for i in range(1, gx_count)]
    down = [(i, i + 1) for i in range(gx_count - 1)]
    top = lax.ppermute(row_pay(TR - HALO, block_rows - 1), "gx", down)
    bottom = lax.ppermute(row_pay(0, 0), "gx", up)

    def meta(pay, start, count):
        return pay[-8, start : start + count].astype(jnp.int32)

    def stack(mid, start, count):
        return jnp.concatenate(
            [meta(top, start, count)[None], mid, meta(bottom, start, count)[None]], axis=0
        )

    bits_tall = stack(bits, 0, TC)
    lost_tall = stack(lost, TC, block_cols)
    ids_tall = stack(ids, TC + block_cols, block_cols)

    def col_pay(col):
        def cut(cells):
            return lax.slice_in_dim(cells, col, col + HALO, axis=1)

        cells = jnp.concatenate(
            [
                cut(top[: HALO * TC].reshape(HALO, TC, C)),
                cut(state),
                cut(bottom[: HALO * TC].reshape(HALO, TC, C)),
            ],
            axis=0,
        ).reshape(TALL * HALO, C)
        edge = 0 if col == 0 else -1
        return jnp.concatenate(
            [cells, meta_row(bits_tall[:, edge], lost_tall[:, edge], ids_tall[:, edge])],
            axis=0,
        )

    west = [(i, i - 1) for i in range(1, gy_count)]
    east = [(i, i + 1) for i in range(gy_count - 1)]
    left = lax.ppermute(col_pay(TC - HALO), "gy", east)
    right = lax.ppermute(col_pay(0), "gy", west)

    tall = TR + 2
    bits_wide = jnp.concatenate(
        [
            bits_tall,
            meta(right, 0, tall)[:, None],
            jnp.zeros((tall, 6), jnp.int32),
            meta(left, 0, tall)[:, None],
        ],
        axis=1,
    )
    bits_wide = jnp.pad(bits_wide, ((1, 1), (0, 0)))

    def widen(mid, start):
        return jnp.concatenate(
            [mid, meta(right, start, BROWS)[:, None], meta(left, start, BROWS)[:, None]],
            axis=1,
        )

    lost_wide = widen(lost_tall, tall)
    ids_wide = widen(ids_tall, tall + BROWS)

    def embed(bits_at, lost_at):
        return jnp.where(
            lost_at[:, :, None] > 0,
            erasure_vector,
            jnp.where(bits_at[:, :, None] == 1, syndrome_table[1], syndrome_table[0]),
        )

    def sites(blocks):
        return jnp.repeat(jnp.repeat(blocks, BS, axis=0), BS, axis=1)

    inputs_first = embed(bits_wide, sites(lost_wide)[2 : 2 + CONV_ROWS])
    inputs_second = embed(syndromes[1], sites(erased[1]))

    vmem = pl.BlockSpec(memory_space=pltpu.VMEM)
    smem = pl.BlockSpec(memory_space=pltpu.SMEM)
    anywhere = pl.BlockSpec(memory_space=pl.ANY)
    ext, pre, weights = pl.pallas_call(
        first_kernel,
        name="conv_first",
        out_shape=(
            jax.ShapeDtypeStruct((TALL, WIDE, C), f32),
            jax.ShapeDtypeStruct((CONV_ROWS, WIDE, C), f32),
            jax.ShapeDtypeStruct((9 * C, 3 * C), jnp.bfloat16),
        ),
        in_specs=[vmem] * 7,
        out_specs=(vmem, vmem, vmem),
        cost_estimate=pl.CostEstimate(
            flops=2_000_000_000, bytes_accessed=6_000_000, transcendentals=0
        ),
    )(state, top, bottom, right, left, conv_weight, inputs_first)

    slots = slots_of(ids_wide).reshape(-1)
    lost_second = jnp.pad(erased[1], ((1, 1), (0, 2))).reshape(-1)
    flags = jnp.concatenate([lost_wide.reshape(-1), lost_second])
    inside = jnp.stack(
        [gx > 0, gx < gx_count - 1, gy < gy_count - 1, gy > 0]
    ).astype(jnp.int32)
    return pl.pallas_call(
        second_kernel,
        name="read_and_finish",
        out_shape=jax.ShapeDtypeStruct((TR, TC, C), f32),
        in_specs=[smem] * 3 + [vmem] * 5 + [anywhere] * 14,
        out_specs=vmem,
        scratch_shapes=[
            pltpu.VMEM((128, C, C), f32),
            pltpu.VMEM((BROWS * GROUPS, 2 * C, 2 * C), jnp.bfloat16),
            pltpu.VMEM((BROWS, WIDE, C), f32),
            pltpu.VMEM((TR + 2, WIDE, C), f32),
            pltpu.VMEM((TR // BS, TC, C), f32),
            pltpu.SemaphoreType.DMA((14,)),
        ],
        cost_estimate=pl.CostEstimate(
            flops=4_000_000_000, bytes_accessed=12_000_000, transcendentals=1_000_000
        ),
    )(
        slots,
        flags,
        inside,
        ext,
        pre,
        inputs_second,
        weights,
        erasure_offset[None],
        *pieces,
    )


def solution(mesh):
    placed = (
        P("gx", "gy", None),
        P(None, "gx", "gy"),
        P(None, "gx", "gy"),
        P(("gx", "gy"), None),
        P(),
        P(),
        P(),
        P(("gx", "gy"), None),
        P(),
    )
    return jax.shard_map(
        decode, mesh=mesh, in_specs=placed, out_specs=P("gx", "gy", None), check_vma=False
    )
```

profile of v0, /device:TPU:33, one launch (start us, length us, event | category | flops | bytes accessed | tf_op | source)
XLA Modules:
  0.0 92.4 jit_solution(4107774809742221070)
XLA Ops:
  0.0 0.7 convert_bitcast_fusion.5
  0.7 0.8 convert_bitcast_fusion.4
  1.5 0.8 convert_bitcast_fusion.3
  2.3 1.0 %fusion.26 = (f32[4,64,128]{2,1,0:T(8,128)S(1)}, f32[4,64,128]{2,1,0:T(8,128)S(1)}) fusion(f32[32,64,128]{2,1,0:T(8,128)} %state.1), kind=kLoop, calls=%fused_computation.115 | loop fusion | bytes 524288 | tf_op jit(solution)/shard_map/slice | solution.py:275
  3.3 0.1 maximum_bitcast_fusion
  3.4 3.2 %collective-permute-start = (f32[264,128]{1,0:T(8,128)S(1)}, f32[264,128]{1,0:T(8,128)S(1)}, u32[]{:S(2)}, u32[]{:S(2)}) collective-permute-start(f32[264,128]{1,0:T(8,128)S(1)} %select_maximum_fusion.1), channel_id=1, source_target_pairs={{0,8},{8,16},{16,24},{24,32},{32,40},{40,48},{48,56},{56,64},{64,7... | collective-permute-start | bytes 405512 | tf_op jit(solution)/shard_map/ppermute | solution.py:283
  6.6 0.1 maximum_bitcast_fusion.1
  6.7 4.2 %collective-permute-start.1 = (f32[264,128]{1,0:T(8,128)S(1)}, f32[264,128]{1,0:T(8,128)S(1)}, u32[]{:S(2)}, u32[]{:S(2)}) collective-permute-start(f32[264,128]{1,0:T(8,128)S(1)} %select_maximum_fusion), channel_id=1, source_target_pairs={{8,0},{16,8},{24,16},{32,24},{40,32},{48,40},{56,48},{64,56},{72,6... | collective-permute-start | bytes 405512 | tf_op jit(solution)/shard_map/ppermute | solution.py:284
  10.9 1.9 %broadcast_in_dim.126 = f32[16,128,128]{2,1,0:T(8,128)} broadcast(f32[128,128]{1,0:T(8,128)} %param.16), dimensions={1,2} | broadcast | bytes 1114112 | tf_op jit(solution)/shard_map/broadcast_in_dim | solution.py:49
  12.8 8.0 %all-to-all-start = ((f32[16,128,128]{2,1,0:T(8,128)}), f32[16,128,128]{2,1,0:T(8,128)S(1)}, u32[]{:S(2)}, u32[]{:S(2)}) async-start(f32[16,128,128]{2,1,0:T(8,128)} %broadcast_in_dim.126), calls=%async_computation | async-start | bytes 2097152 | tf_op jit(solution)/shard_map/all_to_all | solution.py:50
  20.8 1.0 %fusion.25 = (f32[32,4,128]{2,1,0:T(4,128)S(1)}, f32[32,4,128]{2,1,0:T(4,128)S(1)}) fusion(f32[32,64,128]{2,1,0:T(8,128)} %state.1), kind=kLoop, calls=%fused_computation.114 | loop fusion | bytes 262144 | tf_op jit(solution)/shard_map/slice | solution.py:300
  21.9 0.1 copy.44
  22.0 0.1 copy.45
  22.1 1.5 %select_select_fusion.1.inputs = f32[32,64,128]{2,1,0:T(8,128)} fusion(f32[128]{0:T(128)S(1)} %get-tuple-element.42, f32[128]{0:T(128)S(1)} %get-tuple-element.41, f32[128]{0:T(128)S(1)} %copy-done.5, pred[32,64]{1,0:T(8,128)(4,1)S(1)} %fusion.2, pred[32,64]{1,0:T(8,128)(4,1)S(1)} %copy.45), kind=kLoop, calls=%fused_computation.1 | loop fusion | flops 524288 | bytes 1054208 | tf_op jit(solution)/shard_map/jit(_where)/select_n | solution.py:343
  23.6 0.5 broadcast.205
  24.1 0.6 reduce.15
  24.7 0.1 reshape.161
  24.8 0.1 pad.32.clone
  24.9 0.1 reshape.168
  25.0 0.7 add_convert_fusion.inside
  25.7 0.1 slice_convert_fusion.13
  25.8 0.2 fusion.6
  26.0 0.2 fusion.5
  26.3 0.2 fusion.1
  26.5 0.1 maximum_bitcast_fusion.2
  26.6 3.7 %collective-permute-start.2 = (f32[168,128]{1,0:T(8,128)S(1)}, f32[168,128]{1,0:T(8,128)S(1)}, u32[]{:S(2)}, u32[]{:S(2)}) collective-permute-start(f32[168,128]{1,0:T(8,128)S(1)} %select_maximum_fusion.3), channel_id=1, source_target_pairs={{1,0},{2,1},{3,2},{4,3},{5,4},{6,5},{7,6},{9,8},{10,9},{11,10},{12... | collective-permute-start | bytes 258056 | tf_op jit(solution)/shard_map/ppermute | solution.py:319
  30.4 0.1 maximum_bitcast_fusion.3
  30.4 3.1 %collective-permute-start.3 = (f32[168,128]{1,0:T(8,128)S(1)}, f32[168,128]{1,0:T(8,128)S(1)}, u32[]{:S(2)}, u32[]{:S(2)}) collective-permute-start(f32[168,128]{1,0:T(8,128)S(1)} %select_maximum_fusion.2), channel_id=1, source_target_pairs={{0,1},{1,2},{2,3},{3,4},{4,5},{5,6},{6,7},{8,9},{9,10},{10,11},{11... | collective-permute-start | bytes 258056 | tf_op jit(solution)/shard_map/ppermute | solution.py:318
  33.6 2.1 %collective-permute-done.2.right = f32[168,128]{1,0:T(8,128)S(1)} collective-permute-done((f32[168,128]{1,0:T(8,128)S(1)}, f32[168,128]{1,0:T(8,128)S(1)}, u32[]{:S(2)}, u32[]{:S(2)}) %collective-permute-start.2) | collective-permute-done | bytes 86048 | tf_op jit(solution)/shard_map/ppermute | solution.py:319
  35.7 0.1 copy.42
  35.8 0.1 copy.43
  36.0 0.1 copy.38
  36.1 0.1 fusion.24
  36.2 1.9 %collective-permute-start.4 = (f32[8,128,128]{2,1,0:T(8,128)S(1)}, f32[8,128,128]{2,1,0:T(8,128)S(1)}, u32[]{:S(2)}, u32[]{:S(2)}) collective-permute-start(f32[8,128,128]{2,1,0:T(8,128)S(1)} %get-tuple-element.18), channel_id=1, source_target_pairs={{0,2},{1,3},{2,4},{3,5},{4,6},{5,7},{6,0},{7,1},{8,10},{9,11},{10,... | collective-permute-start | bytes 1572872 | tf_op jit(solution)/shard_map/ppermute | solution.py:55
  38.1 0.8 collective-permute-start.6
  38.9 0.8 collective-permute-start.5
  39.7 1.9 %collective-permute-start.7 = (f32[8,128,128]{2,1,0:T(8,128)S(1)}, f32[8,128,128]{2,1,0:T(8,128)}, u32[]{:S(2)}, u32[]{:S(2)}) collective-permute-start(f32[8,128,128]{2,1,0:T(8,128)S(1)} %get-tuple-element.17), channel_id=1, source_target_pairs={{0,24},{1,25},{2,26},{3,27},{4,28},{5,29},{6,30},{7,31},{8,0},{9,1... | collective-permute-start | bytes 1572872 | tf_op jit(solution)/shard_map/ppermute | solution.py:56
  41.7 0.1 copy.39
  41.8 0.1 pad_add_fusion.5
  41.9 0.1 copy.46
  42.0 0.1 pad_add_fusion.1
  42.1 0.2 collective-permute-start.8
  42.2 7.8 %collective-permute-done.4.rest_1_ = f32[8,128,128]{2,1,0:T(8,128)S(1)} collective-permute-done((f32[8,128,128]{2,1,0:T(8,128)S(1)}, f32[8,128,128]{2,1,0:T(8,128)S(1)}, u32[]{:S(2)}, u32[]{:S(2)}) %collective-permute-start.4) | collective-permute-done | bytes 524320 | tf_op jit(solution)/shard_map/ppermute | solution.py:55
  50.1 1.8 %collective-permute-done.5.rest_2_ = f32[8,128,128]{2,1,0:T(8,128)} collective-permute-done((f32[8,128,128]{2,1,0:T(8,128)S(1)}, f32[8,128,128]{2,1,0:T(8,128)}, u32[]{:S(2)}, u32[]{:S(2)}) %collective-permute-start.5) | collective-permute-done | bytes 524320 | tf_op jit(solution)/shard_map/ppermute | solution.py:56
  51.9 1.5 %collective-permute-start.10 = (f32[16,128,128]{2,1,0:T(8,128)S(1)}, f32[16,128,128]{2,1,0:T(8,128)}, u32[]{:S(2)}, u32[]{:S(2)}) collective-permute-start(f32[16,128,128]{2,1,0:T(8,128)S(1)} %all-to-all-done.rest_0_), channel_id=1, source_target_pairs={{0,1},{1,0},{2,3},{3,2},{4,5},{5,4},{6,7},{7,6},{8,9},{9,8},{10,11... | collective-permute-start | bytes 3145736 | tf_op jit(solution)/shard_map/ppermute | solution.py:57
  53.4 0.4 collective-permute-start.11
  53.8 0.4 collective-permute-start.12
  54.2 0.1 copy.41
  54.3 0.1 copy.36
  54.4 0.1 copy.37
  54.5 2.2 %select_select_fusion.inputs = f32[36,72,128]{2,1,0:T(8,128)} fusion(f32[128]{0:T(128)S(1)} %get-tuple-element.42, f32[128]{0:T(128)S(1)} %get-tuple-element.41, f32[128]{0:T(128)S(1)} %copy-done.5, pred[36,72]{1,0:T(8,128)(4,1)S(1)} %pad_compare_fusion, pred[36,72]{1,0:T(8,128)(4,1)S(1)} %copy.41), kind=kLoop, calls=%fused_computation | loop fusion | flops 663552 | bytes 1333824 | tf_op jit(solution)/shard_map/jit(_where)/select_n | solution.py:343
  56.8 0.2 collective-permute-start.13
  57.0 4.9 %collective-permute-done.9.rest_6_ = f32[8,128,128]{2,1,0:T(8,128)} collective-permute-done((f32[8,128,128]{2,1,0:T(8,128)S(1)}, f32[8,128,128]{2,1,0:T(8,128)}, u32[]{:S(2)}, u32[]{:S(2)}) %collective-permute-start.9) | collective-permute-done | bytes 524320 | tf_op jit(solution)/shard_map/ppermute | solution.py:56
  61.9 2.6 %collective-permute-start.14 = (f32[8,128,128]{2,1,0:T(8,128)}, f32[8,128,128]{2,1,0:T(8,128)S(1)}, u32[]{:S(2)}, u32[]{:S(2)}) collective-permute-start(f32[8,128,128]{2,1,0:T(8,128)} %collective-permute-done.7.rest_4_), channel_id=1, source_target_pairs={{0,1},{1,0},{2,3},{3,2},{4,5},{5,4},{6,7},{7,6},{8,9},{9,8},{10,11... | collective-permute-start | bytes 1572872 | tf_op jit(solution)/shard_map/ppermute | solution.py:57
  64.5 0.5 collective-permute-start.16
  65.0 0.1 pad_add_fusion.4
  65.1 0.1 reshape.167
  65.2 0.1 concatenate.67
  65.3 0.7 pad_add_fusion.6.flags
  65.9 7.4 %conv_first.1 = (f32[40,72,128]{2,1,0:T(8,128)}, f32[36,72,128]{2,1,0:T(8,128)}, bf16[1152,384]{1,0:T(8,128)(2,1)}) custom-call(f32[32,64,128]{2,1,0:T(8,128)} %state.1, f32[264,128]{1,0:T(8,128)} %copy-done.1, f32[264,128]{1,0:T(8,128)} %copy-done.2, f32[168,128]{1,0:T(8,128)} %copy-done.8, f32[168,128]{1,0:T(8,128)} %copy-done.9, f32[9,128,128]{2,1,0:T(8,128)} %taps.1, ...), custom_call_target="tpu_custom_call" | custom-call | flops 2000000000 | bytes 6000000 | tf_op jit(solution)/shard_map/conv_first/pallas_call | solution.py:358
  73.3 0.6 fusion.17.slots
  74.0 0.8 copy-done.11
  74.7 0.2 copy-done.12
  74.9 17.5 %read_and_finish.1 = f32[32,64,128]{2,1,0:T(8,128)} custom-call(s32[180]{0:T(256)} %fusion.17.slots, s32[360]{0:T(512)} %pad_add_fusion.6.flags, s32[4]{0:T(128)} %add_convert_fusion.inside, f32[40,72,128]{2,1,0:T(8,128)} %get-tuple-element.8.ext, f32[36,72,128]{2,1,0:T(8,128)} %get-tuple-element.9.pre, f32[32,64,128]{2,1,0:T(8,128)} %select_select_fusion.1.inputs, ...), custom_call_target="tpu_custom_call" | custom-call | flops 4000000000 | bytes 12000000 | tf_op jit(solution)/shard_map/read_and_finish/pallas_call | solution.py:379
  (72 shorter events, 0.6 us)
Async XLA Ops:
  3.4 22.3 %collective-permute-start = (f32[264,128]{1,0:T(8,128)S(1)}, f32[264,128]{1,0:T(8,128)S(1)}, u32[]{:S(2)}, u32[]{:S(2)}) collective-permute-start(f32[264,128]{1,0:T(8,128)S(1)} %select_maximum_fusion.1), channel_id=1, source_target_pairs={{0,8},{8,16},{16,24},{24,32},{32,40},{40,48},{48,56},{56,64},{64,7... | collective-permute-start | bytes 405512 | tf_op jit(solution)/shard_map/ppermute | solution.py:283
  6.7 14.1 %copy-start.3 = (s32[2,32,64]{2,1,0:T(8,128)S(1)}, s32[2,32,64]{2,1,0:T(8,128)}, u32[]{:S(2)}) copy-start(s32[2,32,64]{2,1,0:T(8,128)} %param.10) | copy-start | bytes 49156
  6.7 19.1 %collective-permute-start.1 = (f32[264,128]{1,0:T(8,128)S(1)}, f32[264,128]{1,0:T(8,128)S(1)}, u32[]{:S(2)}, u32[]{:S(2)}) collective-permute-start(f32[264,128]{1,0:T(8,128)S(1)} %select_maximum_fusion), channel_id=1, source_target_pairs={{8,0},{16,8},{24,16},{32,24},{40,32},{48,40},{56,48},{64,56},{72,6... | collective-permute-start | bytes 405512 | tf_op jit(solution)/shard_map/ppermute | solution.py:284
  12.8 9.0 %copy-start.4 = (s32[2,8,16]{2,1,0:T(8,128)S(1)}, s32[2,8,16]{2,1,0:T(8,128)}, u32[]{:S(2)}) copy-start(s32[2,8,16]{2,1,0:T(8,128)} %param.11) | copy-start | bytes 3076
  12.8 9.0 %copy-start.7 = (f32[2,128]{1,0:T(2,128)S(1)}, f32[2,128]{1,0:T(2,128)}, u32[]{:S(2)}) copy-start(f32[2,128]{1,0:T(2,128)} %param.14) | copy-start | bytes 3076
  12.8 9.3 %copy-start.5 = (f32[128]{0:T(128)S(1)}, f32[128]{0:T(128)}, u32[]{:S(2)}) copy-start(f32[128]{0:T(128)} %param.15) | copy-start | bytes 1540
  12.8 11.3 %copy-start.6 = (s32[128,1]{0,1:T(1,128)S(1)}, s32[128,1]{0,1:T(1,128)}, u32[]{:S(2)}) copy-start(s32[128,1]{0,1:T(1,128)} %param.12) | copy-start | bytes 1540
  12.8 23.3 %all-to-all-start = ((f32[16,128,128]{2,1,0:T(8,128)}), f32[16,128,128]{2,1,0:T(8,128)S(1)}, u32[]{:S(2)}, u32[]{:S(2)}) async-start(f32[16,128,128]{2,1,0:T(8,128)} %broadcast_in_dim.126), calls=%async_computation | async-start | bytes 2097152 | tf_op jit(solution)/shard_map/all_to_all | solution.py:50
  25.7 10.5 %copy-start.1 = (f32[264,128]{1,0:T(8,128)}, f32[264,128]{1,0:T(8,128)S(1)}, u32[]{:S(2)}) copy-start(f32[264,128]{1,0:T(8,128)S(1)} %collective-permute-done.top) | copy-start | bytes 405508
  25.8 10.5 %copy-start.2 = (f32[264,128]{1,0:T(8,128)}, f32[264,128]{1,0:T(8,128)S(1)}, u32[]{:S(2)}) copy-start(f32[264,128]{1,0:T(8,128)S(1)} %collective-permute-done.1.bottom) | copy-start | bytes 405508
  26.6 9.1 %collective-permute-start.2 = (f32[168,128]{1,0:T(8,128)S(1)}, f32[168,128]{1,0:T(8,128)S(1)}, u32[]{:S(2)}, u32[]{:S(2)}) collective-permute-start(f32[168,128]{1,0:T(8,128)S(1)} %select_maximum_fusion.3), channel_id=1, source_target_pairs={{1,0},{2,1},{3,2},{4,3},{5,4},{6,5},{7,6},{9,8},{10,9},{11,10},{12... | collective-permute-start | bytes 258056 | tf_op jit(solution)/shard_map/ppermute | solution.py:319
  30.4 5.4 %collective-permute-start.3 = (f32[168,128]{1,0:T(8,128)S(1)}, f32[168,128]{1,0:T(8,128)S(1)}, u32[]{:S(2)}, u32[]{:S(2)}) collective-permute-start(f32[168,128]{1,0:T(8,128)S(1)} %select_maximum_fusion.2), channel_id=1, source_target_pairs={{0,1},{1,2},{2,3},{3,4},{4,5},{5,6},{6,7},{8,9},{9,10},{10,11},{11... | collective-permute-start | bytes 258056 | tf_op jit(solution)/shard_map/ppermute | solution.py:318
  35.7 21.1 %copy-start.8 = (f32[168,128]{1,0:T(8,128)}, f32[168,128]{1,0:T(8,128)S(1)}, u32[]{:S(2)}) copy-start(f32[168,128]{1,0:T(8,128)S(1)} %collective-permute-done.2.right) | copy-start | bytes 258052
  35.8 21.0 %copy-start.9 = (f32[168,128]{1,0:T(8,128)}, f32[168,128]{1,0:T(8,128)S(1)}, u32[]{:S(2)}) copy-start(f32[168,128]{1,0:T(8,128)S(1)} %collective-permute-done.3.left) | copy-start | bytes 258052
  36.1 20.7 %copy-start = (f32[16,128,128]{2,1,0:T(8,128)}, f32[16,128,128]{2,1,0:T(8,128)S(1)}, u32[]{:S(2)}) copy-start(f32[16,128,128]{2,1,0:T(8,128)S(1)} %all-to-all-done.rest_0_) | copy-start | bytes 3145732
  36.2 13.8 %collective-permute-start.4 = (f32[8,128,128]{2,1,0:T(8,128)S(1)}, f32[8,128,128]{2,1,0:T(8,128)S(1)}, u32[]{:S(2)}, u32[]{:S(2)}) collective-permute-start(f32[8,128,128]{2,1,0:T(8,128)S(1)} %get-tuple-element.18), channel_id=1, source_target_pairs={{0,2},{1,3},{2,4},{3,5},{4,6},{5,7},{6,0},{7,1},{8,10},{9,11},{10,... | collective-permute-start | bytes 1572872 | tf_op jit(solution)/shard_map/ppermute | solution.py:55
  38.1 15.3 %collective-permute-start.6 = (f32[8,128,128]{2,1,0:T(8,128)S(1)}, f32[8,128,128]{2,1,0:T(8,128)}, u32[]{:S(2)}, u32[]{:S(2)}) collective-permute-start(f32[8,128,128]{2,1,0:T(8,128)S(1)} %get-tuple-element.18), channel_id=1, source_target_pairs={{0,8},{1,9},{2,10},{3,11},{4,12},{5,13},{6,14},{7,15},{8,16},{9,17... | collective-permute-start | bytes 1572872 | tf_op jit(solution)/shard_map/ppermute | solution.py:55
  38.9 12.9 %collective-permute-start.5 = (f32[8,128,128]{2,1,0:T(8,128)S(1)}, f32[8,128,128]{2,1,0:T(8,128)}, u32[]{:S(2)}, u32[]{:S(2)}) collective-permute-start(f32[8,128,128]{2,1,0:T(8,128)S(1)} %get-tuple-element.17), channel_id=1, source_target_pairs={{0,6},{1,7},{2,0},{3,1},{4,2},{5,3},{6,4},{7,5},{8,14},{9,15},{10,... | collective-permute-start | bytes 1572872 | tf_op jit(solution)/shard_map/ppermute | solution.py:56
  39.7 14.0 %collective-permute-start.7 = (f32[8,128,128]{2,1,0:T(8,128)S(1)}, f32[8,128,128]{2,1,0:T(8,128)}, u32[]{:S(2)}, u32[]{:S(2)}) collective-permute-start(f32[8,128,128]{2,1,0:T(8,128)S(1)} %get-tuple-element.17), channel_id=1, source_target_pairs={{0,24},{1,25},{2,26},{3,27},{4,28},{5,29},{6,30},{7,31},{8,0},{9,1... | collective-permute-start | bytes 1572872 | tf_op jit(solution)/shard_map/ppermute | solution.py:56
  42.1 14.7 %collective-permute-start.8 = (f32[8,128,128]{2,1,0:T(8,128)S(1)}, f32[8,128,128]{2,1,0:T(8,128)}, u32[]{:S(2)}, u32[]{:S(2)}) collective-permute-start(f32[8,128,128]{2,1,0:T(8,128)S(1)} %get-tuple-element.18), channel_id=1, source_target_pairs={{0,32},{1,33},{2,34},{3,35},{4,36},{5,37},{6,38},{7,39},{8,40},{9,... | collective-permute-start | bytes 1572872 | tf_op jit(solution)/shard_map/ppermute | solution.py:55
  50.0 23.3 %copy-start.10 = (f32[8,128,128]{2,1,0:T(8,128)}, f32[8,128,128]{2,1,0:T(8,128)S(1)}, u32[]{:S(2)}) copy-start(f32[8,128,128]{2,1,0:T(8,128)S(1)} %collective-permute-done.4.rest_1_) | copy-start | bytes 1572868
  50.1 11.8 %collective-permute-start.9 = (f32[8,128,128]{2,1,0:T(8,128)S(1)}, f32[8,128,128]{2,1,0:T(8,128)}, u32[]{:S(2)}, u32[]{:S(2)}) collective-permute-start(f32[8,128,128]{2,1,0:T(8,128)S(1)} %get-tuple-element.17), channel_id=1, source_target_pairs={{0,96},{1,97},{2,98},{3,99},{4,100},{5,101},{6,102},{7,103},{8,104... | collective-permute-start | bytes 1572872 | tf_op jit(solution)/shard_map/ppermute | solution.py:56
  51.9 22.1 %collective-permute-start.10 = (f32[16,128,128]{2,1,0:T(8,128)S(1)}, f32[16,128,128]{2,1,0:T(8,128)}, u32[]{:S(2)}, u32[]{:S(2)}) collective-permute-start(f32[16,128,128]{2,1,0:T(8,128)S(1)} %all-to-all-done.rest_0_), channel_id=1, source_target_pairs={{0,1},{1,0},{2,3},{3,2},{4,5},{5,4},{6,7},{7,6},{8,9},{9,8},{10,11... | collective-permute-start | bytes 3145736 | tf_op jit(solution)/shard_map/ppermute | solution.py:57
  53.4 11.1 %collective-permute-start.11 = (f32[8,128,128]{2,1,0:T(8,128)S(1)}, f32[8,128,128]{2,1,0:T(8,128)}, u32[]{:S(2)}, u32[]{:S(2)}) collective-permute-start(f32[8,128,128]{2,1,0:T(8,128)S(1)} %collective-permute-done.4.rest_1_), channel_id=1, source_target_pairs={{0,1},{1,0},{2,3},{3,2},{4,5},{5,4},{6,7},{7,6},{8,9},{9,8},{10,11... | collective-permute-start | bytes 1572872 | tf_op jit(solution)/shard_map/ppermute | solution.py:57
  53.8 10.7 %collective-permute-start.12 = (f32[8,128,128]{2,1,0:T(8,128)}, f32[8,128,128]{2,1,0:T(8,128)}, u32[]{:S(2)}, u32[]{:S(2)}) collective-permute-start(f32[8,128,128]{2,1,0:T(8,128)} %collective-permute-done.5.rest_2_), channel_id=1, source_target_pairs={{0,1},{1,0},{2,3},{3,2},{4,5},{5,4},{6,7},{7,6},{8,9},{9,8},{10,11... | collective-permute-start | bytes 1572872 | tf_op jit(solution)/shard_map/ppermute | solution.py:57
  56.8 17.2 %collective-permute-start.13 = (f32[8,128,128]{2,1,0:T(8,128)}, f32[8,128,128]{2,1,0:T(8,128)S(1)}, u32[]{:S(2)}, u32[]{:S(2)}) collective-permute-start(f32[8,128,128]{2,1,0:T(8,128)} %collective-permute-done.6.rest_3_), channel_id=1, source_target_pairs={{0,1},{1,0},{2,3},{3,2},{4,5},{5,4},{6,7},{7,6},{8,9},{9,8},{10,11... | collective-permute-start | bytes 1572872 | tf_op jit(solution)/shard_map/ppermute | solution.py:57
  61.9 12.1 %collective-permute-start.14 = (f32[8,128,128]{2,1,0:T(8,128)}, f32[8,128,128]{2,1,0:T(8,128)S(1)}, u32[]{:S(2)}, u32[]{:S(2)}) collective-permute-start(f32[8,128,128]{2,1,0:T(8,128)} %collective-permute-done.7.rest_4_), channel_id=1, source_target_pairs={{0,1},{1,0},{2,3},{3,2},{4,5},{5,4},{6,7},{7,6},{8,9},{9,8},{10,11... | collective-permute-start | bytes 1572872 | tf_op jit(solution)/shard_map/ppermute | solution.py:57
  64.5 9.4 %collective-permute-start.15 = (f32[8,128,128]{2,1,0:T(8,128)}, f32[8,128,128]{2,1,0:T(8,128)}, u32[]{:S(2)}, u32[]{:S(2)}) collective-permute-start(f32[8,128,128]{2,1,0:T(8,128)} %collective-permute-done.8.rest_5_), channel_id=1, source_target_pairs={{0,1},{1,0},{2,3},{3,2},{4,5},{5,4},{6,7},{7,6},{8,9},{9,8},{10,11... | collective-permute-start | bytes 1572872 | tf_op jit(solution)/shard_map/ppermute | solution.py:57
  64.5 9.5 %collective-permute-start.16 = (f32[8,128,128]{2,1,0:T(8,128)}, f32[8,128,128]{2,1,0:T(8,128)}, u32[]{:S(2)}, u32[]{:S(2)}) collective-permute-start(f32[8,128,128]{2,1,0:T(8,128)} %collective-permute-done.9.rest_6_), channel_id=1, source_target_pairs={{0,1},{1,0},{2,3},{3,2},{4,5},{5,4},{6,7},{7,6},{8,9},{9,8},{10,11... | collective-permute-start | bytes 1572872 | tf_op jit(solution)/shard_map/ppermute | solution.py:57
  73.9 0.8 copy-start.11
  73.9 1.0 %copy-start.12 = (f32[8,128,128]{2,1,0:T(8,128)}, f32[8,128,128]{2,1,0:T(8,128)S(1)}, u32[]{:S(2)}) copy-start(f32[8,128,128]{2,1,0:T(8,128)S(1)} %collective-permute-done.14.rest_11_) | copy-start | bytes 1572868
where the time goes:
time: 94.1 us; the launch traced here: 92.4 us
  starting transfers between devices  33.4 us (35%)
  Pallas kernels  24.8 us (26%)
  waiting for transfers between devices  16.6 us (18%)
  other arithmetic  10.1 us (11%)
  local copies, waits for them, and re-layouts  6.96 us (7%)
    pallas_call x1, Pallas kernels, decode(): pl.pallas_call(second_kernel, name='read_and_finish', out_shape=jax.Shape...  17.5 us
    all_to_all x1, starting transfers between devices, gather_weights(): lax.all_to_all(copies, AX, 0, 0, tiled=True, axis_index_groups=class_grou...  7.98 us
    ppermute x3, waiting for transfers between devices, gather_weights(): pieces.append(lax.ppermute(low, AX, moved(*step)))  7.82 us
    pallas_call x1, Pallas kernels, decode(): pl.pallas_call(first_kernel, name='conv_first', out_shape=(jax.ShapeDtype...  7.39 us
    ppermute x3, waiting for transfers between devices, gather_weights(): pieces.append(lax.ppermute(high, AX, moved(*back)))  6.68 us
    ppermute x7, starting transfers between devices, gather_weights(): pieces += [lax.ppermute(piece, AX, PARTNER) for piece in pieces]  5.67 us
    ppermute x1, starting transfers between devices, decode(): bottom = lax.ppermute(row_pay(0, 0), 'gx', up)  4.19 us
    select_n x2, other arithmetic, embed(): jnp.where(lost_at[:, :, None] > 0, erasure_vector, jnp.where(bits_at[:, :...  3.74 us
  transfers between devices with their start and end apart: 18, of which 4 were waited for; matrix products, arithmetic and copies ran while one was open for 14% of the time, Pallas kernels for 8%

commit v1 on v0

v1 whole, which is shorter than its diff:
```python
import jax
import jax.numpy as jnp
from jax import lax
from jax.experimental import pallas as pl
from jax.experimental.pallas import tpu as pltpu
from jax.sharding import PartitionSpec as P


BS = 4
C = 128
TR = 32
TC = 64
HALO = 4
WIDE = TC + 2 * HALO
TALL = TR + 2 * HALO
BROWS = TALL // BS
GROUPS = WIDE // 8
CONV_ROWS = TR + 4
AX = ("gx", "gy")


def flat_id(z, y, x, c):
    return ((z % 4 * 4 + y % 4) * 4 + x % 4) * 2 + c


SITES = [
    (z, y, x, c) for z in range(4) for y in range(4) for x in range(4) for c in range(2)
]


def class_groups():
    groups = {}
    for z, y, x, c in SITES:
        groups.setdefault(((x + z) % 2, (y + z) % 2, c), []).append(flat_id(z, y, x, c))
    return [groups[k] for k in sorted(groups)]


def moved(dz, dy, dx):
    return [
        (flat_id(z, y, x, c), flat_id(z + dz, y + dy, x + dx, c)) for z, y, x, c in SITES
    ]


PARTNER = [(flat_id(z, y, x, c), flat_id(z, y, x, 1 - c)) for z, y, x, c in SITES]


def gather_weights(copies):
    own = lax.all_to_all(copies, AX, 0, 0, tiled=True, axis_index_groups=class_groups())
    low, high = own[:8], own[8:]
    pieces = [own]
    for step in ((0, 0, 1), (0, 1, 0), (1, 0, 0)):
        back = tuple(-s for s in step)
        pieces.append(lax.ppermute(low, AX, moved(*step)))
        pieces.append(lax.ppermute(high, AX, moved(*back)))
    pieces += [lax.ppermute(piece, AX, PARTNER) for piece in pieces]
    return pieces


def split(value):
    high = value.astype(jnp.bfloat16)
    return high, (value - high.astype(jnp.float32)).astype(jnp.bfloat16)


def conv_chunk(read, weights, rows):
    highs, lows = [], []
    for a in range(3):
        high, low = split(read(a).reshape(rows * WIDE, C))
        highs.append(high)
        lows.append(low)
    left = jnp.concatenate(highs + highs + lows, axis=1)
    sums = jnp.dot(left, weights, preferred_element_type=jnp.float32)
    sums = sums.reshape(rows, WIDE, 3 * C)
    return (
        pltpu.roll(sums[:, :, :C], 1, 1)
        + sums[:, :, C : 2 * C]
        + pltpu.roll(sums[:, :, 2 * C :], WIDE - 1, 1)
    )


def rows_kernel(
    state, weight, syndromes, erased, readers, up, down, copies, rows_sem, copies_sem
):
    moves = [
        pltpu.make_async_copy(state.at[pl.ds(0, HALO)], up.at[pl.ds(0, HALO)], rows_sem.at[0]),
        pltpu.make_async_copy(
            state.at[pl.ds(TR - HALO, HALO)], down.at[pl.ds(0, HALO)], rows_sem.at[1]
        ),
    ]
    moves += [
        pltpu.make_async_copy(weight, copies.at[i], copies_sem.at[i]) for i in range(16)
    ]
    for move in moves:
        move.start()
    ids = readers[...].astype(jnp.float32)
    for pay, row, block_row in ((up, 0, 0), (down, TR - 1, TR // BS - 1)):
        pay[HALO] = jnp.zeros((TC, C), jnp.float32)
        pay[HALO, 0:1, :TC] = syndromes[0, row : row + 1, :].astype(jnp.float32)
        pay[HALO, 1:2, : TC // BS] = erased[0, block_row : block_row + 1, :].astype(
            jnp.float32
        )
        first = block_row * (TC // BS)
        pay[HALO, 2:3, :] = pltpu.roll(ids, (C - first) % C, 1)
    for move in moves:
        move.wait()


def repeat_blocks(blocks, rows):
    count = blocks.shape[0]
    row = lax.broadcasted_iota(jnp.int32, (rows, count), 0)
    tall = (row // BS == lax.broadcasted_iota(jnp.int32, (rows, count), 1)).astype(jnp.bfloat16)
    col = lax.broadcasted_iota(jnp.int32, (TC // BS, TC), 1)
    wide = (col // BS == lax.broadcasted_iota(jnp.int32, (TC // BS, TC), 0)).astype(jnp.bfloat16)
    half = jnp.dot(tall, blocks.astype(jnp.bfloat16), preferred_element_type=jnp.float32)
    return jnp.dot(half.astype(jnp.bfloat16), wide, preferred_element_type=jnp.float32)


def embed(code, table, lost_vector):
    return jnp.where(
        code > 1.5, lost_vector, jnp.where(code > 0.5, table[1:2], table[0:1])
    )


def cols_kernel(
    state,
    top,
    bottom,
    syndromes,
    erased,
    readers,
    table,
    lost_vector,
    west,
    east,
    code_out,
    lost_out,
    ids_out,
    vectors,
):
    f32 = jnp.float32
    block_rows, block_cols = TR // BS, TC // BS
    lost_out[...] = jnp.zeros((16, C), f32)
    ids_out[...] = jnp.zeros((16, C), f32)
    code_out[...] = jnp.zeros((TALL, TC), f32)
    lost_out[0:1, :block_cols] = top[HALO, 1:2, :block_cols]
    lost_out[BROWS - 1 : BROWS, :block_cols] = bottom[HALO, 1:2, :block_cols]
    lost_out[1 : 1 + block_rows, :block_cols] = erased[0].astype(f32)
    lane = lax.broadcasted_iota(jnp.int32, (1, C), 1)
    ids_out[0:1, :] = jnp.where(lane < block_cols, top[HALO, 2:3, :], 0.0)
    ids_out[BROWS - 1 : BROWS, :] = jnp.where(lane < block_cols, bottom[HALO, 2:3, :], 0.0)
    ids = readers[...].astype(f32)
    for k in range(block_rows):
        turned = pltpu.roll(ids, (C - k * block_cols) % C, 1)
        ids_out[k + 1 : k + 2, :] = jnp.where(lane < block_cols, turned, 0.0)
    code_out[HALO - 1 : HALO, :] = top[HALO, 0:1, :TC]
    code_out[HALO : HALO + TR, :] = syndromes[0].astype(f32)
    code_out[HALO + TR : HALO + TR + 1, :] = bottom[HALO, 0:1, :TC]
    sites = repeat_blocks(lost_out[:, :block_cols], TALL)
    code_out[...] = jnp.where(sites > 0.5, 2.0, code_out[...])
    sub = lax.broadcasted_iota(jnp.int32, (8, C), 0)
    for pay, edge, keep, at in ((west, 0, sub < 4, 4), (east, TC - 1, sub >= 4, 0)):
        block = edge // BS
        group = edge // 8 * 8
        code = jnp.broadcast_to(code_out[:, edge : edge + 1], (TALL, C))
        vectors[:TALL] = embed(code, table, lost_vector[...])
        vectors[TALL : TALL + 16] = jnp.broadcast_to(lost_out[:, block : block + 1], (16, C))
        vectors[TALL + 16 :] = jnp.broadcast_to(ids_out[:, block : block + 1], (16, C))
        _, second, third = (4, 5, 6) if at == 4 else (3, 2, 1)
        for r in range(TALL):
            if r < HALO:
                cells = top[r, group : group + 8]
            elif r < HALO + TR:
                cells = state[r - HALO, group : group + 8]
            else:
                cells = bottom[r - HALO - TR, group : group + 8]
            extra = jnp.broadcast_to(vectors[r : r + 1], (8, C))
            if r < BROWS:
                flag = jnp.broadcast_to(vectors[TALL + r : TALL + r + 1], (8, C))
                name = jnp.broadcast_to(vectors[TALL + 16 + r : TALL + 17 + r], (8, C))
                extra = jnp.where(sub == second, flag, jnp.where(sub == third, name, extra))
            pay[r] = jnp.where(keep, cells, extra)


def slots_of(ids, gx, gy):
    mz, my, mx, mc = gx >> 2, gx & 3, gy >> 1, gy & 1
    z, y, x, c = ids >> 5, (ids >> 3) & 3, (ids >> 1) & 3, ids & 1
    side = ((x + z + mx + mz) & 1) + 2 * ((y + z + my + mz) & 1)
    return (((c + mc) & 1) * 4 + side) * 16 + z * 4 + (y >> 1) * 2 + (x >> 1)


def first_kernel(
    me,
    state,
    top,
    bottom,
    right,
    left,
    taps,
    code,
    lost,
    ids,
    syndromes,
    erased,
    table,
    lost_vector,
    ext_out,
    pre_out,
    inputs_out,
    weights_out,
    slots_out,
    flags_out,
    codes,
    turned,
    names,
):
    f32 = jnp.float32
    sub = lax.broadcasted_iota(jnp.int32, (8, C), 0)
    ext_out[HALO : HALO + TR, :TC] = state[...]
    ext_out[:HALO, :TC] = top[:HALO]
    ext_out[HALO + TR :, :TC] = bottom[:HALO]
    for r in range(TALL):
        ext_out[r, TC:] = jnp.where(sub < 4, right[r], left[r])
    for a in range(3):
        for b in range(3):
            high, low = split(taps[3 * a + b])
            cols = slice(b * C, (b + 1) * C)
            weights_out[a * C : (a + 1) * C, cols] = high
            weights_out[(3 + a) * C : (4 + a) * C, cols] = low
            weights_out[(6 + a) * C : (7 + a) * C, cols] = high

    for r in range(BROWS):
        names[r : r + 1] = right[r, 5:6, :]
        names[16 + r : 17 + r] = left[r, 2:3, :]
        names[32 + r : 33 + r] = right[r, 6:7, :]
        names[48 + r : 49 + r] = left[r, 1:2, :]
    lane = lax.broadcasted_iota(jnp.int32, (16, C), 1)
    wide = TC // BS

    def widen(mid, at):
        return jnp.where(
            lane < wide,
            mid,
            jnp.where(
                lane == wide,
                names[at : at + 16],
                jnp.where(lane == wide + 1, names[at + 16 : at + 32], 0.0),
            ),
        ).astype(jnp.int32)

    names[BROWS:16] = jnp.zeros((16 - BROWS, C), f32)
    names[16 + BROWS : 32] = jnp.zeros((16 - BROWS, C), f32)
    names[32 + BROWS : 48] = jnp.zeros((16 - BROWS, C), f32)
    names[48 + BROWS :] = jnp.zeros((16 - BROWS, C), f32)
    flags_out[:16] = widen(lost[...], 0)
    flags_out[16:] = jnp.zeros((16, C), jnp.int32)
    flags_out[17 : 17 + TR // BS, :wide] = erased[1]
    slots_out[...] = slots_of(widen(ids[...], 32) & 127, me[0], me[1])

    codes[...] = jnp.zeros((C, C), f32)
    codes[:TALL, :TC] = code[...]
    second = repeat_blocks(erased[1].astype(f32), TR)
    codes[TALL : TALL + TR, :TC] = jnp.where(second > 0.5, 2.0, syndromes[1].astype(f32))
    turned[...] = codes[...].T
    values, vector = table[...], lost_vector[...]
    pre_out[0] = jnp.zeros((WIDE, C), f32)
    pre_out[CONV_ROWS - 1] = jnp.zeros((WIDE, C), f32)
    for r in range(HALO - 1, HALO + TR + 1):
        column = jnp.broadcast_to(turned[:TC, r : r + 1], (TC, C))
        pre_out[r - 2, :TC] = embed(column, values, vector)
        pre_out[r - 2, TC:] = jnp.where(
            sub == 0,
            pltpu.roll(right[r], 4, 0),
            jnp.where(sub == 7, pltpu.roll(left[r], 4, 0), 0.0),
        )
    for r in range(TR):
        column = jnp.broadcast_to(turned[:TC, TALL + r : TALL + r + 1], (TC, C))
        inputs_out[r] = embed(column, values, vector)

    rows = 12

    def step(i, carry):
        start = i * rows
        pre_out[pl.ds(start, rows)] += conv_chunk(
            lambda a: ext_out[pl.ds(start + 1 + a, rows)], weights_out[...], rows
        )
        return carry

    lax.fori_loop(0, CONV_ROWS // rows, step, 0)


def group_sum(total, sub):
    near = jnp.where(sub % 2 == 0, pltpu.roll(total, 7, 0), pltpu.roll(total, 1, 0))
    total = total + near
    far = jnp.where(sub % 4 < 2, pltpu.roll(total, 6, 0), pltpu.roll(total, 2, 0))
    return total + far


def readout(sites, right, flag_a, flag_b, offset, sub):
    high, low = split(sites.reshape(32, C))
    left = jnp.concatenate(
        [jnp.concatenate([high, high], axis=1), jnp.concatenate([low, low], axis=1)],
        axis=0,
    )
    mixed = jnp.dot(left, right, preferred_element_type=jnp.float32)
    mixed = (mixed[:32] + mixed[32:]).reshape(4, 8, 2 * C)
    mixed = jnp.tanh(jnp.where(sub[None] < 4, mixed[:, :, :C], mixed[:, :, C:]))
    total = mixed[0] + mixed[1] + mixed[2] + mixed[3]
    flags = jnp.where(sub < 4, flag_a, flag_b)
    return jnp.tanh(group_sum(total, sub) * 0.0625 + flags * offset)


PIECES = (16, 8, 8, 8, 8, 8, 8) * 2


def second_kernel(
    slots, flags, me, offset, ext_hbm, pre_hbm, inputs_hbm, weights_hbm, *rest
):
    pieces = rest[:14]
    out, table, pairs, first, field, second, ext, pre, inputs, weights, sems, late = rest[14:]
    copies = [pltpu.make_async_copy(ext_hbm, ext, sems.at[14])]
    at = 0
    for i, (piece, count) in enumerate(zip(pieces, PIECES)):
        copies.append(
            pltpu.make_async_copy(piece, table.at[pl.ds(at, count)], sems.at[i])
        )
        at += count
    later = [
        pltpu.make_async_copy(pre_hbm, pre, late.at[0]),
        pltpu.make_async_copy(weights_hbm, weights, late.at[1]),
        pltpu.make_async_copy(inputs_hbm, inputs, late.at[2]),
    ]
    for copy in copies + later:
        copy.start()
    for copy in copies:
        copy.wait()
    sub = lax.broadcasted_iota(jnp.int32, (8, C), 0)
    shift = offset[...]

    def read_first(br, carry):
        for g in range(GROUPS):
            high_a, low_a = split(table[slots[br, 2 * g]])
            high_b, low_b = split(table[slots[br, 2 * g + 1]])
            right = jnp.concatenate(
                [
                    jnp.concatenate([high_a, high_b], axis=1),
                    jnp.concatenate([low_a, low_b], axis=1),
                ],
                axis=0,
            )
            pairs[br * GROUPS + g] = right
            first[br, 8 * g : 8 * g + 8] = readout(
                ext[pl.ds(br * BS, BS), 8 * g : 8 * g + 8],
                right,
                flags[br, 2 * g].astype(jnp.float32),
                flags[br, 2 * g + 1].astype(jnp.float32),
                shift,
                sub,
            )
        return carry

    lax.fori_loop(0, BROWS, read_first, 0)
    later[0].wait()

    def update(row, br):
        field[row + 1] = 0.5 * ext[row + HALO] + jnp.tanh(pre[row + 2] + first[br])

    update(-1, 0)
    update(TR, BROWS - 1)

    def update_block(br, carry):
        for r in range(BS):
            update(br * BS + r, br + 1)
        return carry

    lax.fori_loop(0, TR // BS, update_block, 0)
    field[0] = field[0] * (me[0] > 0).astype(jnp.float32)
    field[TR + 1] = field[TR + 1] * (me[0] < me[2]).astype(jnp.float32)
    edge = lax.broadcasted_iota(jnp.int32, (TR + 2, 8, C), 1)
    kept = jnp.where(
        edge < 4, (me[1] < me[3]).astype(jnp.float32), (me[1] > 0).astype(jnp.float32)
    )
    field[:, TC:] = field[:, TC:] * kept

    def read_second(br, carry):
        for g in range(TC // 8):
            second[br, 8 * g : 8 * g + 8] = readout(
                field[pl.ds(br * BS + 1, BS), 8 * g : 8 * g + 8],
                pairs[(br + 1) * GROUPS + g],
                flags[17 + br, 2 * g].astype(jnp.float32),
                flags[17 + br, 2 * g + 1].astype(jnp.float32),
                shift,
                sub,
            )
        return carry

    lax.fori_loop(0, TR // BS, read_second, 0)
    later[1].wait()
    later[2].wait()
    rows = 8

    def finish(i, carry):
        start = i * rows
        sums = conv_chunk(
            lambda a: field[pl.ds(start + a, rows)], weights[...], rows
        )[:, :TC]
        for half in range(rows // BS):
            at = start + half * BS
            out[pl.ds(at, BS)] = 0.5 * field[pl.ds(at + 1, BS), :TC] + jnp.tanh(
                sums[half * BS : (half + 1) * BS]
                + inputs[pl.ds(at, BS)]
                + second[i * (rows // BS) + half][None]
            )
        return carry

    lax.fori_loop(0, TR // rows, finish, 0)


def decode(
    state,
    syndromes,
    erased,
    readers,
    conv_weight,
    syndrome_table,
    erasure_vector,
    read_weight,
    erasure_offset,
):
    f32 = jnp.float32
    gx, gy = lax.axis_index("gx"), lax.axis_index("gy")
    gx_count, gy_count = lax.axis_size("gx"), lax.axis_size("gy")
    me = jnp.stack([gx, gy, gx_count - 1, gy_count - 1]).astype(jnp.int32)
    names = readers.reshape(1, -1)
    lost_vector, offset = erasure_vector[None], erasure_offset[None]
    vmem = pl.BlockSpec(memory_space=pltpu.VMEM)
    smem = pl.BlockSpec(memory_space=pltpu.SMEM)
    anywhere = pl.BlockSpec(memory_space=pl.ANY)

    def shape(*dims, dtype=f32):
        return jax.ShapeDtypeStruct(dims, dtype)

    up_pay, down_pay, copies = pl.pallas_call(
        rows_kernel,
        name="pack_rows",
        out_shape=(
            shape(HALO + 1, TC, C),
            shape(HALO + 1, TC, C),
            shape(16, C, C),
        ),
        in_specs=[anywhere, vmem, vmem, vmem, vmem],
        out_specs=(vmem, vmem, anywhere),
        scratch_shapes=[pltpu.SemaphoreType.DMA((2,)), pltpu.SemaphoreType.DMA((16,))],
    )(state, read_weight, syndromes, erased, names)

    up = [(i, i - 1) for i in range(1, gx_count)]
    down = [(i, i + 1) for i in range(gx_count - 1)]
    top = lax.ppermute(down_pay, "gx", down)
    bottom = lax.ppermute(up_pay, "gx", up)

    west_pay, east_pay, code, lost, ids = pl.pallas_call(
        cols_kernel,
        name="pack_cols",
        out_shape=(
            shape(TALL, 8, C),
            shape(TALL, 8, C),
            shape(TALL, TC),
            shape(16, C),
            shape(16, C),
        ),
        in_specs=[vmem] * 8,
        out_specs=(vmem,) * 5,
        scratch_shapes=[pltpu.VMEM((TALL + 32, C), f32)],
    )(state, top, bottom, syndromes, erased, names, syndrome_table, lost_vector)

    west = [(i, i - 1) for i in range(1, gy_count)]
    east = [(i, i + 1) for i in range(gy_count - 1)]
    left = lax.ppermute(east_pay, "gy", east)
    right = lax.ppermute(west_pay, "gy", west)
    pieces = gather_weights(copies)

    ext, pre, inputs, weights, slots, flags = pl.pallas_call(
        first_kernel,
        name="conv_first",
        out_shape=(
            shape(TALL, WIDE, C),
            shape(CONV_ROWS, WIDE, C),
            shape(TR, TC, C),
            shape(9 * C, 3 * C, dtype=jnp.bfloat16),
            shape(16, C, dtype=jnp.int32),
            shape(32, C, dtype=jnp.int32),
        ),
        in_specs=[smem] + [vmem] * 13,
        out_specs=(vmem,) * 6,
        scratch_shapes=[pltpu.VMEM((C, C), f32), pltpu.VMEM((C, C), f32), pltpu.VMEM((64, C), f32)],
        cost_estimate=pl.CostEstimate(
            flops=2_000_000_000, bytes_accessed=6_000_000, transcendentals=0
        ),
    )(
        me,
        state,
        top,
        bottom,
        right,
        left,
        conv_weight,
        code,
        lost,
        ids,
        syndromes,
        erased,
        syndrome_table,
        lost_vector,
    )

    return pl.pallas_call(
        second_kernel,
        name="read_and_finish",
        out_shape=shape(TR, TC, C),
        in_specs=[smem] * 3 + [vmem] + [anywhere] * 18,
        out_specs=vmem,
        scratch_shapes=[
            pltpu.VMEM((128, C, C), f32),
            pltpu.VMEM((BROWS * GROUPS, 2 * C, 2 * C), jnp.bfloat16),
            pltpu.VMEM((BROWS, WIDE, C), f32),
            pltpu.VMEM((TR + 2, WIDE, C), f32),
            pltpu.VMEM((TR // BS, TC, C), f32),
            pltpu.VMEM((TALL, WIDE, C), f32),
            pltpu.VMEM((CONV_ROWS, WIDE, C), f32),
            pltpu.VMEM((TR, TC, C), f32),
            pltpu.VMEM((9 * C, 3 * C), jnp.bfloat16),
            pltpu.SemaphoreType.DMA((15,)),
            pltpu.SemaphoreType.DMA((3,)),
        ],
        cost_estimate=pl.CostEstimate(
            flops=4_000_000_000, bytes_accessed=12_000_000, transcendentals=1_000_000
        ),
    )(slots, flags, me, offset, ext, pre, inputs, weights, *pieces)


def solution(mesh):
    placed = (
        P("gx", "gy", None),
        P(None, "gx", "gy"),
        P(None, "gx", "gy"),
        P(("gx", "gy"), None),
        P(),
        P(),
        P(),
        P(("gx", "gy"), None),
        P(),
    )
    return jax.shard_map(
        decode, mesh=mesh, in_specs=placed, out_specs=P("gx", "gy", None), check_vma=False
    )
```

time: 94.1 us -> 110 us (1.17)
  the two profiles are of different devices: /device:TPU:33 before, /device:TPU:1 now
where the time goes in v1:
time: 110 us; the launch traced here: 109 us
  waiting for transfers between devices  42.4 us (39%)
  starting transfers between devices  32.5 us (30%)
  Pallas kernels  31 us (28%)
  local copies, waits for them, and re-layouts  2.73 us (2%)
    pallas_call x1, Pallas kernels, decode(): pl.pallas_call(second_kernel, name='read_and_finish', out_shape=shape(TR,...  17.3 us
    all_to_all x1, waiting for transfers between devices, gather_weights(): lax.all_to_all(copies, AX, 0, 0, tiled=True, axis_index_groups=class_grou...  14.6 us
    ppermute x3, waiting for transfers between devices, gather_weights(): pieces.append(lax.ppermute(low, AX, moved(*step)))  11.4 us
    all_to_all x1, starting transfers between devices, gather_weights(): lax.all_to_all(copies, AX, 0, 0, tiled=True, axis_index_groups=class_grou...  11 us
    ppermute x1, waiting for transfers between devices, decode(): bottom = lax.ppermute(up_pay, 'gx', up)  9.03 us
    pallas_call x1, Pallas kernels, decode(): pl.pallas_call(first_kernel, name='conv_first', out_shape=(shape(TALL, WI...  8.24 us
    ppermute x1, starting transfers between devices, decode(): right = lax.ppermute(west_pay, 'gy', west)  4.81 us
    ppermute x1, waiting for transfers between devices, decode(): right = lax.ppermute(west_pay, 'gy', west)  4.77 us
  transfers between devices with their start and end apart: 18, of which 6 were waited for; matrix products, arithmetic and copies ran while one was open for 1% of the time, Pallas kernels for 10%

profile of v1, /device:TPU:1, one launch (start us, length us, event | category | flops | bytes accessed | tf_op | source)
XLA Modules:
  0.0 109.4 jit_solution(35086350351189043)
XLA Ops:
  0.0 3.0 %pack_rows.1 = (f32[5,64,128]{2,1,0:T(8,128)}, f32[5,64,128]{2,1,0:T(8,128)}, f32[16,128,128]{2,1,0:T(8,128)}) custom-call(f32[32,64,128]{2,1,0:T(8,128)} %state.5, f32[128,128]{1,0:T(8,128)} %weight.1, s32[2,32,64]{2,1,0:T(8,128)} %syndromes.5, s32[2,8,16]{2,1,0:T(8,128)} %erased.5, s32[1,128]{1,0:T(1,128)} %bitcast.5), custom_call_target="tpu_custom_call" | custom-call | tf_op jit(solution)/shard_map/pack_rows/pallas_call | solution.py:441
  3.0 0.0 copy-start.10
  3.0 11.0 %all-to-all-start = ((f32[16,128,128]{2,1,0:T(8,128)}), f32[16,128,128]{2,1,0:T(8,128)S(1)}, u32[]{:S(2)}, u32[]{:S(2)}) async-start(f32[16,128,128]{2,1,0:T(8,128)} %get-tuple-element.32), calls=%async_computation | async-start | bytes 2097152 | tf_op jit(solution)/shard_map/all_to_all | solution.py:48
  14.1 0.0 copy-start.9
  14.1 0.0 copy-done.10
  14.1 2.4 %collective-permute-start = (f32[5,64,128]{2,1,0:T(8,128)S(1)}, f32[5,64,128]{2,1,0:T(8,128)S(1)}, u32[]{:S(2)}, u32[]{:S(2)}) collective-permute-start(f32[5,64,128]{2,1,0:T(8,128)S(1)} %copy-done.10), channel_id=1, source_target_pairs={{0,8},{8,16},{16,24},{24,32},{32,40},{40,48},{48,56},{56,64},{64,7... | collective-permute-start | bytes 491528 | tf_op jit(solution)/shard_map/ppermute | solution.py:456
  16.6 14.6 %all-to-all-done.rest_0_ = f32[16,128,128]{2,1,0:T(8,128)S(1)} async-done(((f32[16,128,128]{2,1,0:T(8,128)}), f32[16,128,128]{2,1,0:T(8,128)S(1)}, u32[]{:S(2)}, u32[]{:S(2)}) %all-to-all-start) | async-done | bytes 1048608 | tf_op jit(solution)/shard_map/all_to_all | solution.py:48
  31.1 0.0 copy-start
  31.1 0.1 fusion
  31.2 0.2 collective-permute-start.9
  31.4 1.4 %collective-permute-start.7 = (f32[8,128,128]{2,1,0:T(8,128)S(1)}, f32[8,128,128]{2,1,0:T(8,128)}, u32[]{:S(2)}, u32[]{:S(2)}) collective-permute-start(f32[8,128,128]{2,1,0:T(8,128)S(1)} %get-tuple-element.33), channel_id=1, source_target_pairs={{0,24},{1,25},{2,26},{3,27},{4,28},{5,29},{6,30},{7,31},{8,0},{9,1... | collective-permute-start | bytes 1572872 | tf_op jit(solution)/shard_map/ppermute | solution.py:54
  32.8 3.2 %collective-permute-start.5 = (f32[8,128,128]{2,1,0:T(8,128)S(1)}, f32[8,128,128]{2,1,0:T(8,128)}, u32[]{:S(2)}, u32[]{:S(2)}) collective-permute-start(f32[8,128,128]{2,1,0:T(8,128)S(1)} %get-tuple-element.33), channel_id=1, source_target_pairs={{0,6},{1,7},{2,0},{3,1},{4,2},{5,3},{6,4},{7,5},{8,14},{9,15},{10,... | collective-permute-start | bytes 1572872 | tf_op jit(solution)/shard_map/ppermute | solution.py:54
  36.0 0.0 collective-permute-start.8
  36.0 0.0 collective-permute-done.top
  36.0 0.0 copy-start.1
  36.0 0.0 copy-done.9
  36.0 1.3 %collective-permute-start.1 = (f32[5,64,128]{2,1,0:T(8,128)S(1)}, f32[5,64,128]{2,1,0:T(8,128)S(1)}, u32[]{:S(2)}, u32[]{:S(2)}) collective-permute-start(f32[5,64,128]{2,1,0:T(8,128)S(1)} %copy-done.9), channel_id=1, source_target_pairs={{8,0},{16,8},{24,16},{32,24},{40,32},{48,40},{56,48},{64,56},{72,6... | collective-permute-start | bytes 491528 | tf_op jit(solution)/shard_map/ppermute | solution.py:457
  37.3 9.0 %collective-permute-done.1.bottom = f32[5,64,128]{2,1,0:T(8,128)S(1)} collective-permute-done((f32[5,64,128]{2,1,0:T(8,128)S(1)}, f32[5,64,128]{2,1,0:T(8,128)S(1)}, u32[]{:S(2)}, u32[]{:S(2)}) %collective-permute-start.1) | collective-permute-done | bytes 163872 | tf_op jit(solution)/shard_map/ppermute | solution.py:457
  46.3 0.0 copy-start.2
  46.3 0.0 copy-done.1
  46.3 0.7 copy-done.2
  47.0 2.5 %pack_cols.1 = (f32[40,8,128]{2,1,0:T(8,128)}, f32[40,8,128]{2,1,0:T(8,128)}, f32[40,64]{1,0:T(8,128)}, f32[16,128]{1,0:T(8,128)}, f32[16,128]{1,0:T(8,128)}) custom-call(f32[32,64,128]{2,1,0:T(8,128)} %state.5, f32[5,64,128]{2,1,0:T(8,128)} %copy-done.1, f32[5,64,128]{2,1,0:T(8,128)} %copy-done.2, s32[2,32,64]{2,1,0:T(8,128)} %syndromes.5, ...), custom_call_target="tpu_custom_call" | custom-call | tf_op jit(solution)/shard_map/pack_cols/pallas_call | solution.py:459
  49.5 4.8 %collective-permute-start.2 = (f32[40,8,128]{2,1,0:T(8,128)}, f32[40,8,128]{2,1,0:T(8,128)S(1)}, u32[]{:S(2)}, u32[]{:S(2)}) collective-permute-start(f32[40,8,128]{2,1,0:T(8,128)} %get-tuple-element.21), channel_id=1, source_target_pairs={{1,0},{2,1},{3,2},{4,3},{5,4},{6,5},{7,6},{9,8},{10,9},{11,10},{12... | collective-permute-start | bytes 491528 | tf_op jit(solution)/shard_map/ppermute | solution.py:477
  54.3 4.8 %collective-permute-done.2.right = f32[40,8,128]{2,1,0:T(8,128)S(1)} collective-permute-done((f32[40,8,128]{2,1,0:T(8,128)}, f32[40,8,128]{2,1,0:T(8,128)S(1)}, u32[]{:S(2)}, u32[]{:S(2)}) %collective-permute-start.2) | collective-permute-done | bytes 163872 | tf_op jit(solution)/shard_map/ppermute | solution.py:477
  59.1 0.0 copy-start.7
  59.1 1.9 %collective-permute-start.3 = (f32[40,8,128]{2,1,0:T(8,128)}, f32[40,8,128]{2,1,0:T(8,128)S(1)}, u32[]{:S(2)}, u32[]{:S(2)}) collective-permute-start(f32[40,8,128]{2,1,0:T(8,128)} %get-tuple-element.22), channel_id=1, source_target_pairs={{0,1},{1,2},{2,3},{3,4},{4,5},{5,6},{6,7},{8,9},{9,10},{10,11},{11... | collective-permute-start | bytes 491528 | tf_op jit(solution)/shard_map/ppermute | solution.py:476
  61.0 2.6 %collective-permute-done.3.left = f32[40,8,128]{2,1,0:T(8,128)S(1)} collective-permute-done((f32[40,8,128]{2,1,0:T(8,128)}, f32[40,8,128]{2,1,0:T(8,128)S(1)}, u32[]{:S(2)}, u32[]{:S(2)}) %collective-permute-start.3) | collective-permute-done | bytes 163872 | tf_op jit(solution)/shard_map/ppermute | solution.py:476
  63.5 0.0 copy-start.8
  63.6 1.5 %collective-permute-start.6 = (f32[8,128,128]{2,1,0:T(8,128)S(1)}, f32[8,128,128]{2,1,0:T(8,128)}, u32[]{:S(2)}, u32[]{:S(2)}) collective-permute-start(f32[8,128,128]{2,1,0:T(8,128)S(1)} %get-tuple-element.34), channel_id=1, source_target_pairs={{0,8},{1,9},{2,10},{3,11},{4,12},{5,13},{6,14},{7,15},{8,16},{9,17... | collective-permute-start | bytes 1572872 | tf_op jit(solution)/shard_map/ppermute | solution.py:53
  65.0 0.0 collective-permute-done.9.rest_6_
  65.0 0.0 copy-start.4
  65.0 0.2 collective-permute-start.4
  65.2 0.0 collective-permute-done.7.rest_4_
  65.2 2.9 %collective-permute-start.16 = (f32[8,128,128]{2,1,0:T(8,128)S(1)}, f32[8,128,128]{2,1,0:T(8,128)S(1)}, u32[]{:S(2)}, u32[]{:S(2)}) collective-permute-start(f32[8,128,128]{2,1,0:T(8,128)S(1)} %collective-permute-done.9.rest_6_), channel_id=1, source_target_pairs={{0,1},{1,0},{2,3},{3,2},{4,5},{5,4},{6,7},{7,6},{8,9},{9,8},{10,11... | collective-permute-start | bytes 1572872 | tf_op jit(solution)/shard_map/ppermute | solution.py:55
  68.1 0.0 collective-permute-done.5.rest_2_
  68.1 0.1 collective-permute-start.14
  68.2 0.0 collective-permute-done.8.rest_5_
  68.2 0.0 copy-done
  68.2 0.4 collective-permute-start.10
  68.6 9.8 %collective-permute-done.6.rest_3_ = f32[8,128,128]{2,1,0:T(8,128)} collective-permute-done((f32[8,128,128]{2,1,0:T(8,128)S(1)}, f32[8,128,128]{2,1,0:T(8,128)}, u32[]{:S(2)}, u32[]{:S(2)}) %collective-permute-start.6) | collective-permute-done | bytes 524320 | tf_op jit(solution)/shard_map/ppermute | solution.py:53
  78.4 0.0 collective-permute-start.12
  78.4 1.6 %collective-permute-done.4.rest_1_ = f32[8,128,128]{2,1,0:T(8,128)} collective-permute-done((f32[8,128,128]{2,1,0:T(8,128)S(1)}, f32[8,128,128]{2,1,0:T(8,128)}, u32[]{:S(2)}, u32[]{:S(2)}) %collective-permute-start.4) | collective-permute-done | bytes 524320 | tf_op jit(solution)/shard_map/ppermute | solution.py:53
  80.0 0.7 collective-permute-start.15
  80.7 0.0 collective-permute-done.16.rest_13_
  80.7 0.0 copy-start.5
  80.7 0.8 copy-done.5
  81.5 0.0 collective-permute-start.13
  81.5 0.0 collective-permute-done.14.rest_11_
  81.5 0.5 collective-permute-start.11
  82.0 0.7 pad_add_fusion.me
  82.7 0.0 copy-done.7
  82.7 0.0 copy-done.8
  82.7 8.2 %conv_first.1 = (f32[40,72,128]{2,1,0:T(8,128)}, f32[36,72,128]{2,1,0:T(8,128)}, f32[32,64,128]{2,1,0:T(8,128)}, bf16[1152,384]{1,0:T(8,128)(2,1)}, s32[16,128]{1,0:T(8,128)}, /*index=5*/s32[32,128]{1,0:T(8,128)}) custom-call(s32[4]{0:T(128)} %pad_add_fusion.me, f32[32,64,128]{2,1,0:T(8,128)} %state.5, f32[5,64,128]{2,1,0:T(8,128)} %copy-done.1, ...), custom_call_target="tpu_custom_call" | custom-call | flops 2000000000 | bytes 6000000 | tf_op jit(solution)/shard_map/conv_first/pallas_call | solution.py:480
  90.9 0.0 copy-done.4
  90.9 0.0 collective-permute-done.12.rest_9_
  90.9 0.0 collective-permute-done.15.rest_12_
  90.9 0.0 copy-start.6
  90.9 0.0 collective-permute-done.13.rest_10_
  91.0 0.0 collective-permute-done.11.rest_8_
  91.0 0.0 collective-permute-done.10.rest_7_
  91.0 0.0 copy-start.3
  91.0 0.8 copy-done.6
  91.8 0.4 copy-done.3
  92.1 17.3 %read_and_finish.1 = f32[32,64,128]{2,1,0:T(8,128)} custom-call(s32[16,128]{1,0:T(8,128)} %get-tuple-element.26.slots, s32[32,128]{1,0:T(8,128)} %get-tuple-element.27.flags, s32[4]{0:T(128)} %pad_add_fusion.me, f32[1,128]{1,0:T(1,128)} %bitcast.9, f32[40,72,128]{2,1,0:T(8,128)} %get-tuple-element.28.ext_hbm, f32[36,72,128]{2,1,0:T(8,128)} %get-tuple-element.29.pre_hbm, ...), custom_call_target="tpu_custom_call" | custom-call | flops 4000000000 | bytes 12000000 | tf_op jit(solution)/shard_map/read_and_finish/pallas_call | solution.py:514
Async XLA Ops:
  3.0 11.1 %copy-start.10 = (f32[5,64,128]{2,1,0:T(8,128)S(1)}, f32[5,64,128]{2,1,0:T(8,128)}, u32[]{:S(2)}) copy-start(f32[5,64,128]{2,1,0:T(8,128)} %get-tuple-element.19) | copy-start | bytes 491524
  3.0 28.1 %all-to-all-start = ((f32[16,128,128]{2,1,0:T(8,128)}), f32[16,128,128]{2,1,0:T(8,128)S(1)}, u32[]{:S(2)}, u32[]{:S(2)}) async-start(f32[16,128,128]{2,1,0:T(8,128)} %get-tuple-element.32), calls=%async_computation | async-start | bytes 2097152 | tf_op jit(solution)/shard_map/all_to_all | solution.py:48
  14.1 21.9 %copy-start.9 = (f32[5,64,128]{2,1,0:T(8,128)S(1)}, f32[5,64,128]{2,1,0:T(8,128)}, u32[]{:S(2)}) copy-start(f32[5,64,128]{2,1,0:T(8,128)} %get-tuple-element.20) | copy-start | bytes 491524
  14.1 21.9 %collective-permute-start = (f32[5,64,128]{2,1,0:T(8,128)S(1)}, f32[5,64,128]{2,1,0:T(8,128)S(1)}, u32[]{:S(2)}, u32[]{:S(2)}) collective-permute-start(f32[5,64,128]{2,1,0:T(8,128)S(1)} %copy-done.10), channel_id=1, source_target_pairs={{0,8},{8,16},{16,24},{24,32},{32,40},{40,48},{48,56},{56,64},{64,7... | collective-permute-start | bytes 491528 | tf_op jit(solution)/shard_map/ppermute | solution.py:456
  31.1 37.0 %copy-start = (f32[16,128,128]{2,1,0:T(8,128)}, f32[16,128,128]{2,1,0:T(8,128)S(1)}, u32[]{:S(2)}) copy-start(f32[16,128,128]{2,1,0:T(8,128)S(1)} %all-to-all-done.rest_0_) | copy-start | bytes 3145732
  31.2 33.8 %collective-permute-start.9 = (f32[8,128,128]{2,1,0:T(8,128)S(1)}, f32[8,128,128]{2,1,0:T(8,128)S(1)}, u32[]{:S(2)}, u32[]{:S(2)}) collective-permute-start(f32[8,128,128]{2,1,0:T(8,128)S(1)} %get-tuple-element.33), channel_id=1, source_target_pairs={{0,96},{1,97},{2,98},{3,99},{4,100},{5,101},{6,102},{7,103},{8,104... | collective-permute-start | bytes 1572872 | tf_op jit(solution)/shard_map/ppermute | solution.py:54
  31.4 33.8 %collective-permute-start.7 = (f32[8,128,128]{2,1,0:T(8,128)S(1)}, f32[8,128,128]{2,1,0:T(8,128)}, u32[]{:S(2)}, u32[]{:S(2)}) collective-permute-start(f32[8,128,128]{2,1,0:T(8,128)S(1)} %get-tuple-element.33), channel_id=1, source_target_pairs={{0,24},{1,25},{2,26},{3,27},{4,28},{5,29},{6,30},{7,31},{8,0},{9,1... | collective-permute-start | bytes 1572872 | tf_op jit(solution)/shard_map/ppermute | solution.py:54
  32.8 35.3 %collective-permute-start.5 = (f32[8,128,128]{2,1,0:T(8,128)S(1)}, f32[8,128,128]{2,1,0:T(8,128)}, u32[]{:S(2)}, u32[]{:S(2)}) collective-permute-start(f32[8,128,128]{2,1,0:T(8,128)S(1)} %get-tuple-element.33), channel_id=1, source_target_pairs={{0,6},{1,7},{2,0},{3,1},{4,2},{5,3},{6,4},{7,5},{8,14},{9,15},{10,... | collective-permute-start | bytes 1572872 | tf_op jit(solution)/shard_map/ppermute | solution.py:54
  36.0 32.2 %collective-permute-start.8 = (f32[8,128,128]{2,1,0:T(8,128)S(1)}, f32[8,128,128]{2,1,0:T(8,128)}, u32[]{:S(2)}, u32[]{:S(2)}) collective-permute-start(f32[8,128,128]{2,1,0:T(8,128)S(1)} %get-tuple-element.34), channel_id=1, source_target_pairs={{0,32},{1,33},{2,34},{3,35},{4,36},{5,37},{6,38},{7,39},{8,40},{9,... | collective-permute-start | bytes 1572872 | tf_op jit(solution)/shard_map/ppermute | solution.py:53
  36.0 10.3 %copy-start.1 = (f32[5,64,128]{2,1,0:T(8,128)}, f32[5,64,128]{2,1,0:T(8,128)S(1)}, u32[]{:S(2)}) copy-start(f32[5,64,128]{2,1,0:T(8,128)S(1)} %collective-permute-done.top) | copy-start | bytes 491524
  36.0 10.3 %collective-permute-start.1 = (f32[5,64,128]{2,1,0:T(8,128)S(1)}, f32[5,64,128]{2,1,0:T(8,128)S(1)}, u32[]{:S(2)}, u32[]{:S(2)}) collective-permute-start(f32[5,64,128]{2,1,0:T(8,128)S(1)} %copy-done.9), channel_id=1, source_target_pairs={{8,0},{16,8},{24,16},{32,24},{40,32},{48,40},{56,48},{64,56},{72,6... | collective-permute-start | bytes 491528 | tf_op jit(solution)/shard_map/ppermute | solution.py:457
  46.3 0.7 copy-start.2
  49.5 9.6 %collective-permute-start.2 = (f32[40,8,128]{2,1,0:T(8,128)}, f32[40,8,128]{2,1,0:T(8,128)S(1)}, u32[]{:S(2)}, u32[]{:S(2)}) collective-permute-start(f32[40,8,128]{2,1,0:T(8,128)} %get-tuple-element.21), channel_id=1, source_target_pairs={{1,0},{2,1},{3,2},{4,3},{5,4},{6,5},{7,6},{9,8},{10,9},{11,10},{12... | collective-permute-start | bytes 491528 | tf_op jit(solution)/shard_map/ppermute | solution.py:477
  59.1 23.6 %copy-start.7 = (f32[40,8,128]{2,1,0:T(8,128)}, f32[40,8,128]{2,1,0:T(8,128)S(1)}, u32[]{:S(2)}) copy-start(f32[40,8,128]{2,1,0:T(8,128)S(1)} %collective-permute-done.2.right) | copy-start | bytes 491524
  59.1 4.5 %collective-permute-start.3 = (f32[40,8,128]{2,1,0:T(8,128)}, f32[40,8,128]{2,1,0:T(8,128)S(1)}, u32[]{:S(2)}, u32[]{:S(2)}) collective-permute-start(f32[40,8,128]{2,1,0:T(8,128)} %get-tuple-element.22), channel_id=1, source_target_pairs={{0,1},{1,2},{2,3},{3,4},{4,5},{5,6},{6,7},{8,9},{9,10},{10,11},{11... | collective-permute-start | bytes 491528 | tf_op jit(solution)/shard_map/ppermute | solution.py:476
  63.5 19.1 %copy-start.8 = (f32[40,8,128]{2,1,0:T(8,128)}, f32[40,8,128]{2,1,0:T(8,128)S(1)}, u32[]{:S(2)}) copy-start(f32[40,8,128]{2,1,0:T(8,128)S(1)} %collective-permute-done.3.left) | copy-start | bytes 491524
  63.6 14.9 %collective-permute-start.6 = (f32[8,128,128]{2,1,0:T(8,128)S(1)}, f32[8,128,128]{2,1,0:T(8,128)}, u32[]{:S(2)}, u32[]{:S(2)}) collective-permute-start(f32[8,128,128]{2,1,0:T(8,128)S(1)} %get-tuple-element.34), channel_id=1, source_target_pairs={{0,8},{1,9},{2,10},{3,11},{4,12},{5,13},{6,14},{7,15},{8,16},{9,17... | collective-permute-start | bytes 1572872 | tf_op jit(solution)/shard_map/ppermute | solution.py:53
  65.0 25.9 %copy-start.4 = (f32[8,128,128]{2,1,0:T(8,128)}, f32[8,128,128]{2,1,0:T(8,128)S(1)}, u32[]{:S(2)}) copy-start(f32[8,128,128]{2,1,0:T(8,128)S(1)} %collective-permute-done.9.rest_6_) | copy-start | bytes 1572868
  65.0 15.0 %collective-permute-start.4 = (f32[8,128,128]{2,1,0:T(8,128)S(1)}, f32[8,128,128]{2,1,0:T(8,128)}, u32[]{:S(2)}, u32[]{:S(2)}) collective-permute-start(f32[8,128,128]{2,1,0:T(8,128)S(1)} %get-tuple-element.34), channel_id=1, source_target_pairs={{0,2},{1,3},{2,4},{3,5},{4,6},{5,7},{6,0},{7,1},{8,10},{9,11},{10,... | collective-permute-start | bytes 1572872 | tf_op jit(solution)/shard_map/ppermute | solution.py:53
  65.2 15.5 %collective-permute-start.16 = (f32[8,128,128]{2,1,0:T(8,128)S(1)}, f32[8,128,128]{2,1,0:T(8,128)S(1)}, u32[]{:S(2)}, u32[]{:S(2)}) collective-permute-start(f32[8,128,128]{2,1,0:T(8,128)S(1)} %collective-permute-done.9.rest_6_), channel_id=1, source_target_pairs={{0,1},{1,0},{2,3},{3,2},{4,5},{5,4},{6,7},{7,6},{8,9},{9,8},{10,11... | collective-permute-start | bytes 1572872 | tf_op jit(solution)/shard_map/ppermute | solution.py:55
  68.1 13.4 %collective-permute-start.14 = (f32[8,128,128]{2,1,0:T(8,128)}, f32[8,128,128]{2,1,0:T(8,128)}, u32[]{:S(2)}, u32[]{:S(2)}) collective-permute-start(f32[8,128,128]{2,1,0:T(8,128)} %collective-permute-done.7.rest_4_), channel_id=1, source_target_pairs={{0,1},{1,0},{2,3},{3,2},{4,5},{5,4},{6,7},{7,6},{8,9},{9,8},{10,11... | collective-permute-start | bytes 1572872 | tf_op jit(solution)/shard_map/ppermute | solution.py:55
  68.2 22.8 %collective-permute-start.10 = (f32[16,128,128]{2,1,0:T(8,128)S(1)}, f32[16,128,128]{2,1,0:T(8,128)S(1)}, u32[]{:S(2)}, u32[]{:S(2)}) collective-permute-start(f32[16,128,128]{2,1,0:T(8,128)S(1)} %all-to-all-done.rest_0_), channel_id=1, source_target_pairs={{0,1},{1,0},{2,3},{3,2},{4,5},{5,4},{6,7},{7,6},{8,9},{9,8},{10,11... | collective-permute-start | bytes 3145736 | tf_op jit(solution)/shard_map/ppermute | solution.py:55
  78.4 12.5 %collective-permute-start.12 = (f32[8,128,128]{2,1,0:T(8,128)}, f32[8,128,128]{2,1,0:T(8,128)}, u32[]{:S(2)}, u32[]{:S(2)}) collective-permute-start(f32[8,128,128]{2,1,0:T(8,128)} %collective-permute-done.5.rest_2_), channel_id=1, source_target_pairs={{0,1},{1,0},{2,3},{3,2},{4,5},{5,4},{6,7},{7,6},{8,9},{9,8},{10,11... | collective-permute-start | bytes 1572872 | tf_op jit(solution)/shard_map/ppermute | solution.py:55
  80.0 10.9 %collective-permute-start.15 = (f32[8,128,128]{2,1,0:T(8,128)}, f32[8,128,128]{2,1,0:T(8,128)S(1)}, u32[]{:S(2)}, u32[]{:S(2)}) collective-permute-start(f32[8,128,128]{2,1,0:T(8,128)} %collective-permute-done.8.rest_5_), channel_id=1, source_target_pairs={{0,1},{1,0},{2,3},{3,2},{4,5},{5,4},{6,7},{7,6},{8,9},{9,8},{10,11... | collective-permute-start | bytes 1572872 | tf_op jit(solution)/shard_map/ppermute | solution.py:55
  80.7 0.8 copy-start.5
  81.5 9.5 %collective-permute-start.13 = (f32[8,128,128]{2,1,0:T(8,128)}, f32[8,128,128]{2,1,0:T(8,128)}, u32[]{:S(2)}, u32[]{:S(2)}) collective-permute-start(f32[8,128,128]{2,1,0:T(8,128)} %collective-permute-done.6.rest_3_), channel_id=1, source_target_pairs={{0,1},{1,0},{2,3},{3,2},{4,5},{5,4},{6,7},{7,6},{8,9},{9,8},{10,11... | collective-permute-start | bytes 1572872 | tf_op jit(solution)/shard_map/ppermute | solution.py:55
  81.5 9.5 %collective-permute-start.11 = (f32[8,128,128]{2,1,0:T(8,128)}, f32[8,128,128]{2,1,0:T(8,128)}, u32[]{:S(2)}, u32[]{:S(2)}) collective-permute-start(f32[8,128,128]{2,1,0:T(8,128)} %collective-permute-done.4.rest_1_), channel_id=1, source_target_pairs={{0,1},{1,0},{2,3},{3,2},{4,5},{5,4},{6,7},{7,6},{8,9},{9,8},{10,11... | collective-permute-start | bytes 1572872 | tf_op jit(solution)/shard_map/ppermute | solution.py:55
  90.9 0.8 copy-start.6
  91.0 1.1 %copy-start.3 = (f32[16,128,128]{2,1,0:T(8,128)}, f32[16,128,128]{2,1,0:T(8,128)S(1)}, u32[]{:S(2)}) copy-start(f32[16,128,128]{2,1,0:T(8,128)S(1)} %collective-permute-done.10.rest_7_) | copy-start | bytes 3145732

commit v2 on v1

--- a/solution.py
+++ b/solution.py
@@ -67,14 +67,15 @@
         high, low = split(read(a).reshape(rows * WIDE, C))
         highs.append(high)
         lows.append(low)
-    left = jnp.concatenate(highs + highs + lows, axis=1)
-    sums = jnp.dot(left, weights, preferred_element_type=jnp.float32)
-    sums = sums.reshape(rows, WIDE, 3 * C)
-    return (
-        pltpu.roll(sums[:, :, :C], 1, 1)
-        + sums[:, :, C : 2 * C]
-        + pltpu.roll(sums[:, :, 2 * C :], WIDE - 1, 1)
-    )
+    left = jnp.concatenate(highs + lows, axis=1)
+    near = jnp.dot(left, weights[:, : 4 * C], preferred_element_type=jnp.float32)
+    far = jnp.dot(left[:, : 4 * C], weights[: 4 * C, 4 * C :], preferred_element_type=jnp.float32)
+    sums = [
+        (near[:, :C] + near[:, 3 * C :]).reshape(rows, WIDE, C),
+        (near[:, C : 2 * C] + far[:, :C]).reshape(rows, WIDE, C),
+        (near[:, 2 * C : 3 * C] + far[:, C:]).reshape(rows, WIDE, C),
+    ]
+    return pltpu.roll(sums[0], 1, 1) + sums[1] + pltpu.roll(sums[2], WIDE - 1, 1)
 
 
 def rows_kernel(
@@ -223,9 +224,11 @@
         for b in range(3):
             high, low = split(taps[3 * a + b])
             cols = slice(b * C, (b + 1) * C)
+            lows = slice((3 + b) * C, (4 + b) * C)
             weights_out[a * C : (a + 1) * C, cols] = high
-            weights_out[(3 + a) * C : (4 + a) * C, cols] = low
-            weights_out[(6 + a) * C : (7 + a) * C, cols] = high
+            weights_out[a * C : (a + 1) * C, lows] = low
+            weights_out[(3 + a) * C : (4 + a) * C, cols] = high
+            weights_out[(3 + a) * C : (4 + a) * C, lows] = jnp.zeros((C, C), jnp.bfloat16)
 
     for r in range(BROWS):
         names[r : r + 1] = right[r, 5:6, :]
@@ -315,38 +318,36 @@
     slots, flags, me, offset, ext_hbm, pre_hbm, inputs_hbm, weights_hbm, *rest
 ):
     pieces = rest[:14]
-    out, table, pairs, first, field, second, ext, pre, inputs, weights, sems, late = rest[14:]
-    copies = [pltpu.make_async_copy(ext_hbm, ext, sems.at[14])]
+    out, table, first, field, second, ext, pre, inputs, weights, sems = rest[14:]
+    later = [
+        pltpu.make_async_copy(ext_hbm, ext, sems.at[0]),
+        pltpu.make_async_copy(pre_hbm, pre, sems.at[1]),
+        pltpu.make_async_copy(weights_hbm, weights, sems.at[2]),
+        pltpu.make_async_copy(inputs_hbm, inputs, sems.at[3]),
+    ]
+    for copy in later:
+        copy.start()
     at = 0
-    for i, (piece, count) in enumerate(zip(pieces, PIECES)):
-        copies.append(
-            pltpu.make_async_copy(piece, table.at[pl.ds(at, count)], sems.at[i])
-        )
+    for piece, count in zip(pieces, PIECES):
+
+        def halve(i, carry, piece=piece, at=at):
+            for k in range(4):
+                high, low = split(piece[4 * i + k])
+                table[at + 4 * i + k, :C] = high
+                table[at + 4 * i + k, C:] = low
+            return carry
+
+        lax.fori_loop(0, count // 4, halve, 0)
         at += count
-    later = [
-        pltpu.make_async_copy(pre_hbm, pre, late.at[0]),
-        pltpu.make_async_copy(weights_hbm, weights, late.at[1]),
-        pltpu.make_async_copy(inputs_hbm, inputs, late.at[2]),
-    ]
-    for copy in copies + later:
-        copy.start()
-    for copy in copies:
-        copy.wait()
+    later[0].wait()
     sub = lax.broadcasted_iota(jnp.int32, (8, C), 0)
     shift = offset[...]
 
-    def read_first(br, carry):
-        for g in range(GROUPS):
-            high_a, low_a = split(table[slots[br, 2 * g]])
-            high_b, low_b = split(table[slots[br, 2 * g + 1]])
+    def read_first(step, carry):
+        for br, g in [(5 * step + k, g) for k in range(5) for g in range(GROUPS)]:
             right = jnp.concatenate(
-                [
-                    jnp.concatenate([high_a, high_b], axis=1),
-                    jnp.concatenate([low_a, low_b], axis=1),
-                ],
-                axis=0,
+                [table[slots[br, 2 * g]], table[slots[br, 2 * g + 1]]], axis=1
             )
-            pairs[br * GROUPS + g] = right
             first[br, 8 * g : 8 * g + 8] = readout(
                 ext[pl.ds(br * BS, BS), 8 * g : 8 * g + 8],
                 right,
@@ -357,8 +358,9 @@
             )
         return carry
 
-    lax.fori_loop(0, BROWS, read_first, 0)
-    later[0].wait()
+    lax.fori_loop(0, BROWS // 5, read_first, 0)
+
+    later[1].wait()
 
     def update(row, br):
         field[row + 1] = 0.5 * ext[row + HALO] + jnp.tanh(pre[row + 2] + first[br])
@@ -380,11 +382,13 @@
     )
     field[:, TC:] = field[:, TC:] * kept
 
-    def read_second(br, carry):
-        for g in range(TC // 8):
+    def read_second(step, carry):
+        for br, g in [(4 * step + k, g) for k in range(4) for g in range(TC // 8)]:
             second[br, 8 * g : 8 * g + 8] = readout(
                 field[pl.ds(br * BS + 1, BS), 8 * g : 8 * g + 8],
-                pairs[(br + 1) * GROUPS + g],
+                jnp.concatenate(
+                    [table[slots[br + 1, 2 * g]], table[slots[br + 1, 2 * g + 1]]], axis=1
+                ),
                 flags[17 + br, 2 * g].astype(jnp.float32),
                 flags[17 + br, 2 * g + 1].astype(jnp.float32),
                 shift,
@@ -392,9 +396,9 @@
             )
         return carry
 
-    lax.fori_loop(0, TR // BS, read_second, 0)
-    later[1].wait()
+    lax.fori_loop(0, TR // BS // 4, read_second, 0)
     later[2].wait()
+    later[3].wait()
     rows = 8
 
     def finish(i, carry):
@@ -434,6 +438,7 @@
     vmem = pl.BlockSpec(memory_space=pltpu.VMEM)
     smem = pl.BlockSpec(memory_space=pltpu.SMEM)
     anywhere = pl.BlockSpec(memory_space=pl.ANY)
+    hbm = pl.BlockSpec(memory_space=pltpu.HBM)
 
     def shape(*dims, dtype=f32):
         return jax.ShapeDtypeStruct(dims, dtype)
@@ -484,7 +489,7 @@
             shape(TALL, WIDE, C),
             shape(CONV_ROWS, WIDE, C),
             shape(TR, TC, C),
-            shape(9 * C, 3 * C, dtype=jnp.bfloat16),
+            shape(6 * C, 6 * C, dtype=jnp.bfloat16),
             shape(16, C, dtype=jnp.int32),
             shape(32, C, dtype=jnp.int32),
         ),
@@ -514,21 +519,20 @@
     return pl.pallas_call(
         second_kernel,
         name="read_and_finish",
+        compiler_params=pltpu.CompilerParams(vmem_limit_bytes=47 * 2**20),
         out_shape=shape(TR, TC, C),
-        in_specs=[smem] * 3 + [vmem] + [anywhere] * 18,
+        in_specs=[smem] * 3 + [vmem] + [hbm] * 4 + [vmem] * 14,
         out_specs=vmem,
         scratch_shapes=[
-            pltpu.VMEM((128, C, C), f32),
-            pltpu.VMEM((BROWS * GROUPS, 2 * C, 2 * C), jnp.bfloat16),
+            pltpu.VMEM((128, 2 * C, C), jnp.bfloat16),
             pltpu.VMEM((BROWS, WIDE, C), f32),
             pltpu.VMEM((TR + 2, WIDE, C), f32),
             pltpu.VMEM((TR // BS, TC, C), f32),
             pltpu.VMEM((TALL, WIDE, C), f32),
             pltpu.VMEM((CONV_ROWS, WIDE, C), f32),
             pltpu.VMEM((TR, TC, C), f32),
-            pltpu.VMEM((9 * C, 3 * C), jnp.bfloat16),
-            pltpu.SemaphoreType.DMA((15,)),
-            pltpu.SemaphoreType.DMA((3,)),
+            pltpu.VMEM((6 * C, 6 * C), jnp.bfloat16),
+            pltpu.SemaphoreType.DMA((4,)),
         ],
         cost_estimate=pl.CostEstimate(
             flops=4_000_000_000, bytes_accessed=12_000_000, transcendentals=1_000_000

time: 110 us -> 109 us (level)
  Pallas kernels: 31 us -> 25.4 us
  local copies, waits for them, and re-layouts: 2.73 us -> 7.09 us
    pallas_call x1, Pallas kernels: 17.3 us -> 12.2 us  [decode(): pl.pallas_call(second_kernel, name='read_and_finish', compiler_params=plt...]
    unnamed x22 -> x30, local copies, waits for them, and re-layouts: 2.66 us -> 5.94 us
  transfers between devices with their start and end apart: 18 -> 18, of which waited for: 6 -> 6; matrix products, arithmetic and copies ran while one was open for 1% -> 2% of each run, Pallas kernels for 10% -> 9%
where the time goes in v2:
time: 109 us; the launch traced here: 108 us
  waiting for transfers between devices  42.6 us (39%)
  starting transfers between devices  32.5 us (30%)
  Pallas kernels  25.4 us (23%)
  local copies, waits for them, and re-layouts  7.09 us (7%)
    all_to_all x1, waiting for transfers between devices, gather_weights(): lax.all_to_all(copies, AX, 0, 0, tiled=True, axis_index_groups=class_grou...  14.6 us
    pallas_call x1, Pallas kernels, decode(): pl.pallas_call(second_kernel, name='read_and_finish', compiler_params=plt...  12.2 us
    ppermute x3, waiting for transfers between devices, gather_weights(): pieces.append(lax.ppermute(low, AX, moved(*step)))  11.5 us
    all_to_all x1, starting transfers between devices, gather_weights(): lax.all_to_all(copies, AX, 0, 0, tiled=True, axis_index_groups=class_grou...  11 us
    ppermute x1, waiting for transfers between devices, decode(): bottom = lax.ppermute(up_pay, 'gx', up)  9.13 us
    pallas_call x1, Pallas kernels, decode(): pl.pallas_call(first_kernel, name='conv_first', out_shape=(shape(TALL, WI...  7.74 us
    unnamed x30, local copies, waits for them, and re-layouts  5.94 us
    ppermute x1, starting transfers between devices, decode(): right = lax.ppermute(west_pay, 'gy', west)  4.91 us
  transfers between devices with their start and end apart: 18, of which 6 were waited for; matrix products, arithmetic and copies ran while one was open for 2% of the time, Pallas kernels for 9%

profile of v2, /device:TPU:1, one launch (start us, length us, event | category | flops | bytes accessed | tf_op | source)
XLA Modules:
  0.0 108.4 jit_solution(13785532994637706102)
XLA Ops:
  0.0 3.0 %pack_rows.1 = (f32[5,64,128]{2,1,0:T(8,128)}, f32[5,64,128]{2,1,0:T(8,128)}, f32[16,128,128]{2,1,0:T(8,128)}) custom-call(f32[32,64,128]{2,1,0:T(8,128)} %state.5, f32[128,128]{1,0:T(8,128)} %weight.1, s32[2,32,64]{2,1,0:T(8,128)} %syndromes.5, s32[2,8,16]{2,1,0:T(8,128)} %erased.5, s32[1,128]{1,0:T(1,128)} %bitcast.6), custom_call_target="tpu_custom_call" | custom-call | tf_op jit(solution)/shard_map/pack_rows/pallas_call | solution.py:446
  3.0 0.0 copy-start.14
  3.1 11.0 %all-to-all-start = ((f32[16,128,128]{2,1,0:T(8,128)}), f32[16,128,128]{2,1,0:T(8,128)S(1)}, u32[]{:S(2)}, u32[]{:S(2)}) async-start(f32[16,128,128]{2,1,0:T(8,128)} %get-tuple-element.32), calls=%async_computation | async-start | bytes 2097152 | tf_op jit(solution)/shard_map/all_to_all | solution.py:48
  14.1 0.0 copy-start.13
  14.1 0.0 copy-done.14
  14.1 2.4 %collective-permute-start = (f32[5,64,128]{2,1,0:T(8,128)S(1)}, f32[5,64,128]{2,1,0:T(8,128)S(1)}, u32[]{:S(2)}, u32[]{:S(2)}) collective-permute-start(f32[5,64,128]{2,1,0:T(8,128)S(1)} %copy-done.14), channel_id=1, source_target_pairs={{0,8},{8,16},{16,24},{24,32},{32,40},{40,48},{48,56},{56,64},{64,7... | collective-permute-start | bytes 491528 | tf_op jit(solution)/shard_map/ppermute | solution.py:461
  16.6 14.6 %all-to-all-done.rest_0_ = f32[16,128,128]{2,1,0:T(8,128)S(1)} async-done(((f32[16,128,128]{2,1,0:T(8,128)}), f32[16,128,128]{2,1,0:T(8,128)S(1)}, u32[]{:S(2)}, u32[]{:S(2)}) %all-to-all-start) | async-done | bytes 1048608 | tf_op jit(solution)/shard_map/all_to_all | solution.py:48
  31.1 0.0 copy-start.8
  31.2 1.2 %fusion = (f32[8,128,128]{2,1,0:T(8,128)}, f32[8,128,128]{2,1,0:T(8,128)}) fusion(f32[16,128,128]{2,1,0:T(8,128)S(1)} %all-to-all-done.rest_0_), kind=kLoop, calls=%fused_computation.1 | loop fusion | bytes 2097152 | tf_op jit(solution)/shard_map/slice | solution.py:49
  32.3 0.2 copy-done.8
  32.5 0.1 collective-permute-start.9
  32.6 1.4 %collective-permute-start.7 = (f32[8,128,128]{2,1,0:T(8,128)}, f32[8,128,128]{2,1,0:T(8,128)S(1)}, u32[]{:S(2)}, u32[]{:S(2)}) collective-permute-start(f32[8,128,128]{2,1,0:T(8,128)} %get-tuple-element.33), channel_id=1, source_target_pairs={{0,24},{1,25},{2,26},{3,27},{4,28},{5,29},{6,30},{7,31},{8,0},{9,1... | collective-permute-start | bytes 1572872 | tf_op jit(solution)/shard_map/ppermute | solution.py:54
  34.0 3.2 %collective-permute-start.5 = (f32[8,128,128]{2,1,0:T(8,128)}, f32[8,128,128]{2,1,0:T(8,128)S(1)}, u32[]{:S(2)}, u32[]{:S(2)}) collective-permute-start(f32[8,128,128]{2,1,0:T(8,128)} %get-tuple-element.33), channel_id=1, source_target_pairs={{0,6},{1,7},{2,0},{3,1},{4,2},{5,3},{6,4},{7,5},{8,14},{9,15},{10,... | collective-permute-start | bytes 1572872 | tf_op jit(solution)/shard_map/ppermute | solution.py:54
  37.1 0.0 collective-permute-start.8
  37.2 0.0 collective-permute-done.top
  37.2 0.0 copy-start.9
  37.2 0.0 copy-done.13
  37.2 1.3 %collective-permute-start.1 = (f32[5,64,128]{2,1,0:T(8,128)S(1)}, f32[5,64,128]{2,1,0:T(8,128)S(1)}, u32[]{:S(2)}, u32[]{:S(2)}) collective-permute-start(f32[5,64,128]{2,1,0:T(8,128)S(1)} %copy-done.13), channel_id=1, source_target_pairs={{8,0},{16,8},{24,16},{32,24},{40,32},{48,40},{56,48},{64,56},{72,6... | collective-permute-start | bytes 491528 | tf_op jit(solution)/shard_map/ppermute | solution.py:462
  38.5 9.1 %collective-permute-done.1.bottom = f32[5,64,128]{2,1,0:T(8,128)S(1)} collective-permute-done((f32[5,64,128]{2,1,0:T(8,128)S(1)}, f32[5,64,128]{2,1,0:T(8,128)S(1)}, u32[]{:S(2)}, u32[]{:S(2)}) %collective-permute-start.1) | collective-permute-done | bytes 163872 | tf_op jit(solution)/shard_map/ppermute | solution.py:462
  47.6 0.0 copy-start.10
  47.6 0.0 copy-done.9
  47.6 0.7 copy-done.10
  48.3 2.5 %pack_cols.1 = (f32[40,8,128]{2,1,0:T(8,128)}, f32[40,8,128]{2,1,0:T(8,128)}, f32[40,64]{1,0:T(8,128)}, f32[16,128]{1,0:T(8,128)}, f32[16,128]{1,0:T(8,128)}) custom-call(f32[32,64,128]{2,1,0:T(8,128)} %state.5, f32[5,64,128]{2,1,0:T(8,128)} %copy-done.9, f32[5,64,128]{2,1,0:T(8,128)} %copy-done.10, s32[2,32,64]{2,1,0:T(8,128)} %syndromes.5, ...), custom_call_target="tpu_custom_call" | custom-call | tf_op jit(solution)/shard_map/pack_cols/pallas_call | solution.py:464
  50.8 4.9 %collective-permute-start.2 = (f32[40,8,128]{2,1,0:T(8,128)}, f32[40,8,128]{2,1,0:T(8,128)S(1)}, u32[]{:S(2)}, u32[]{:S(2)}) collective-permute-start(f32[40,8,128]{2,1,0:T(8,128)} %get-tuple-element.21), channel_id=1, source_target_pairs={{1,0},{2,1},{3,2},{4,3},{5,4},{6,5},{7,6},{9,8},{10,9},{11,10},{12... | collective-permute-start | bytes 491528 | tf_op jit(solution)/shard_map/ppermute | solution.py:482
  55.7 4.8 %collective-permute-done.2.right = f32[40,8,128]{2,1,0:T(8,128)S(1)} collective-permute-done((f32[40,8,128]{2,1,0:T(8,128)}, f32[40,8,128]{2,1,0:T(8,128)S(1)}, u32[]{:S(2)}, u32[]{:S(2)}) %collective-permute-start.2) | collective-permute-done | bytes 163872 | tf_op jit(solution)/shard_map/ppermute | solution.py:482
  60.5 0.0 copy-start.11
  60.5 1.9 %collective-permute-start.3 = (f32[40,8,128]{2,1,0:T(8,128)}, f32[40,8,128]{2,1,0:T(8,128)S(1)}, u32[]{:S(2)}, u32[]{:S(2)}) collective-permute-start(f32[40,8,128]{2,1,0:T(8,128)} %get-tuple-element.22), channel_id=1, source_target_pairs={{0,1},{1,2},{2,3},{3,4},{4,5},{5,6},{6,7},{8,9},{9,10},{10,11},{11... | collective-permute-start | bytes 491528 | tf_op jit(solution)/shard_map/ppermute | solution.py:481
  62.4 2.6 %collective-permute-done.3.left = f32[40,8,128]{2,1,0:T(8,128)S(1)} collective-permute-done((f32[40,8,128]{2,1,0:T(8,128)}, f32[40,8,128]{2,1,0:T(8,128)S(1)}, u32[]{:S(2)}, u32[]{:S(2)}) %collective-permute-start.3) | collective-permute-done | bytes 163872 | tf_op jit(solution)/shard_map/ppermute | solution.py:481
  65.0 1.4 %collective-permute-start.6 = (f32[8,128,128]{2,1,0:T(8,128)}, f32[8,128,128]{2,1,0:T(8,128)S(1)}, u32[]{:S(2)}, u32[]{:S(2)}) collective-permute-start(f32[8,128,128]{2,1,0:T(8,128)} %get-tuple-element.34), channel_id=1, source_target_pairs={{0,8},{1,9},{2,10},{3,11},{4,12},{5,13},{6,14},{7,15},{8,16},{9,17... | collective-permute-start | bytes 1572872 | tf_op jit(solution)/shard_map/ppermute | solution.py:53
  66.4 0.0 collective-permute-done.9.rest_6_
  66.4 0.2 collective-permute-start.4
  66.6 0.0 collective-permute-done.7.rest_4_
  66.6 2.9 %collective-permute-start.16 = (f32[8,128,128]{2,1,0:T(8,128)S(1)}, f32[8,128,128]{2,1,0:T(8,128)S(1)}, u32[]{:S(2)}, u32[]{:S(2)}) collective-permute-start(f32[8,128,128]{2,1,0:T(8,128)S(1)} %collective-permute-done.9.rest_6_), channel_id=1, source_target_pairs={{0,1},{1,0},{2,3},{3,2},{4,5},{5,4},{6,7},{7,6},{8,9},{9,8},{10,11... | collective-permute-start | bytes 1572872 | tf_op jit(solution)/shard_map/ppermute | solution.py:55
  69.5 0.0 collective-permute-done.5.rest_2_
  69.5 0.1 collective-permute-start.14
  69.5 0.0 collective-permute-done.8.rest_5_
  69.5 0.4 collective-permute-start.10
  70.0 10.0 %collective-permute-done.6.rest_3_ = f32[8,128,128]{2,1,0:T(8,128)S(1)} collective-permute-done((f32[8,128,128]{2,1,0:T(8,128)}, f32[8,128,128]{2,1,0:T(8,128)S(1)}, u32[]{:S(2)}, u32[]{:S(2)}) %collective-permute-start.6) | collective-permute-done | bytes 524320 | tf_op jit(solution)/shard_map/ppermute | solution.py:53
  79.9 0.0 collective-permute-start.12
  80.0 1.5 %collective-permute-done.4.rest_1_ = f32[8,128,128]{2,1,0:T(8,128)S(1)} collective-permute-done((f32[8,128,128]{2,1,0:T(8,128)}, f32[8,128,128]{2,1,0:T(8,128)S(1)}, u32[]{:S(2)}, u32[]{:S(2)}) %collective-permute-start.4) | collective-permute-done | bytes 524320 | tf_op jit(solution)/shard_map/ppermute | solution.py:53
  81.5 0.7 collective-permute-start.15
  82.2 0.0 collective-permute-done.16.rest_13_
  82.2 0.8 copy-done.1
  83.0 0.0 collective-permute-start.13
  83.0 0.0 collective-permute-done.14.rest_11_
  83.0 0.8 copy-done.3
  83.8 0.5 collective-permute-start.11
  84.3 0.6 pad_add_fusion.me
  84.9 0.0 copy-done.11
  84.9 0.0 copy-done.12
  84.9 7.7 %conv_first.1 = (f32[40,72,128]{2,1,0:T(8,128)}, f32[36,72,128]{2,1,0:T(8,128)}, f32[32,64,128]{2,1,0:T(8,128)}, bf16[768,768]{1,0:T(8,128)(2,1)}, s32[16,128]{1,0:T(8,128)}, /*index=5*/s32[32,128]{1,0:T(8,128)}) custom-call(s32[4]{0:T(128)} %pad_add_fusion.me, f32[32,64,128]{2,1,0:T(8,128)} %state.5, f32[5,64,128]{2,1,0:T(8,128)} %copy-done.9, ...), custom_call_target="tpu_custom_call" | custom-call | flops 2000000000 | bytes 6000000 | tf_op jit(solution)/shard_map/conv_first/pallas_call | solution.py:485
  92.6 0.0 collective-permute-done.12.rest_9_
  92.6 0.0 collective-permute-done.15.rest_12_
  92.6 0.0 collective-permute-done.13.rest_10_
  92.7 0.0 collective-permute-done.11.rest_8_
  92.7 0.0 collective-permute-done.10.rest_7_
  92.7 0.0 copy-done
  92.7 0.0 copy-done.5
  92.7 0.0 copy-start.2
  92.7 1.0 copy-done.2
  93.7 1.0 copy-done.4
  94.8 0.7 copy-done.6
  95.5 0.7 copy-done.7
  96.2 12.2 %read_and_finish.1 = f32[32,64,128]{2,1,0:T(8,128)} custom-call(s32[16,128]{1,0:T(8,128)S(1)} %copy-done.7, s32[32,128]{1,0:T(8,128)S(1)} %copy-done.6, s32[4]{0:T(128)S(1)} %copy-done, f32[1,128]{1,0:T(1,128)S(1)} %bitcast.5, f32[40,72,128]{2,1,0:T(8,128)} %get-tuple-element.28.ext_hbm, f32[36,72,128]{2,1,0:T(8,128)} %get-tuple-element.29.pre_hbm, ...), custom_call_target="tpu_custom_call" | custom-call | flops 4000000000 | bytes 12000000 | tf_op jit(solution)/shard_map/read_and_finish/pallas_call | solution.py:519
  (8 shorter events, 0.0 us)
Async XLA Ops:
  3.0 11.1 %copy-start.14 = (f32[5,64,128]{2,1,0:T(8,128)S(1)}, f32[5,64,128]{2,1,0:T(8,128)}, u32[]{:S(2)}) copy-start(f32[5,64,128]{2,1,0:T(8,128)} %get-tuple-element.19) | copy-start | bytes 491524
  3.1 28.1 %all-to-all-start = ((f32[16,128,128]{2,1,0:T(8,128)}), f32[16,128,128]{2,1,0:T(8,128)S(1)}, u32[]{:S(2)}, u32[]{:S(2)}) async-start(f32[16,128,128]{2,1,0:T(8,128)} %get-tuple-element.32), calls=%async_computation | async-start | bytes 2097152 | tf_op jit(solution)/shard_map/all_to_all | solution.py:48
  14.1 23.1 %copy-start.13 = (f32[5,64,128]{2,1,0:T(8,128)S(1)}, f32[5,64,128]{2,1,0:T(8,128)}, u32[]{:S(2)}) copy-start(f32[5,64,128]{2,1,0:T(8,128)} %get-tuple-element.20) | copy-start | bytes 491524
  14.1 23.0 %collective-permute-start = (f32[5,64,128]{2,1,0:T(8,128)S(1)}, f32[5,64,128]{2,1,0:T(8,128)S(1)}, u32[]{:S(2)}, u32[]{:S(2)}) collective-permute-start(f32[5,64,128]{2,1,0:T(8,128)S(1)} %copy-done.14), channel_id=1, source_target_pairs={{0,8},{8,16},{16,24},{24,32},{32,40},{40,48},{48,56},{56,64},{64,7... | collective-permute-start | bytes 491528 | tf_op jit(solution)/shard_map/ppermute | solution.py:461
  31.1 1.3 %copy-start.8 = (f32[16,128,128]{2,1,0:T(8,128)}, f32[16,128,128]{2,1,0:T(8,128)S(1)}, u32[]{:S(2)}) copy-start(f32[16,128,128]{2,1,0:T(8,128)S(1)} %all-to-all-done.rest_0_) | copy-start | bytes 3145732
  32.5 33.9 %collective-permute-start.9 = (f32[8,128,128]{2,1,0:T(8,128)}, f32[8,128,128]{2,1,0:T(8,128)S(1)}, u32[]{:S(2)}, u32[]{:S(2)}) collective-permute-start(f32[8,128,128]{2,1,0:T(8,128)} %get-tuple-element.33), channel_id=1, source_target_pairs={{0,96},{1,97},{2,98},{3,99},{4,100},{5,101},{6,102},{7,103},{8,104... | collective-permute-start | bytes 1572872 | tf_op jit(solution)/shard_map/ppermute | solution.py:54
  32.6 34.0 %collective-permute-start.7 = (f32[8,128,128]{2,1,0:T(8,128)}, f32[8,128,128]{2,1,0:T(8,128)S(1)}, u32[]{:S(2)}, u32[]{:S(2)}) collective-permute-start(f32[8,128,128]{2,1,0:T(8,128)} %get-tuple-element.33), channel_id=1, source_target_pairs={{0,24},{1,25},{2,26},{3,27},{4,28},{5,29},{6,30},{7,31},{8,0},{9,1... | collective-permute-start | bytes 1572872 | tf_op jit(solution)/shard_map/ppermute | solution.py:54
  34.0 35.5 %collective-permute-start.5 = (f32[8,128,128]{2,1,0:T(8,128)}, f32[8,128,128]{2,1,0:T(8,128)S(1)}, u32[]{:S(2)}, u32[]{:S(2)}) collective-permute-start(f32[8,128,128]{2,1,0:T(8,128)} %get-tuple-element.33), channel_id=1, source_target_pairs={{0,6},{1,7},{2,0},{3,1},{4,2},{5,3},{6,4},{7,5},{8,14},{9,15},{10,... | collective-permute-start | bytes 1572872 | tf_op jit(solution)/shard_map/ppermute | solution.py:54
  37.1 32.4 %collective-permute-start.8 = (f32[8,128,128]{2,1,0:T(8,128)}, f32[8,128,128]{2,1,0:T(8,128)S(1)}, u32[]{:S(2)}, u32[]{:S(2)}) collective-permute-start(f32[8,128,128]{2,1,0:T(8,128)} %get-tuple-element.34), channel_id=1, source_target_pairs={{0,32},{1,33},{2,34},{3,35},{4,36},{5,37},{6,38},{7,39},{8,40},{9,... | collective-permute-start | bytes 1572872 | tf_op jit(solution)/shard_map/ppermute | solution.py:53
  37.2 10.5 %copy-start.9 = (f32[5,64,128]{2,1,0:T(8,128)}, f32[5,64,128]{2,1,0:T(8,128)S(1)}, u32[]{:S(2)}) copy-start(f32[5,64,128]{2,1,0:T(8,128)S(1)} %collective-permute-done.top) | copy-start | bytes 491524
  37.2 10.4 %collective-permute-start.1 = (f32[5,64,128]{2,1,0:T(8,128)S(1)}, f32[5,64,128]{2,1,0:T(8,128)S(1)}, u32[]{:S(2)}, u32[]{:S(2)}) collective-permute-start(f32[5,64,128]{2,1,0:T(8,128)S(1)} %copy-done.13), channel_id=1, source_target_pairs={{8,0},{16,8},{24,16},{32,24},{40,32},{48,40},{56,48},{64,56},{72,6... | collective-permute-start | bytes 491528 | tf_op jit(solution)/shard_map/ppermute | solution.py:462
  47.6 0.7 copy-start.10
  50.8 9.7 %collective-permute-start.2 = (f32[40,8,128]{2,1,0:T(8,128)}, f32[40,8,128]{2,1,0:T(8,128)S(1)}, u32[]{:S(2)}, u32[]{:S(2)}) collective-permute-start(f32[40,8,128]{2,1,0:T(8,128)} %get-tuple-element.21), channel_id=1, source_target_pairs={{1,0},{2,1},{3,2},{4,3},{5,4},{6,5},{7,6},{9,8},{10,9},{11,10},{12... | collective-permute-start | bytes 491528 | tf_op jit(solution)/shard_map/ppermute | solution.py:482
  60.5 24.4 %copy-start.11 = (f32[40,8,128]{2,1,0:T(8,128)}, f32[40,8,128]{2,1,0:T(8,128)S(1)}, u32[]{:S(2)}) copy-start(f32[40,8,128]{2,1,0:T(8,128)S(1)} %collective-permute-done.2.right) | copy-start | bytes 491524
  60.5 4.5 %collective-permute-start.3 = (f32[40,8,128]{2,1,0:T(8,128)}, f32[40,8,128]{2,1,0:T(8,128)S(1)}, u32[]{:S(2)}, u32[]{:S(2)}) collective-permute-start(f32[40,8,128]{2,1,0:T(8,128)} %get-tuple-element.22), channel_id=1, source_target_pairs={{0,1},{1,2},{2,3},{3,4},{4,5},{5,6},{6,7},{8,9},{9,10},{10,11},{11... | collective-permute-start | bytes 491528 | tf_op jit(solution)/shard_map/ppermute | solution.py:481
  65.0 19.9 %copy-start.12 = (f32[40,8,128]{2,1,0:T(8,128)}, f32[40,8,128]{2,1,0:T(8,128)S(1)}, u32[]{:S(2)}) copy-start(f32[40,8,128]{2,1,0:T(8,128)S(1)} %collective-permute-done.3.left) | copy-start | bytes 491524
  65.0 15.0 %collective-permute-start.6 = (f32[8,128,128]{2,1,0:T(8,128)}, f32[8,128,128]{2,1,0:T(8,128)S(1)}, u32[]{:S(2)}, u32[]{:S(2)}) collective-permute-start(f32[8,128,128]{2,1,0:T(8,128)} %get-tuple-element.34), channel_id=1, source_target_pairs={{0,8},{1,9},{2,10},{3,11},{4,12},{5,13},{6,14},{7,15},{8,16},{9,17... | collective-permute-start | bytes 1572872 | tf_op jit(solution)/shard_map/ppermute | solution.py:53
  66.4 15.1 %collective-permute-start.4 = (f32[8,128,128]{2,1,0:T(8,128)}, f32[8,128,128]{2,1,0:T(8,128)S(1)}, u32[]{:S(2)}, u32[]{:S(2)}) collective-permute-start(f32[8,128,128]{2,1,0:T(8,128)} %get-tuple-element.34), channel_id=1, source_target_pairs={{0,2},{1,3},{2,4},{3,5},{4,6},{5,7},{6,0},{7,1},{8,10},{9,11},{10,... | collective-permute-start | bytes 1572872 | tf_op jit(solution)/shard_map/ppermute | solution.py:53
  66.6 15.6 %collective-permute-start.16 = (f32[8,128,128]{2,1,0:T(8,128)S(1)}, f32[8,128,128]{2,1,0:T(8,128)S(1)}, u32[]{:S(2)}, u32[]{:S(2)}) collective-permute-start(f32[8,128,128]{2,1,0:T(8,128)S(1)} %collective-permute-done.9.rest_6_), channel_id=1, source_target_pairs={{0,1},{1,0},{2,3},{3,2},{4,5},{5,4},{6,7},{7,6},{8,9},{9,8},{10,11... | collective-permute-start | bytes 1572872 | tf_op jit(solution)/shard_map/ppermute | solution.py:55
  69.5 13.5 %collective-permute-start.14 = (f32[8,128,128]{2,1,0:T(8,128)S(1)}, f32[8,128,128]{2,1,0:T(8,128)S(1)}, u32[]{:S(2)}, u32[]{:S(2)}) collective-permute-start(f32[8,128,128]{2,1,0:T(8,128)S(1)} %collective-permute-done.7.rest_4_), channel_id=1, source_target_pairs={{0,1},{1,0},{2,3},{3,2},{4,5},{5,4},{6,7},{7,6},{8,9},{9,8},{10,11... | collective-permute-start | bytes 1572872 | tf_op jit(solution)/shard_map/ppermute | solution.py:55
  69.5 23.1 %collective-permute-start.10 = (f32[16,128,128]{2,1,0:T(8,128)}, f32[16,128,128]{2,1,0:T(8,128)}, u32[]{:S(2)}, u32[]{:S(2)}) collective-permute-start(f32[16,128,128]{2,1,0:T(8,128)} %copy-done.8), channel_id=1, source_target_pairs={{0,1},{1,0},{2,3},{3,2},{4,5},{5,4},{6,7},{7,6},{8,9},{9,8},{10,11... | collective-permute-start | bytes 3145736 | tf_op jit(solution)/shard_map/ppermute | solution.py:55
  79.9 12.7 %collective-permute-start.12 = (f32[8,128,128]{2,1,0:T(8,128)S(1)}, f32[8,128,128]{2,1,0:T(8,128)}, u32[]{:S(2)}, u32[]{:S(2)}) collective-permute-start(f32[8,128,128]{2,1,0:T(8,128)S(1)} %collective-permute-done.5.rest_2_), channel_id=1, source_target_pairs={{0,1},{1,0},{2,3},{3,2},{4,5},{5,4},{6,7},{7,6},{8,9},{9,8},{10,11... | collective-permute-start | bytes 1572872 | tf_op jit(solution)/shard_map/ppermute | solution.py:55
  81.5 11.2 %collective-permute-start.15 = (f32[8,128,128]{2,1,0:T(8,128)S(1)}, f32[8,128,128]{2,1,0:T(8,128)}, u32[]{:S(2)}, u32[]{:S(2)}) collective-permute-start(f32[8,128,128]{2,1,0:T(8,128)S(1)} %collective-permute-done.8.rest_5_), channel_id=1, source_target_pairs={{0,1},{1,0},{2,3},{3,2},{4,5},{5,4},{6,7},{7,6},{8,9},{9,8},{10,11... | collective-permute-start | bytes 1572872 | tf_op jit(solution)/shard_map/ppermute | solution.py:55
  82.2 0.8 copy-start.1
  83.0 9.7 %collective-permute-start.13 = (f32[8,128,128]{2,1,0:T(8,128)S(1)}, f32[8,128,128]{2,1,0:T(8,128)}, u32[]{:S(2)}, u32[]{:S(2)}) collective-permute-start(f32[8,128,128]{2,1,0:T(8,128)S(1)} %collective-permute-done.6.rest_3_), channel_id=1, source_target_pairs={{0,1},{1,0},{2,3},{3,2},{4,5},{5,4},{6,7},{7,6},{8,9},{9,8},{10,11... | collective-permute-start | bytes 1572872 | tf_op jit(solution)/shard_map/ppermute | solution.py:55
  83.0 0.8 copy-start.3
  83.8 8.9 %collective-permute-start.11 = (f32[8,128,128]{2,1,0:T(8,128)S(1)}, f32[8,128,128]{2,1,0:T(8,128)}, u32[]{:S(2)}, u32[]{:S(2)}) collective-permute-start(f32[8,128,128]{2,1,0:T(8,128)S(1)} %collective-permute-done.4.rest_1_), channel_id=1, source_target_pairs={{0,1},{1,0},{2,3},{3,2},{4,5},{5,4},{6,7},{7,6},{8,9},{9,8},{10,11... | collective-permute-start | bytes 1572872 | tf_op jit(solution)/shard_map/ppermute | solution.py:55
  84.9 7.8 %copy-start = (s32[4]{0:T(128)S(1)}, s32[4]{0:T(128)}, u32[]{:S(2)}) copy-start(s32[4]{0:T(128)} %pad_add_fusion.me) | copy-start | bytes 52
  84.9 7.8 %copy-start.5 = (f32[128]{0:T(128)S(1)}, f32[128]{0:T(128)}, u32[]{:S(2)}) copy-start(f32[128]{0:T(128)} %param.17) | copy-start | bytes 1540
  92.7 1.0 copy-start.2
  93.7 1.0 copy-start.4
  94.8 0.7 copy-start.6
  95.5 0.7 copy-start.7

commit v3 on v2

--- a/solution.py
+++ b/solution.py
@@ -78,17 +78,12 @@
     return pltpu.roll(sums[0], 1, 1) + sums[1] + pltpu.roll(sums[2], WIDE - 1, 1)
 
 
-def rows_kernel(
-    state, weight, syndromes, erased, readers, up, down, copies, rows_sem, copies_sem
-):
+def rows_kernel(state, syndromes, erased, readers, up, down, rows_sem):
     moves = [
         pltpu.make_async_copy(state.at[pl.ds(0, HALO)], up.at[pl.ds(0, HALO)], rows_sem.at[0]),
         pltpu.make_async_copy(
             state.at[pl.ds(TR - HALO, HALO)], down.at[pl.ds(0, HALO)], rows_sem.at[1]
         ),
-    ]
-    moves += [
-        pltpu.make_async_copy(weight, copies.at[i], copies_sem.at[i]) for i in range(16)
     ]
     for move in moves:
         move.start()
@@ -208,7 +203,6 @@
     inputs_out,
     weights_out,
     slots_out,
-    flags_out,
     codes,
     turned,
     names,
@@ -253,10 +247,10 @@
     names[16 + BROWS : 32] = jnp.zeros((16 - BROWS, C), f32)
     names[32 + BROWS : 48] = jnp.zeros((16 - BROWS, C), f32)
     names[48 + BROWS :] = jnp.zeros((16 - BROWS, C), f32)
-    flags_out[:16] = widen(lost[...], 0)
-    flags_out[16:] = jnp.zeros((16, C), jnp.int32)
-    flags_out[17 : 17 + TR // BS, :wide] = erased[1]
-    slots_out[...] = slots_of(widen(ids[...], 32) & 127, me[0], me[1])
+    slots_out[...] = slots_of(widen(ids[...], 32) & 127, me[0], me[1]) + 128 * widen(
+        lost[...], 0
+    )
+    slots_out[1 : 1 + TR // BS, :wide] += 256 * erased[1]
 
     codes[...] = jnp.zeros((C, C), f32)
     codes[:TALL, :TC] = code[...]
@@ -315,7 +309,7 @@
 
 
 def second_kernel(
-    slots, flags, me, offset, ext_hbm, pre_hbm, inputs_hbm, weights_hbm, *rest
+    slots, me, offset, ext_hbm, pre_hbm, inputs_hbm, weights_hbm, *rest
 ):
     pieces = rest[:14]
     out, table, first, field, second, ext, pre, inputs, weights, sems = rest[14:]
@@ -345,14 +339,12 @@
 
     def read_first(step, carry):
         for br, g in [(5 * step + k, g) for k in range(5) for g in range(GROUPS)]:
-            right = jnp.concatenate(
-                [table[slots[br, 2 * g]], table[slots[br, 2 * g + 1]]], axis=1
-            )
+            one, two = slots[br, 2 * g], slots[br, 2 * g + 1]
             first[br, 8 * g : 8 * g + 8] = readout(
                 ext[pl.ds(br * BS, BS), 8 * g : 8 * g + 8],
-                right,
-                flags[br, 2 * g].astype(jnp.float32),
-                flags[br, 2 * g + 1].astype(jnp.float32),
+                jnp.concatenate([table[one & 127], table[two & 127]], axis=1),
+                ((one >> 7) & 1).astype(jnp.float32),
+                ((two >> 7) & 1).astype(jnp.float32),
                 shift,
                 sub,
             )
@@ -384,13 +376,12 @@
 
     def read_second(step, carry):
         for br, g in [(4 * step + k, g) for k in range(4) for g in range(TC // 8)]:
+            one, two = slots[br + 1, 2 * g], slots[br + 1, 2 * g + 1]
             second[br, 8 * g : 8 * g + 8] = readout(
                 field[pl.ds(br * BS + 1, BS), 8 * g : 8 * g + 8],
-                jnp.concatenate(
-                    [table[slots[br + 1, 2 * g]], table[slots[br + 1, 2 * g + 1]]], axis=1
-                ),
-                flags[17 + br, 2 * g].astype(jnp.float32),
-                flags[17 + br, 2 * g + 1].astype(jnp.float32),
+                jnp.concatenate([table[one & 127], table[two & 127]], axis=1),
+                (one >> 8).astype(jnp.float32),
+                (two >> 8).astype(jnp.float32),
                 shift,
                 sub,
             )
@@ -443,18 +434,18 @@
     def shape(*dims, dtype=f32):
         return jax.ShapeDtypeStruct(dims, dtype)
 
-    up_pay, down_pay, copies = pl.pallas_call(
+    copies = jnp.broadcast_to(read_weight[None], (16, C, C))
+    up_pay, down_pay = pl.pallas_call(
         rows_kernel,
         name="pack_rows",
         out_shape=(
             shape(HALO + 1, TC, C),
             shape(HALO + 1, TC, C),
-            shape(16, C, C),
         ),
-        in_specs=[anywhere, vmem, vmem, vmem, vmem],
-        out_specs=(vmem, vmem, anywhere),
-        scratch_shapes=[pltpu.SemaphoreType.DMA((2,)), pltpu.SemaphoreType.DMA((16,))],
-    )(state, read_weight, syndromes, erased, names)
+        in_specs=[anywhere, vmem, vmem, vmem],
+        out_specs=(vmem, vmem),
+        scratch_shapes=[pltpu.SemaphoreType.DMA((2,))],
+    )(state, syndromes, erased, names)
 
     up = [(i, i - 1) for i in range(1, gx_count)]
     down = [(i, i + 1) for i in range(gx_count - 1)]
@@ -482,19 +473,19 @@
     right = lax.ppermute(west_pay, "gy", west)
     pieces = gather_weights(copies)
 
-    ext, pre, inputs, weights, slots, flags = pl.pallas_call(
+    ext, pre, inputs, weights, slots = pl.pallas_call(
         first_kernel,
         name="conv_first",
+        compiler_params=pltpu.CompilerParams(vmem_limit_bytes=16 * 2**20),
         out_shape=(
             shape(TALL, WIDE, C),
             shape(CONV_ROWS, WIDE, C),
             shape(TR, TC, C),
             shape(6 * C, 6 * C, dtype=jnp.bfloat16),
             shape(16, C, dtype=jnp.int32),
-            shape(32, C, dtype=jnp.int32),
         ),
         in_specs=[smem] + [vmem] * 13,
-        out_specs=(vmem,) * 6,
+        out_specs=(vmem,) * 5,
         scratch_shapes=[pltpu.VMEM((C, C), f32), pltpu.VMEM((C, C), f32), pltpu.VMEM((64, C), f32)],
         cost_estimate=pl.CostEstimate(
             flops=2_000_000_000, bytes_accessed=6_000_000, transcendentals=0
@@ -519,9 +510,9 @@
     return pl.pallas_call(
         second_kernel,
         name="read_and_finish",
-        compiler_params=pltpu.CompilerParams(vmem_limit_bytes=47 * 2**20),
+        compiler_params=pltpu.CompilerParams(vmem_limit_bytes=44 * 2**20),
         out_shape=shape(TR, TC, C),
-        in_specs=[smem] * 3 + [vmem] + [hbm] * 4 + [vmem] * 14,
+        in_specs=[smem] * 2 + [vmem] + [hbm] * 4 + [vmem] * 14,
         out_specs=vmem,
         scratch_shapes=[
             pltpu.VMEM((128, 2 * C, C), jnp.bfloat16),
@@ -537,7 +528,7 @@
         cost_estimate=pl.CostEstimate(
             flops=4_000_000_000, bytes_accessed=12_000_000, transcendentals=1_000_000
         ),
-    )(slots, flags, me, offset, ext, pre, inputs, weights, *pieces)
+    )(slots, me, offset, ext, pre, inputs, weights, *pieces)
 
 
 def solution(mesh):

time: 109 us -> 110 us (level)
  local copies, waits for them, and re-layouts: 7.09 us -> 14.2 us
  Pallas kernels: 25.4 us -> 22.6 us
  waiting for transfers between devices: 42.6 us -> 40 us
    unnamed x30 -> x48, local copies, waits for them, and re-layouts: 5.94 us -> 11.2 us
    all_to_all x1, waiting for transfers between devices: 14.6 us -> 12 us  [gather_weights(): lax.all_to_all(copies, AX, 0, 0, tiled=True, axis_index_groups=class_grou...]
    pallas_call x1, Pallas kernels: 7.74 us -> 5.26 us  [decode(): pl.pallas_call(first_kernel, name='conv_first', compiler_params=pltpu.Com...]
    broadcast_in_dim x0 -> x1, local copies, waits for them, and re-layouts: none -> 1.91 us  [decode(): copies = jnp.broadcast_to(read_weight[None], (16, C, C))]
  transfers between devices with their start and end apart: 18 -> 18, of which waited for: 6 -> 6; matrix products, arithmetic and copies ran while one was open for 2% -> 1% of each run, Pallas kernels for 9% -> 9%
where the time goes in v3:
time: 110 us; the launch traced here: 109 us
  waiting for transfers between devices  40 us (36%)
  starting transfers between devices  31.8 us (29%)
  Pallas kernels  22.6 us (21%)
  local copies, waits for them, and re-layouts  14.2 us (13%)
    pallas_call x1, Pallas kernels, decode(): pl.pallas_call(second_kernel, name='read_and_finish', compiler_params=plt...  12.4 us
    all_to_all x1, waiting for transfers between devices, gather_weights(): lax.all_to_all(copies, AX, 0, 0, tiled=True, axis_index_groups=class_grou...  12 us
    ppermute x3, waiting for transfers between devices, gather_weights(): pieces.append(lax.ppermute(low, AX, moved(*step)))  11.3 us
    unnamed x48, local copies, waits for them, and re-layouts  11.2 us
    all_to_all x1, starting transfers between devices, gather_weights(): lax.all_to_all(copies, AX, 0, 0, tiled=True, axis_index_groups=class_grou...  10.9 us
    ppermute x1, waiting for transfers between devices, decode(): bottom = lax.ppermute(up_pay, 'gx', up)  9.29 us
    pallas_call x1, Pallas kernels, decode(): pl.pallas_call(first_kernel, name='conv_first', compiler_params=pltpu.Com...  5.26 us
    ppermute x1, waiting for transfers between devices, decode(): right = lax.ppermute(west_pay, 'gy', west)  4.82 us
  transfers between devices with their start and end apart: 18, of which 6 were waited for; matrix products, arithmetic and copies ran while one was open for 1% of the time, Pallas kernels for 9%

profile of v3, /device:TPU:1, one launch (start us, length us, event | category | flops | bytes accessed | tf_op | source)
XLA Modules:
  0.0 108.9 jit_solution(16662610368968750876)
XLA Ops:
  0.0 1.9 %broadcast_in_dim.14 = f32[16,128,128]{2,1,0:T(8,128)} broadcast(f32[128,128]{1,0:T(8,128)} %param.16), dimensions={1,2} | broadcast | bytes 1114112 | tf_op jit(solution)/shard_map/broadcast_in_dim | solution.py:437
  1.9 10.9 %all-to-all-start = ((f32[16,128,128]{2,1,0:T(8,128)}), f32[16,128,128]{2,1,0:T(8,128)S(1)}, u32[]{:S(2)}, u32[]{:S(2)}) async-start(f32[16,128,128]{2,1,0:T(8,128)} %broadcast_in_dim.14), calls=%async_computation | async-start | bytes 2097152 | tf_op jit(solution)/shard_map/all_to_all | solution.py:48
  12.8 2.5 %pack_rows.1 = (f32[5,64,128]{2,1,0:T(8,128)}, f32[5,64,128]{2,1,0:T(8,128)}) custom-call(f32[32,64,128]{2,1,0:T(8,128)} %state.5, s32[2,32,64]{2,1,0:T(8,128)} %syndromes.5, s32[2,8,16]{2,1,0:T(8,128)} %erased.5, s32[1,128]{1,0:T(1,128)} %bitcast.8), custom_call_target="tpu_custom_call" | custom-call | tf_op jit(solution)/shard_map/pack_rows/pallas_call | solution.py:438
  15.3 0.0 copy-start.23
  15.3 0.0 copy-start
  15.3 0.0 copy-start.5
  15.3 0.0 copy-start.6
  15.4 0.0 copy-start.7
  15.4 0.0 copy-start.8
  15.4 2.4 %collective-permute-start = (f32[5,64,128]{2,1,0:T(8,128)}, f32[5,64,128]{2,1,0:T(8,128)S(1)}, u32[]{:S(2)}, u32[]{:S(2)}) collective-permute-start(f32[5,64,128]{2,1,0:T(8,128)} %get-tuple-element.17), channel_id=1, source_target_pairs={{0,8},{8,16},{16,24},{24,32},{32,40},{40,48},{48,56},{56,64},{64,7... | collective-permute-start | bytes 491528 | tf_op jit(solution)/shard_map/ppermute | solution.py:452
  17.8 12.0 %all-to-all-done.rest_0_ = f32[16,128,128]{2,1,0:T(8,128)S(1)} async-done(((f32[16,128,128]{2,1,0:T(8,128)}), f32[16,128,128]{2,1,0:T(8,128)S(1)}, u32[]{:S(2)}, u32[]{:S(2)}) %all-to-all-start) | async-done | bytes 1048608 | tf_op jit(solution)/shard_map/all_to_all | solution.py:48
  29.8 1.1 fusion
  30.9 0.2 collective-permute-start.9
  31.0 1.4 %collective-permute-start.7 = (f32[8,128,128]{2,1,0:T(8,128)}, f32[8,128,128]{2,1,0:T(8,128)}, u32[]{:S(2)}, u32[]{:S(2)}) collective-permute-start(f32[8,128,128]{2,1,0:T(8,128)} %get-tuple-element.29), channel_id=1, source_target_pairs={{0,24},{1,25},{2,26},{3,27},{4,28},{5,29},{6,30},{7,31},{8,0},{9,1... | collective-permute-start | bytes 1572872 | tf_op jit(solution)/shard_map/ppermute | solution.py:54
  32.4 3.2 %collective-permute-start.5 = (f32[8,128,128]{2,1,0:T(8,128)}, f32[8,128,128]{2,1,0:T(8,128)S(1)}, u32[]{:S(2)}, u32[]{:S(2)}) collective-permute-start(f32[8,128,128]{2,1,0:T(8,128)} %get-tuple-element.29), channel_id=1, source_target_pairs={{0,6},{1,7},{2,0},{3,1},{4,2},{5,3},{6,4},{7,5},{8,14},{9,15},{10,... | collective-permute-start | bytes 1572872 | tf_op jit(solution)/shard_map/ppermute | solution.py:54
  35.6 0.0 collective-permute-start.8
  35.6 0.0 collective-permute-done.top
  35.6 1.3 %collective-permute-start.1 = (f32[5,64,128]{2,1,0:T(8,128)S(1)}, f32[5,64,128]{2,1,0:T(8,128)S(1)}, u32[]{:S(2)}, u32[]{:S(2)}) collective-permute-start(f32[5,64,128]{2,1,0:T(8,128)S(1)} %copy-done.23), channel_id=1, source_target_pairs={{8,0},{16,8},{24,16},{32,24},{40,32},{48,40},{56,48},{64,56},{72,6... | collective-permute-start | bytes 491528 | tf_op jit(solution)/shard_map/ppermute | solution.py:453
  36.9 9.3 %collective-permute-done.1.bottom = f32[5,64,128]{2,1,0:T(8,128)S(1)} collective-permute-done((f32[5,64,128]{2,1,0:T(8,128)S(1)}, f32[5,64,128]{2,1,0:T(8,128)S(1)}, u32[]{:S(2)}, u32[]{:S(2)}) %collective-permute-start.1) | collective-permute-done | bytes 163872 | tf_op jit(solution)/shard_map/ppermute | solution.py:453
  46.2 0.7 copy-done.3
  46.8 2.4 %pack_cols.1 = (f32[40,8,128]{2,1,0:T(8,128)}, f32[40,8,128]{2,1,0:T(8,128)}, f32[40,64]{1,0:T(8,128)}, f32[16,128]{1,0:T(8,128)}, f32[16,128]{1,0:T(8,128)}) custom-call(f32[32,64,128]{2,1,0:T(8,128)} %state.5, f32[5,64,128]{2,1,0:T(8,128)} %copy-done.1, f32[5,64,128]{2,1,0:T(8,128)} %copy-done.3, s32[2,32,64]{2,1,0:T(8,128)} %syndromes.5, ...), custom_call_target="tpu_custom_call" | custom-call | tf_op jit(solution)/shard_map/pack_cols/pallas_call | solution.py:455
  49.3 4.8 %collective-permute-start.2 = (f32[40,8,128]{2,1,0:T(8,128)}, f32[40,8,128]{2,1,0:T(8,128)S(1)}, u32[]{:S(2)}, u32[]{:S(2)}) collective-permute-start(f32[40,8,128]{2,1,0:T(8,128)} %get-tuple-element.19), channel_id=1, source_target_pairs={{1,0},{2,1},{3,2},{4,3},{5,4},{6,5},{7,6},{9,8},{10,9},{11,10},{12... | collective-permute-start | bytes 491528 | tf_op jit(solution)/shard_map/ppermute | solution.py:473
  54.1 4.8 %collective-permute-done.2.right = f32[40,8,128]{2,1,0:T(8,128)S(1)} collective-permute-done((f32[40,8,128]{2,1,0:T(8,128)}, f32[40,8,128]{2,1,0:T(8,128)S(1)}, u32[]{:S(2)}, u32[]{:S(2)}) %collective-permute-start.2) | collective-permute-done | bytes 163872 | tf_op jit(solution)/shard_map/ppermute | solution.py:473
  58.9 1.9 %collective-permute-start.3 = (f32[40,8,128]{2,1,0:T(8,128)}, f32[40,8,128]{2,1,0:T(8,128)S(1)}, u32[]{:S(2)}, u32[]{:S(2)}) collective-permute-start(f32[40,8,128]{2,1,0:T(8,128)} %get-tuple-element.20), channel_id=1, source_target_pairs={{0,1},{1,2},{2,3},{3,4},{4,5},{5,6},{6,7},{8,9},{9,10},{10,11},{11... | collective-permute-start | bytes 491528 | tf_op jit(solution)/shard_map/ppermute | solution.py:472
  60.8 2.6 %collective-permute-done.3.left = f32[40,8,128]{2,1,0:T(8,128)S(1)} collective-permute-done((f32[40,8,128]{2,1,0:T(8,128)}, f32[40,8,128]{2,1,0:T(8,128)S(1)}, u32[]{:S(2)}, u32[]{:S(2)}) %collective-permute-start.3) | collective-permute-done | bytes 163872 | tf_op jit(solution)/shard_map/ppermute | solution.py:472
  63.4 1.4 %collective-permute-start.6 = (f32[8,128,128]{2,1,0:T(8,128)}, f32[8,128,128]{2,1,0:T(8,128)}, u32[]{:S(2)}, u32[]{:S(2)}) collective-permute-start(f32[8,128,128]{2,1,0:T(8,128)} %get-tuple-element.30), channel_id=1, source_target_pairs={{0,8},{1,9},{2,10},{3,11},{4,12},{5,13},{6,14},{7,15},{8,16},{9,17... | collective-permute-start | bytes 1572872 | tf_op jit(solution)/shard_map/ppermute | solution.py:53
  64.8 0.0 collective-permute-done.9.rest_6_
  64.8 0.1 collective-permute-start.4
  64.9 0.0 collective-permute-done.7.rest_4_
  64.9 3.0 %collective-permute-start.16 = (f32[8,128,128]{2,1,0:T(8,128)}, f32[8,128,128]{2,1,0:T(8,128)S(1)}, u32[]{:S(2)}, u32[]{:S(2)}) collective-permute-start(f32[8,128,128]{2,1,0:T(8,128)} %collective-permute-done.9.rest_6_), channel_id=1, source_target_pairs={{0,1},{1,0},{2,3},{3,2},{4,5},{5,4},{6,7},{7,6},{8,9},{9,8},{10,11... | collective-permute-start | bytes 1572872 | tf_op jit(solution)/shard_map/ppermute | solution.py:55
  67.9 0.0 collective-permute-done.5.rest_2_
  67.9 0.1 collective-permute-start.14
  68.0 0.7 copy-done.10
  68.7 0.0 collective-permute-done.8.rest_5_
  68.7 0.0 collective-permute-start.10
  68.7 9.8 %collective-permute-done.6.rest_3_ = f32[8,128,128]{2,1,0:T(8,128)} collective-permute-done((f32[8,128,128]{2,1,0:T(8,128)}, f32[8,128,128]{2,1,0:T(8,128)}, u32[]{:S(2)}, u32[]{:S(2)}) %collective-permute-start.6) | collective-permute-done | bytes 524320 | tf_op jit(solution)/shard_map/ppermute | solution.py:53
  78.5 0.0 collective-permute-start.12
  78.5 1.5 %collective-permute-done.4.rest_1_ = f32[8,128,128]{2,1,0:T(8,128)} collective-permute-done((f32[8,128,128]{2,1,0:T(8,128)}, f32[8,128,128]{2,1,0:T(8,128)}, u32[]{:S(2)}, u32[]{:S(2)}) %collective-permute-start.4) | collective-permute-done | bytes 524320 | tf_op jit(solution)/shard_map/ppermute | solution.py:53
  80.0 0.7 collective-permute-start.15
  80.7 0.0 collective-permute-done.16.rest_13_
  80.7 0.8 copy-done.12
  81.5 0.0 collective-permute-start.13
  81.5 0.0 collective-permute-done.14.rest_11_
  81.5 0.8 copy-done.14
  82.3 0.5 collective-permute-start.11
  82.8 0.1 pad_add_fusion.me
  82.9 0.0 copy-done.6
  82.9 0.9 copy-done.2
  83.8 0.9 copy-done.4
  84.7 1.1 copy-done.9
  85.8 0.7 copy-done.16
  86.5 0.7 copy-done.17
  87.2 0.7 copy-done.18
  87.9 5.3 %conv_first.1 = (f32[40,72,128]{2,1,0:T(8,128)S(1)}, f32[36,72,128]{2,1,0:T(8,128)S(1)}, f32[32,64,128]{2,1,0:T(8,128)S(1)}, bf16[768,768]{1,0:T(8,128)(2,1)S(1)}, s32[16,128]{1,0:T(8,128)S(1)}) custom-call(s32[4]{0:T(128)S(1)} %pad_add_fusion.me, f32[32,64,128]{2,1,0:T(8,128)S(1)} %copy-done, f32[5,64,128]{2,1,0:T(8,128)S(1)} %copy-done.2, ...), custom_call_target="tpu_custom_call" | custom-call | flops 2000000000 | bytes 6000000 | tf_op jit(solution)/shard_map/conv_first/pallas_call | solution.py:476
  93.2 1.1 %copy-done.20 = f32[40,72,128]{2,1,0:T(8,128)} copy-done((f32[40,72,128]{2,1,0:T(8,128)}, f32[40,72,128]{2,1,0:T(8,128)S(1)}, u32[]{:S(2)}) %copy-start.20) | copy-done | bytes 1474584
  94.4 1.1 copy-done.21
  95.4 1.0 copy-done.22
  96.4 0.0 collective-permute-done.12.rest_9_
  96.4 0.0 collective-permute-done.15.rest_12_
  96.4 0.0 collective-permute-done.13.rest_10_
  96.4 0.0 collective-permute-done.11.rest_8_
  96.5 0.0 collective-permute-done.10.rest_7_
  96.5 0.0 copy-done.11
  96.5 12.4 %read_and_finish.1 = f32[32,64,128]{2,1,0:T(8,128)} custom-call(s32[16,128]{1,0:T(8,128)S(1)} %get-tuple-element.24.slots, s32[4]{0:T(128)S(1)} %pad_add_fusion.me, f32[1,128]{1,0:T(1,128)S(1)} %bitcast.7, f32[40,72,128]{2,1,0:T(8,128)} %copy-done.20, f32[36,72,128]{2,1,0:T(8,128)} %copy-done.21, f32[32,64,128]{2,1,0:T(8,128)S(1)} %get-tuple-element.27.inputs_hbm, ...), custom_call_target="tpu_custom_call" | custom-call | flops 4000000000 | bytes 12000000 | tf_op jit(solution)/shard_map/read_and_finish/pallas_call | solution.py:510
  (27 shorter events, 0.0 us)
Async XLA Ops:
  1.9 27.9 %all-to-all-start = ((f32[16,128,128]{2,1,0:T(8,128)}), f32[16,128,128]{2,1,0:T(8,128)S(1)}, u32[]{:S(2)}, u32[]{:S(2)}) async-start(f32[16,128,128]{2,1,0:T(8,128)} %broadcast_in_dim.14), calls=%async_computation | async-start | bytes 2097152 | tf_op jit(solution)/shard_map/all_to_all | solution.py:48
  15.3 20.3 %copy-start.23 = (f32[5,64,128]{2,1,0:T(8,128)S(1)}, f32[5,64,128]{2,1,0:T(8,128)}, u32[]{:S(2)}) copy-start(f32[5,64,128]{2,1,0:T(8,128)} %get-tuple-element.18) | copy-start | bytes 491524
  15.3 67.5 %copy-start = (f32[32,64,128]{2,1,0:T(8,128)S(1)}, f32[32,64,128]{2,1,0:T(8,128)}, u32[]{:S(2)}) copy-start(f32[32,64,128]{2,1,0:T(8,128)} %state.5) | copy-start | bytes 3145732
  15.3 67.5 %copy-start.5 = (s32[2,32,64]{2,1,0:T(8,128)S(1)}, s32[2,32,64]{2,1,0:T(8,128)}, u32[]{:S(2)}) copy-start(s32[2,32,64]{2,1,0:T(8,128)} %syndromes.5) | copy-start | bytes 49156
  15.3 67.5 %copy-start.6 = (s32[2,8,16]{2,1,0:T(8,128)S(1)}, s32[2,8,16]{2,1,0:T(8,128)}, u32[]{:S(2)}) copy-start(s32[2,8,16]{2,1,0:T(8,128)} %erased.5) | copy-start | bytes 3076
  15.4 67.5 %copy-start.7 = (f32[2,128]{1,0:T(2,128)S(1)}, f32[2,128]{1,0:T(2,128)}, u32[]{:S(2)}) copy-start(f32[2,128]{1,0:T(2,128)} %table.3) | copy-start | bytes 3076
  15.4 67.5 %copy-start.8 = (f32[128]{0:T(128)S(1)}, f32[128]{0:T(128)}, u32[]{:S(2)}) copy-start(f32[128]{0:T(128)} %param.15) | copy-start | bytes 1540
  15.4 20.2 %collective-permute-start = (f32[5,64,128]{2,1,0:T(8,128)}, f32[5,64,128]{2,1,0:T(8,128)S(1)}, u32[]{:S(2)}, u32[]{:S(2)}) collective-permute-start(f32[5,64,128]{2,1,0:T(8,128)} %get-tuple-element.17), channel_id=1, source_target_pairs={{0,8},{8,16},{16,24},{24,32},{32,40},{40,48},{48,56},{56,64},{64,7... | collective-permute-start | bytes 491528 | tf_op jit(solution)/shard_map/ppermute | solution.py:452
  30.9 34.0 %collective-permute-start.9 = (f32[8,128,128]{2,1,0:T(8,128)}, f32[8,128,128]{2,1,0:T(8,128)}, u32[]{:S(2)}, u32[]{:S(2)}) collective-permute-start(f32[8,128,128]{2,1,0:T(8,128)} %get-tuple-element.29), channel_id=1, source_target_pairs={{0,96},{1,97},{2,98},{3,99},{4,100},{5,101},{6,102},{7,103},{8,104... | collective-permute-start | bytes 1572872 | tf_op jit(solution)/shard_map/ppermute | solution.py:54
  31.0 33.9 %collective-permute-start.7 = (f32[8,128,128]{2,1,0:T(8,128)}, f32[8,128,128]{2,1,0:T(8,128)}, u32[]{:S(2)}, u32[]{:S(2)}) collective-permute-start(f32[8,128,128]{2,1,0:T(8,128)} %get-tuple-element.29), channel_id=1, source_target_pairs={{0,24},{1,25},{2,26},{3,27},{4,28},{5,29},{6,30},{7,31},{8,0},{9,1... | collective-permute-start | bytes 1572872 | tf_op jit(solution)/shard_map/ppermute | solution.py:54
  32.4 35.5 %collective-permute-start.5 = (f32[8,128,128]{2,1,0:T(8,128)}, f32[8,128,128]{2,1,0:T(8,128)S(1)}, u32[]{:S(2)}, u32[]{:S(2)}) collective-permute-start(f32[8,128,128]{2,1,0:T(8,128)} %get-tuple-element.29), channel_id=1, source_target_pairs={{0,6},{1,7},{2,0},{3,1},{4,2},{5,3},{6,4},{7,5},{8,14},{9,15},{10,... | collective-permute-start | bytes 1572872 | tf_op jit(solution)/shard_map/ppermute | solution.py:54
  35.6 33.1 %collective-permute-start.8 = (f32[8,128,128]{2,1,0:T(8,128)}, f32[8,128,128]{2,1,0:T(8,128)}, u32[]{:S(2)}, u32[]{:S(2)}) collective-permute-start(f32[8,128,128]{2,1,0:T(8,128)} %get-tuple-element.30), channel_id=1, source_target_pairs={{0,32},{1,33},{2,34},{3,35},{4,36},{5,37},{6,38},{7,39},{8,40},{9,... | collective-permute-start | bytes 1572872 | tf_op jit(solution)/shard_map/ppermute | solution.py:53
  35.6 10.6 %copy-start.1 = (f32[5,64,128]{2,1,0:T(8,128)}, f32[5,64,128]{2,1,0:T(8,128)S(1)}, u32[]{:S(2)}) copy-start(f32[5,64,128]{2,1,0:T(8,128)S(1)} %collective-permute-done.top) | copy-start | bytes 491524
  35.6 10.6 %collective-permute-start.1 = (f32[5,64,128]{2,1,0:T(8,128)S(1)}, f32[5,64,128]{2,1,0:T(8,128)S(1)}, u32[]{:S(2)}, u32[]{:S(2)}) collective-permute-start(f32[5,64,128]{2,1,0:T(8,128)S(1)} %copy-done.23), channel_id=1, source_target_pairs={{8,0},{16,8},{24,16},{32,24},{40,32},{48,40},{56,48},{64,56},{72,6... | collective-permute-start | bytes 491528 | tf_op jit(solution)/shard_map/ppermute | solution.py:453
  46.2 0.7 copy-start.3
  49.3 9.6 %collective-permute-start.2 = (f32[40,8,128]{2,1,0:T(8,128)}, f32[40,8,128]{2,1,0:T(8,128)S(1)}, u32[]{:S(2)}, u32[]{:S(2)}) collective-permute-start(f32[40,8,128]{2,1,0:T(8,128)} %get-tuple-element.19), channel_id=1, source_target_pairs={{1,0},{2,1},{3,2},{4,3},{5,4},{6,5},{7,6},{9,8},{10,9},{11,10},{12... | collective-permute-start | bytes 491528 | tf_op jit(solution)/shard_map/ppermute | solution.py:473
  58.9 4.5 %collective-permute-start.3 = (f32[40,8,128]{2,1,0:T(8,128)}, f32[40,8,128]{2,1,0:T(8,128)S(1)}, u32[]{:S(2)}, u32[]{:S(2)}) collective-permute-start(f32[40,8,128]{2,1,0:T(8,128)} %get-tuple-element.20), channel_id=1, source_target_pairs={{0,1},{1,2},{2,3},{3,4},{4,5},{5,6},{6,7},{8,9},{9,10},{10,11},{11... | collective-permute-start | bytes 491528 | tf_op jit(solution)/shard_map/ppermute | solution.py:472
  63.4 15.1 %collective-permute-start.6 = (f32[8,128,128]{2,1,0:T(8,128)}, f32[8,128,128]{2,1,0:T(8,128)}, u32[]{:S(2)}, u32[]{:S(2)}) collective-permute-start(f32[8,128,128]{2,1,0:T(8,128)} %get-tuple-element.30), channel_id=1, source_target_pairs={{0,8},{1,9},{2,10},{3,11},{4,12},{5,13},{6,14},{7,15},{8,16},{9,17... | collective-permute-start | bytes 1572872 | tf_op jit(solution)/shard_map/ppermute | solution.py:53
  64.8 15.2 %collective-permute-start.4 = (f32[8,128,128]{2,1,0:T(8,128)}, f32[8,128,128]{2,1,0:T(8,128)}, u32[]{:S(2)}, u32[]{:S(2)}) collective-permute-start(f32[8,128,128]{2,1,0:T(8,128)} %get-tuple-element.30), channel_id=1, source_target_pairs={{0,2},{1,3},{2,4},{3,5},{4,6},{5,7},{6,0},{7,1},{8,10},{9,11},{10,... | collective-permute-start | bytes 1572872 | tf_op jit(solution)/shard_map/ppermute | solution.py:53
  64.9 15.8 %collective-permute-start.16 = (f32[8,128,128]{2,1,0:T(8,128)}, f32[8,128,128]{2,1,0:T(8,128)S(1)}, u32[]{:S(2)}, u32[]{:S(2)}) collective-permute-start(f32[8,128,128]{2,1,0:T(8,128)} %collective-permute-done.9.rest_6_), channel_id=1, source_target_pairs={{0,1},{1,0},{2,3},{3,2},{4,5},{5,4},{6,7},{7,6},{8,9},{9,8},{10,11... | collective-permute-start | bytes 1572872 | tf_op jit(solution)/shard_map/ppermute | solution.py:55
  67.9 0.8 copy-start.10
  67.9 13.6 %collective-permute-start.14 = (f32[8,128,128]{2,1,0:T(8,128)}, f32[8,128,128]{2,1,0:T(8,128)S(1)}, u32[]{:S(2)}, u32[]{:S(2)}) collective-permute-start(f32[8,128,128]{2,1,0:T(8,128)} %collective-permute-done.7.rest_4_), channel_id=1, source_target_pairs={{0,1},{1,0},{2,3},{3,2},{4,5},{5,4},{6,7},{7,6},{8,9},{9,8},{10,11... | collective-permute-start | bytes 1572872 | tf_op jit(solution)/shard_map/ppermute | solution.py:55
  68.7 27.8 %collective-permute-start.10 = (f32[16,128,128]{2,1,0:T(8,128)S(1)}, f32[16,128,128]{2,1,0:T(8,128)S(1)}, u32[]{:S(2)}, u32[]{:S(2)}) collective-permute-start(f32[16,128,128]{2,1,0:T(8,128)S(1)} %all-to-all-done.rest_0_), channel_id=1, source_target_pairs={{0,1},{1,0},{2,3},{3,2},{4,5},{5,4},{6,7},{7,6},{8,9},{9,8},{10,11... | collective-permute-start | bytes 3145736 | tf_op jit(solution)/shard_map/ppermute | solution.py:55
  78.5 18.0 %collective-permute-start.12 = (f32[8,128,128]{2,1,0:T(8,128)}, f32[8,128,128]{2,1,0:T(8,128)}, u32[]{:S(2)}, u32[]{:S(2)}) collective-permute-start(f32[8,128,128]{2,1,0:T(8,128)} %copy-done.10), channel_id=1, source_target_pairs={{0,1},{1,0},{2,3},{3,2},{4,5},{5,4},{6,7},{7,6},{8,9},{9,8},{10,11... | collective-permute-start | bytes 1572872 | tf_op jit(solution)/shard_map/ppermute | solution.py:55
  80.0 16.4 %collective-permute-start.15 = (f32[8,128,128]{2,1,0:T(8,128)}, f32[8,128,128]{2,1,0:T(8,128)}, u32[]{:S(2)}, u32[]{:S(2)}) collective-permute-start(f32[8,128,128]{2,1,0:T(8,128)} %collective-permute-done.8.rest_5_), channel_id=1, source_target_pairs={{0,1},{1,0},{2,3},{3,2},{4,5},{5,4},{6,7},{7,6},{8,9},{9,8},{10,11... | collective-permute-start | bytes 1572872 | tf_op jit(solution)/shard_map/ppermute | solution.py:55
  80.7 0.8 copy-start.12
  81.5 14.9 %collective-permute-start.13 = (f32[8,128,128]{2,1,0:T(8,128)}, f32[8,128,128]{2,1,0:T(8,128)}, u32[]{:S(2)}, u32[]{:S(2)}) collective-permute-start(f32[8,128,128]{2,1,0:T(8,128)} %collective-permute-done.6.rest_3_), channel_id=1, source_target_pairs={{0,1},{1,0},{2,3},{3,2},{4,5},{5,4},{6,7},{7,6},{8,9},{9,8},{10,11... | collective-permute-start | bytes 1572872 | tf_op jit(solution)/shard_map/ppermute | solution.py:55
  81.5 0.8 copy-start.14
  82.3 14.2 %collective-permute-start.11 = (f32[8,128,128]{2,1,0:T(8,128)}, f32[8,128,128]{2,1,0:T(8,128)}, u32[]{:S(2)}, u32[]{:S(2)}) collective-permute-start(f32[8,128,128]{2,1,0:T(8,128)} %collective-permute-done.4.rest_1_), channel_id=1, source_target_pairs={{0,1},{1,0},{2,3},{3,2},{4,5},{5,4},{6,7},{7,6},{8,9},{9,8},{10,11... | collective-permute-start | bytes 1572872 | tf_op jit(solution)/shard_map/ppermute | solution.py:55
  82.9 0.9 copy-start.2
  83.8 0.9 copy-start.4
  84.7 1.1 copy-start.9
  85.8 0.7 copy-start.16
  86.5 0.7 copy-start.17
  87.2 0.7 copy-start.18
  87.9 8.6 %copy-start.11 = (f32[8,128,128]{2,1,0:T(8,128)S(1)}, f32[8,128,128]{2,1,0:T(8,128)}, u32[]{:S(2)}) copy-start(f32[8,128,128]{2,1,0:T(8,128)} %copy-done.10) | copy-start | bytes 1572868
  87.9 8.6 %copy-start.13 = (f32[8,128,128]{2,1,0:T(8,128)S(1)}, f32[8,128,128]{2,1,0:T(8,128)}, u32[]{:S(2)}) copy-start(f32[8,128,128]{2,1,0:T(8,128)} %copy-done.12) | copy-start | bytes 1572868
  87.9 8.6 %copy-start.15 = (f32[8,128,128]{2,1,0:T(8,128)S(1)}, f32[8,128,128]{2,1,0:T(8,128)}, u32[]{:S(2)}) copy-start(f32[8,128,128]{2,1,0:T(8,128)} %copy-done.14) | copy-start | bytes 1572868
  87.9 8.6 %copy-start.19 = (f32[128]{0:T(128)S(1)}, f32[128]{0:T(128)}, u32[]{:S(2)}) copy-start(f32[128]{0:T(128)} %param.17) | copy-start | bytes 1540
  93.2 1.2 %copy-start.20 = (f32[40,72,128]{2,1,0:T(8,128)}, f32[40,72,128]{2,1,0:T(8,128)S(1)}, u32[]{:S(2)}) copy-start(f32[40,72,128]{2,1,0:T(8,128)S(1)} %get-tuple-element.25.ext_hbm) | copy-start | bytes 4423684
  94.4 1.1 copy-start.21
  95.4 1.0 copy-start.22

commit v4 on v3

--- a/solution.py
+++ b/solution.py
@@ -78,12 +78,17 @@
     return pltpu.roll(sums[0], 1, 1) + sums[1] + pltpu.roll(sums[2], WIDE - 1, 1)
 
 
-def rows_kernel(state, syndromes, erased, readers, up, down, rows_sem):
+def rows_kernel(
+    state, weight, syndromes, erased, readers, up, down, copies, rows_sem, copies_sem
+):
     moves = [
         pltpu.make_async_copy(state.at[pl.ds(0, HALO)], up.at[pl.ds(0, HALO)], rows_sem.at[0]),
         pltpu.make_async_copy(
             state.at[pl.ds(TR - HALO, HALO)], down.at[pl.ds(0, HALO)], rows_sem.at[1]
         ),
+    ]
+    moves += [
+        pltpu.make_async_copy(weight, copies.at[i], copies_sem.at[i]) for i in range(16)
     ]
     for move in moves:
         move.start()
@@ -434,18 +439,18 @@
     def shape(*dims, dtype=f32):
         return jax.ShapeDtypeStruct(dims, dtype)
 
-    copies = jnp.broadcast_to(read_weight[None], (16, C, C))
-    up_pay, down_pay = pl.pallas_call(
+    up_pay, down_pay, copies = pl.pallas_call(
         rows_kernel,
         name="pack_rows",
         out_shape=(
             shape(HALO + 1, TC, C),
             shape(HALO + 1, TC, C),
+            shape(16, C, C),
         ),
-        in_specs=[anywhere, vmem, vmem, vmem],
-        out_specs=(vmem, vmem),
-        scratch_shapes=[pltpu.SemaphoreType.DMA((2,))],
-    )(state, syndromes, erased, names)
+        in_specs=[anywhere, vmem, vmem, vmem, vmem],
+        out_specs=(vmem, vmem, anywhere),
+        scratch_shapes=[pltpu.SemaphoreType.DMA((2,)), pltpu.SemaphoreType.DMA((16,))],
+    )(state, read_weight, syndromes, erased, names)
 
     up = [(i, i - 1) for i in range(1, gx_count)]
     down = [(i, i + 1) for i in range(gx_count - 1)]

time: 110 us -> 111 us (level)
  waiting for transfers between devices: 40 us -> 42.5 us
  local copies, waits for them, and re-layouts: 14.2 us -> 12.3 us
    all_to_all x1, waiting for transfers between devices: 12 us -> 14.5 us  [gather_weights(): lax.all_to_all(copies, AX, 0, 0, tiled=True, axis_index_groups=class_grou...]
    broadcast_in_dim x1 -> x0, local copies, waits for them, and re-layouts: 1.91 us -> none  [decode(): copies = jnp.broadcast_to(read_weight[None], (16, C, C))]
    unnamed x48 -> x50, local copies, waits for them, and re-layouts: 11.2 us -> 11.2 us
  transfers between devices with their start and end apart: 18 -> 18, of which waited for: 6 -> 6; matrix products, arithmetic and copies ran while one was open for 1% -> 1% of each run, Pallas kernels for 9% -> 7%
where the time goes in v4:
time: 111 us; the launch traced here: 110 us
  waiting for transfers between devices  42.5 us (38%)
  starting transfers between devices  32 us (29%)
  Pallas kernels  23 us (21%)
  local copies, waits for them, and re-layouts  12.3 us (11%)
    all_to_all x1, waiting for transfers between devices, gather_weights(): lax.all_to_all(copies, AX, 0, 0, tiled=True, axis_index_groups=class_grou...  14.5 us
    pallas_call x1, Pallas kernels, decode(): pl.pallas_call(second_kernel, name='read_and_finish', compiler_params=plt...  12.3 us
    ppermute x3, waiting for transfers between devices, gather_weights(): pieces.append(lax.ppermute(low, AX, moved(*step)))  11.3 us
    unnamed x50, local copies, waits for them, and re-layouts  11.2 us
    all_to_all x1, starting transfers between devices, gather_weights(): lax.all_to_all(copies, AX, 0, 0, tiled=True, axis_index_groups=class_grou...  11 us
    ppermute x1, waiting for transfers between devices, decode(): bottom = lax.ppermute(up_pay, 'gx', up)  9.24 us
    pallas_call x1, Pallas kernels, decode(): pl.pallas_call(first_kernel, name='conv_first', compiler_params=pltpu.Com...  5.21 us
    ppermute x1, starting transfers between devices, decode(): right = lax.ppermute(west_pay, 'gy', west)  4.81 us
  transfers between devices with their start and end apart: 18, of which 6 were waited for; matrix products, arithmetic and copies ran while one was open for 1% of the time, Pallas kernels for 7%

profile of v4, /device:TPU:1, one launch (start us, length us, event | category | flops | bytes accessed | tf_op | source)
XLA Modules:
  0.0 110.1 jit_solution(8852968223109961531)
XLA Ops:
  0.0 3.0 %pack_rows.1 = (f32[5,64,128]{2,1,0:T(8,128)}, f32[5,64,128]{2,1,0:T(8,128)}, f32[16,128,128]{2,1,0:T(8,128)}) custom-call(f32[32,64,128]{2,1,0:T(8,128)} %state.5, f32[128,128]{1,0:T(8,128)} %weight.1, s32[2,32,64]{2,1,0:T(8,128)} %syndromes.5, s32[2,8,16]{2,1,0:T(8,128)} %erased.5, s32[1,128]{1,0:T(1,128)} %bitcast.8), custom_call_target="tpu_custom_call" | custom-call | tf_op jit(solution)/shard_map/pack_rows/pallas_call | solution.py:442
  3.1 11.0 %all-to-all-start = ((f32[16,128,128]{2,1,0:T(8,128)}), f32[16,128,128]{2,1,0:T(8,128)S(1)}, u32[]{:S(2)}, u32[]{:S(2)}) async-start(f32[16,128,128]{2,1,0:T(8,128)} %get-tuple-element.30), calls=%async_computation | async-start | bytes 2097152 | tf_op jit(solution)/shard_map/all_to_all | solution.py:48
  14.1 0.0 copy-start
  14.1 0.0 copy-start.5
  14.1 0.0 copy-start.6
  14.2 0.0 copy-start.7
  14.2 0.0 copy-start.8
  14.2 2.4 %collective-permute-start = (f32[5,64,128]{2,1,0:T(8,128)S(1)}, f32[5,64,128]{2,1,0:T(8,128)S(1)}, u32[]{:S(2)}, u32[]{:S(2)}) collective-permute-start(f32[5,64,128]{2,1,0:T(8,128)S(1)} %copy-done.24), channel_id=1, source_target_pairs={{0,8},{8,16},{16,24},{24,32},{32,40},{40,48},{48,56},{56,64},{64,7... | collective-permute-start | bytes 491528 | tf_op jit(solution)/shard_map/ppermute | solution.py:457
  16.6 14.5 %all-to-all-done.rest_0_ = f32[16,128,128]{2,1,0:T(8,128)S(1)} async-done(((f32[16,128,128]{2,1,0:T(8,128)}), f32[16,128,128]{2,1,0:T(8,128)S(1)}, u32[]{:S(2)}, u32[]{:S(2)}) %all-to-all-start) | async-done | bytes 1048608 | tf_op jit(solution)/shard_map/all_to_all | solution.py:48
  31.2 1.0 fusion
  32.2 0.1 collective-permute-start.9
  32.3 1.4 %collective-permute-start.7 = (f32[8,128,128]{2,1,0:T(8,128)}, f32[8,128,128]{2,1,0:T(8,128)}, u32[]{:S(2)}, u32[]{:S(2)}) collective-permute-start(f32[8,128,128]{2,1,0:T(8,128)} %get-tuple-element.31), channel_id=1, source_target_pairs={{0,24},{1,25},{2,26},{3,27},{4,28},{5,29},{6,30},{7,31},{8,0},{9,1... | collective-permute-start | bytes 1572872 | tf_op jit(solution)/shard_map/ppermute | solution.py:54
  33.7 3.2 %collective-permute-start.5 = (f32[8,128,128]{2,1,0:T(8,128)}, f32[8,128,128]{2,1,0:T(8,128)S(1)}, u32[]{:S(2)}, u32[]{:S(2)}) collective-permute-start(f32[8,128,128]{2,1,0:T(8,128)} %get-tuple-element.31), channel_id=1, source_target_pairs={{0,6},{1,7},{2,0},{3,1},{4,2},{5,3},{6,4},{7,5},{8,14},{9,15},{10,... | collective-permute-start | bytes 1572872 | tf_op jit(solution)/shard_map/ppermute | solution.py:54
  36.9 0.0 collective-permute-start.8
  36.9 0.0 collective-permute-done.top
  36.9 1.3 %collective-permute-start.1 = (f32[5,64,128]{2,1,0:T(8,128)S(1)}, f32[5,64,128]{2,1,0:T(8,128)S(1)}, u32[]{:S(2)}, u32[]{:S(2)}) collective-permute-start(f32[5,64,128]{2,1,0:T(8,128)S(1)} %copy-done.23), channel_id=1, source_target_pairs={{8,0},{16,8},{24,16},{32,24},{40,32},{48,40},{56,48},{64,56},{72,6... | collective-permute-start | bytes 491528 | tf_op jit(solution)/shard_map/ppermute | solution.py:458
  38.2 9.2 %collective-permute-done.1.bottom = f32[5,64,128]{2,1,0:T(8,128)S(1)} collective-permute-done((f32[5,64,128]{2,1,0:T(8,128)S(1)}, f32[5,64,128]{2,1,0:T(8,128)S(1)}, u32[]{:S(2)}, u32[]{:S(2)}) %collective-permute-start.1) | collective-permute-done | bytes 163872 | tf_op jit(solution)/shard_map/ppermute | solution.py:458
  47.5 0.0 copy-done.1
  47.5 0.7 copy-done.3
  48.1 2.4 %pack_cols.1 = (f32[40,8,128]{2,1,0:T(8,128)}, f32[40,8,128]{2,1,0:T(8,128)}, f32[40,64]{1,0:T(8,128)}, f32[16,128]{1,0:T(8,128)}, f32[16,128]{1,0:T(8,128)}) custom-call(f32[32,64,128]{2,1,0:T(8,128)} %state.5, f32[5,64,128]{2,1,0:T(8,128)} %copy-done.1, f32[5,64,128]{2,1,0:T(8,128)} %copy-done.3, s32[2,32,64]{2,1,0:T(8,128)} %syndromes.5, ...), custom_call_target="tpu_custom_call" | custom-call | tf_op jit(solution)/shard_map/pack_cols/pallas_call | solution.py:460
  50.6 4.8 %collective-permute-start.2 = (f32[40,8,128]{2,1,0:T(8,128)}, f32[40,8,128]{2,1,0:T(8,128)S(1)}, u32[]{:S(2)}, u32[]{:S(2)}) collective-permute-start(f32[40,8,128]{2,1,0:T(8,128)} %get-tuple-element.20), channel_id=1, source_target_pairs={{1,0},{2,1},{3,2},{4,3},{5,4},{6,5},{7,6},{9,8},{10,9},{11,10},{12... | collective-permute-start | bytes 491528 | tf_op jit(solution)/shard_map/ppermute | solution.py:478
  55.4 4.8 %collective-permute-done.2.right = f32[40,8,128]{2,1,0:T(8,128)S(1)} collective-permute-done((f32[40,8,128]{2,1,0:T(8,128)}, f32[40,8,128]{2,1,0:T(8,128)S(1)}, u32[]{:S(2)}, u32[]{:S(2)}) %collective-permute-start.2) | collective-permute-done | bytes 163872 | tf_op jit(solution)/shard_map/ppermute | solution.py:478
  60.2 1.9 %collective-permute-start.3 = (f32[40,8,128]{2,1,0:T(8,128)}, f32[40,8,128]{2,1,0:T(8,128)S(1)}, u32[]{:S(2)}, u32[]{:S(2)}) collective-permute-start(f32[40,8,128]{2,1,0:T(8,128)} %get-tuple-element.21), channel_id=1, source_target_pairs={{0,1},{1,2},{2,3},{3,4},{4,5},{5,6},{6,7},{8,9},{9,10},{10,11},{11... | collective-permute-start | bytes 491528 | tf_op jit(solution)/shard_map/ppermute | solution.py:477
  62.1 2.6 %collective-permute-done.3.left = f32[40,8,128]{2,1,0:T(8,128)S(1)} collective-permute-done((f32[40,8,128]{2,1,0:T(8,128)}, f32[40,8,128]{2,1,0:T(8,128)S(1)}, u32[]{:S(2)}, u32[]{:S(2)}) %collective-permute-start.3) | collective-permute-done | bytes 163872 | tf_op jit(solution)/shard_map/ppermute | solution.py:477
  64.7 1.4 %collective-permute-start.6 = (f32[8,128,128]{2,1,0:T(8,128)}, f32[8,128,128]{2,1,0:T(8,128)}, u32[]{:S(2)}, u32[]{:S(2)}) collective-permute-start(f32[8,128,128]{2,1,0:T(8,128)} %get-tuple-element.32), channel_id=1, source_target_pairs={{0,8},{1,9},{2,10},{3,11},{4,12},{5,13},{6,14},{7,15},{8,16},{9,17... | collective-permute-start | bytes 1572872 | tf_op jit(solution)/shard_map/ppermute | solution.py:53
  66.1 0.0 collective-permute-done.9.rest_6_
  66.1 0.1 collective-permute-start.4
  66.2 0.0 collective-permute-done.7.rest_4_
  66.2 3.0 %collective-permute-start.16 = (f32[8,128,128]{2,1,0:T(8,128)}, f32[8,128,128]{2,1,0:T(8,128)S(1)}, u32[]{:S(2)}, u32[]{:S(2)}) collective-permute-start(f32[8,128,128]{2,1,0:T(8,128)} %collective-permute-done.9.rest_6_), channel_id=1, source_target_pairs={{0,1},{1,0},{2,3},{3,2},{4,5},{5,4},{6,7},{7,6},{8,9},{9,8},{10,11... | collective-permute-start | bytes 1572872 | tf_op jit(solution)/shard_map/ppermute | solution.py:55
  69.1 0.0 collective-permute-done.5.rest_2_
  69.1 0.1 collective-permute-start.14
  69.2 0.7 copy-done.10
  69.9 0.0 collective-permute-done.8.rest_5_
  69.9 0.0 collective-permute-start.10
  70.0 9.8 %collective-permute-done.6.rest_3_ = f32[8,128,128]{2,1,0:T(8,128)} collective-permute-done((f32[8,128,128]{2,1,0:T(8,128)}, f32[8,128,128]{2,1,0:T(8,128)}, u32[]{:S(2)}, u32[]{:S(2)}) %collective-permute-start.6) | collective-permute-done | bytes 524320 | tf_op jit(solution)/shard_map/ppermute | solution.py:53
  79.7 0.0 collective-permute-start.12
  79.8 1.5 %collective-permute-done.4.rest_1_ = f32[8,128,128]{2,1,0:T(8,128)} collective-permute-done((f32[8,128,128]{2,1,0:T(8,128)}, f32[8,128,128]{2,1,0:T(8,128)}, u32[]{:S(2)}, u32[]{:S(2)}) %collective-permute-start.4) | collective-permute-done | bytes 524320 | tf_op jit(solution)/shard_map/ppermute | solution.py:53
  81.3 0.7 collective-permute-start.15
  82.0 0.0 collective-permute-done.16.rest_13_
  82.0 0.8 copy-done.12
  82.8 0.0 collective-permute-start.13
  82.8 0.0 collective-permute-done.14.rest_11_
  82.8 0.8 copy-done.14
  83.5 0.5 collective-permute-start.11
  84.0 0.1 pad_add_fusion.me
  84.1 0.0 copy-done
  84.1 0.0 copy-done.6
  84.2 0.9 copy-done.2
  85.1 0.9 copy-done.4
  86.0 1.1 copy-done.9
  87.1 0.7 copy-done.16
  87.8 0.7 copy-done.17
  88.5 0.7 copy-done.18
  89.2 5.2 %conv_first.1 = (f32[40,72,128]{2,1,0:T(8,128)S(1)}, f32[36,72,128]{2,1,0:T(8,128)S(1)}, f32[32,64,128]{2,1,0:T(8,128)S(1)}, bf16[768,768]{1,0:T(8,128)(2,1)S(1)}, s32[16,128]{1,0:T(8,128)S(1)}) custom-call(s32[4]{0:T(128)S(1)} %pad_add_fusion.me, f32[32,64,128]{2,1,0:T(8,128)S(1)} %copy-done, f32[5,64,128]{2,1,0:T(8,128)S(1)} %copy-done.2, ...), custom_call_target="tpu_custom_call" | custom-call | flops 2000000000 | bytes 6000000 | tf_op jit(solution)/shard_map/conv_first/pallas_call | solution.py:481
  94.4 0.0 copy-start.20
  94.4 1.1 %copy-done.20 = f32[40,72,128]{2,1,0:T(8,128)} copy-done((f32[40,72,128]{2,1,0:T(8,128)}, f32[40,72,128]{2,1,0:T(8,128)S(1)}, u32[]{:S(2)}) %copy-start.20) | copy-done | bytes 1474584
  95.6 1.1 copy-done.21
  96.6 1.0 copy-done.22
  97.6 0.0 collective-permute-done.12.rest_9_
  97.6 0.0 collective-permute-done.15.rest_12_
  97.6 0.0 collective-permute-done.13.rest_10_
  97.7 0.0 collective-permute-done.11.rest_8_
  97.7 0.0 collective-permute-done.10.rest_7_
  97.7 12.3 %read_and_finish.1 = f32[32,64,128]{2,1,0:T(8,128)} custom-call(s32[16,128]{1,0:T(8,128)S(1)} %get-tuple-element.25.slots, s32[4]{0:T(128)S(1)} %pad_add_fusion.me, f32[1,128]{1,0:T(1,128)S(1)} %bitcast.7, f32[40,72,128]{2,1,0:T(8,128)} %copy-done.20, f32[36,72,128]{2,1,0:T(8,128)} %copy-done.21, f32[32,64,128]{2,1,0:T(8,128)S(1)} %get-tuple-element.28.inputs_hbm, ...), custom_call_target="tpu_custom_call" | custom-call | flops 4000000000 | bytes 12000000 | tf_op jit(solution)/shard_map/read_and_finish/pallas_call | solution.py:515
  (28 shorter events, 0.1 us)
Async XLA Ops:
  3.0 11.1 %copy-start.24 = (f32[5,64,128]{2,1,0:T(8,128)S(1)}, f32[5,64,128]{2,1,0:T(8,128)}, u32[]{:S(2)}) copy-start(f32[5,64,128]{2,1,0:T(8,128)} %get-tuple-element.18) | copy-start | bytes 491524
  3.1 28.1 %all-to-all-start = ((f32[16,128,128]{2,1,0:T(8,128)}), f32[16,128,128]{2,1,0:T(8,128)S(1)}, u32[]{:S(2)}, u32[]{:S(2)}) async-start(f32[16,128,128]{2,1,0:T(8,128)} %get-tuple-element.30), calls=%async_computation | async-start | bytes 2097152 | tf_op jit(solution)/shard_map/all_to_all | solution.py:48
  14.1 22.8 %copy-start.23 = (f32[5,64,128]{2,1,0:T(8,128)S(1)}, f32[5,64,128]{2,1,0:T(8,128)}, u32[]{:S(2)}) copy-start(f32[5,64,128]{2,1,0:T(8,128)} %get-tuple-element.19) | copy-start | bytes 491524
  14.1 70.0 %copy-start = (f32[32,64,128]{2,1,0:T(8,128)S(1)}, f32[32,64,128]{2,1,0:T(8,128)}, u32[]{:S(2)}) copy-start(f32[32,64,128]{2,1,0:T(8,128)} %state.5) | copy-start | bytes 3145732
  14.1 70.0 %copy-start.5 = (s32[2,32,64]{2,1,0:T(8,128)S(1)}, s32[2,32,64]{2,1,0:T(8,128)}, u32[]{:S(2)}) copy-start(s32[2,32,64]{2,1,0:T(8,128)} %syndromes.5) | copy-start | bytes 49156
  14.1 70.0 %copy-start.6 = (s32[2,8,16]{2,1,0:T(8,128)S(1)}, s32[2,8,16]{2,1,0:T(8,128)}, u32[]{:S(2)}) copy-start(s32[2,8,16]{2,1,0:T(8,128)} %erased.5) | copy-start | bytes 3076
  14.2 70.0 %copy-start.7 = (f32[2,128]{1,0:T(2,128)S(1)}, f32[2,128]{1,0:T(2,128)}, u32[]{:S(2)}) copy-start(f32[2,128]{1,0:T(2,128)} %table.3) | copy-start | bytes 3076
  14.2 70.0 %copy-start.8 = (f32[128]{0:T(128)S(1)}, f32[128]{0:T(128)}, u32[]{:S(2)}) copy-start(f32[128]{0:T(128)} %param.15) | copy-start | bytes 1540
  14.2 22.7 %collective-permute-start = (f32[5,64,128]{2,1,0:T(8,128)S(1)}, f32[5,64,128]{2,1,0:T(8,128)S(1)}, u32[]{:S(2)}, u32[]{:S(2)}) collective-permute-start(f32[5,64,128]{2,1,0:T(8,128)S(1)} %copy-done.24), channel_id=1, source_target_pairs={{0,8},{8,16},{16,24},{24,32},{32,40},{40,48},{48,56},{56,64},{64,7... | collective-permute-start | bytes 491528 | tf_op jit(solution)/shard_map/ppermute | solution.py:457
  32.2 33.9 %collective-permute-start.9 = (f32[8,128,128]{2,1,0:T(8,128)}, f32[8,128,128]{2,1,0:T(8,128)}, u32[]{:S(2)}, u32[]{:S(2)}) collective-permute-start(f32[8,128,128]{2,1,0:T(8,128)} %get-tuple-element.31), channel_id=1, source_target_pairs={{0,96},{1,97},{2,98},{3,99},{4,100},{5,101},{6,102},{7,103},{8,104... | collective-permute-start | bytes 1572872 | tf_op jit(solution)/shard_map/ppermute | solution.py:54
  32.3 33.9 %collective-permute-start.7 = (f32[8,128,128]{2,1,0:T(8,128)}, f32[8,128,128]{2,1,0:T(8,128)}, u32[]{:S(2)}, u32[]{:S(2)}) collective-permute-start(f32[8,128,128]{2,1,0:T(8,128)} %get-tuple-element.31), channel_id=1, source_target_pairs={{0,24},{1,25},{2,26},{3,27},{4,28},{5,29},{6,30},{7,31},{8,0},{9,1... | collective-permute-start | bytes 1572872 | tf_op jit(solution)/shard_map/ppermute | solution.py:54
  33.7 35.5 %collective-permute-start.5 = (f32[8,128,128]{2,1,0:T(8,128)}, f32[8,128,128]{2,1,0:T(8,128)S(1)}, u32[]{:S(2)}, u32[]{:S(2)}) collective-permute-start(f32[8,128,128]{2,1,0:T(8,128)} %get-tuple-element.31), channel_id=1, source_target_pairs={{0,6},{1,7},{2,0},{3,1},{4,2},{5,3},{6,4},{7,5},{8,14},{9,15},{10,... | collective-permute-start | bytes 1572872 | tf_op jit(solution)/shard_map/ppermute | solution.py:54
  36.9 33.1 %collective-permute-start.8 = (f32[8,128,128]{2,1,0:T(8,128)}, f32[8,128,128]{2,1,0:T(8,128)}, u32[]{:S(2)}, u32[]{:S(2)}) collective-permute-start(f32[8,128,128]{2,1,0:T(8,128)} %get-tuple-element.32), channel_id=1, source_target_pairs={{0,32},{1,33},{2,34},{3,35},{4,36},{5,37},{6,38},{7,39},{8,40},{9,... | collective-permute-start | bytes 1572872 | tf_op jit(solution)/shard_map/ppermute | solution.py:53
  36.9 10.6 %copy-start.1 = (f32[5,64,128]{2,1,0:T(8,128)}, f32[5,64,128]{2,1,0:T(8,128)S(1)}, u32[]{:S(2)}) copy-start(f32[5,64,128]{2,1,0:T(8,128)S(1)} %collective-permute-done.top) | copy-start | bytes 491524
  36.9 10.5 %collective-permute-start.1 = (f32[5,64,128]{2,1,0:T(8,128)S(1)}, f32[5,64,128]{2,1,0:T(8,128)S(1)}, u32[]{:S(2)}, u32[]{:S(2)}) collective-permute-start(f32[5,64,128]{2,1,0:T(8,128)S(1)} %copy-done.23), channel_id=1, source_target_pairs={{8,0},{16,8},{24,16},{32,24},{40,32},{48,40},{56,48},{64,56},{72,6... | collective-permute-start | bytes 491528 | tf_op jit(solution)/shard_map/ppermute | solution.py:458
  47.5 0.7 copy-start.3
  50.6 9.6 %collective-permute-start.2 = (f32[40,8,128]{2,1,0:T(8,128)}, f32[40,8,128]{2,1,0:T(8,128)S(1)}, u32[]{:S(2)}, u32[]{:S(2)}) collective-permute-start(f32[40,8,128]{2,1,0:T(8,128)} %get-tuple-element.20), channel_id=1, source_target_pairs={{1,0},{2,1},{3,2},{4,3},{5,4},{6,5},{7,6},{9,8},{10,9},{11,10},{12... | collective-permute-start | bytes 491528 | tf_op jit(solution)/shard_map/ppermute | solution.py:478
  60.2 4.5 %collective-permute-start.3 = (f32[40,8,128]{2,1,0:T(8,128)}, f32[40,8,128]{2,1,0:T(8,128)S(1)}, u32[]{:S(2)}, u32[]{:S(2)}) collective-permute-start(f32[40,8,128]{2,1,0:T(8,128)} %get-tuple-element.21), channel_id=1, source_target_pairs={{0,1},{1,2},{2,3},{3,4},{4,5},{5,6},{6,7},{8,9},{9,10},{10,11},{11... | collective-permute-start | bytes 491528 | tf_op jit(solution)/shard_map/ppermute | solution.py:477
  64.7 15.1 %collective-permute-start.6 = (f32[8,128,128]{2,1,0:T(8,128)}, f32[8,128,128]{2,1,0:T(8,128)}, u32[]{:S(2)}, u32[]{:S(2)}) collective-permute-start(f32[8,128,128]{2,1,0:T(8,128)} %get-tuple-element.32), channel_id=1, source_target_pairs={{0,8},{1,9},{2,10},{3,11},{4,12},{5,13},{6,14},{7,15},{8,16},{9,17... | collective-permute-start | bytes 1572872 | tf_op jit(solution)/shard_map/ppermute | solution.py:53
  66.1 15.2 %collective-permute-start.4 = (f32[8,128,128]{2,1,0:T(8,128)}, f32[8,128,128]{2,1,0:T(8,128)}, u32[]{:S(2)}, u32[]{:S(2)}) collective-permute-start(f32[8,128,128]{2,1,0:T(8,128)} %get-tuple-element.32), channel_id=1, source_target_pairs={{0,2},{1,3},{2,4},{3,5},{4,6},{5,7},{6,0},{7,1},{8,10},{9,11},{10,... | collective-permute-start | bytes 1572872 | tf_op jit(solution)/shard_map/ppermute | solution.py:53
  66.2 15.8 %collective-permute-start.16 = (f32[8,128,128]{2,1,0:T(8,128)}, f32[8,128,128]{2,1,0:T(8,128)S(1)}, u32[]{:S(2)}, u32[]{:S(2)}) collective-permute-start(f32[8,128,128]{2,1,0:T(8,128)} %collective-permute-done.9.rest_6_), channel_id=1, source_target_pairs={{0,1},{1,0},{2,3},{3,2},{4,5},{5,4},{6,7},{7,6},{8,9},{9,8},{10,11... | collective-permute-start | bytes 1572872 | tf_op jit(solution)/shard_map/ppermute | solution.py:55
  69.1 0.8 copy-start.10
  69.1 13.6 %collective-permute-start.14 = (f32[8,128,128]{2,1,0:T(8,128)}, f32[8,128,128]{2,1,0:T(8,128)S(1)}, u32[]{:S(2)}, u32[]{:S(2)}) collective-permute-start(f32[8,128,128]{2,1,0:T(8,128)} %collective-permute-done.7.rest_4_), channel_id=1, source_target_pairs={{0,1},{1,0},{2,3},{3,2},{4,5},{5,4},{6,7},{7,6},{8,9},{9,8},{10,11... | collective-permute-start | bytes 1572872 | tf_op jit(solution)/shard_map/ppermute | solution.py:55
  69.9 27.7 %collective-permute-start.10 = (f32[16,128,128]{2,1,0:T(8,128)S(1)}, f32[16,128,128]{2,1,0:T(8,128)S(1)}, u32[]{:S(2)}, u32[]{:S(2)}) collective-permute-start(f32[16,128,128]{2,1,0:T(8,128)S(1)} %all-to-all-done.rest_0_), channel_id=1, source_target_pairs={{0,1},{1,0},{2,3},{3,2},{4,5},{5,4},{6,7},{7,6},{8,9},{9,8},{10,11... | collective-permute-start | bytes 3145736 | tf_op jit(solution)/shard_map/ppermute | solution.py:55
  79.7 17.9 %collective-permute-start.12 = (f32[8,128,128]{2,1,0:T(8,128)}, f32[8,128,128]{2,1,0:T(8,128)}, u32[]{:S(2)}, u32[]{:S(2)}) collective-permute-start(f32[8,128,128]{2,1,0:T(8,128)} %copy-done.10), channel_id=1, source_target_pairs={{0,1},{1,0},{2,3},{3,2},{4,5},{5,4},{6,7},{7,6},{8,9},{9,8},{10,11... | collective-permute-start | bytes 1572872 | tf_op jit(solution)/shard_map/ppermute | solution.py:55
  81.3 16.4 %collective-permute-start.15 = (f32[8,128,128]{2,1,0:T(8,128)}, f32[8,128,128]{2,1,0:T(8,128)}, u32[]{:S(2)}, u32[]{:S(2)}) collective-permute-start(f32[8,128,128]{2,1,0:T(8,128)} %collective-permute-done.8.rest_5_), channel_id=1, source_target_pairs={{0,1},{1,0},{2,3},{3,2},{4,5},{5,4},{6,7},{7,6},{8,9},{9,8},{10,11... | collective-permute-start | bytes 1572872 | tf_op jit(solution)/shard_map/ppermute | solution.py:55
  82.0 0.8 copy-start.12
  82.8 14.9 %collective-permute-start.13 = (f32[8,128,128]{2,1,0:T(8,128)}, f32[8,128,128]{2,1,0:T(8,128)}, u32[]{:S(2)}, u32[]{:S(2)}) collective-permute-start(f32[8,128,128]{2,1,0:T(8,128)} %collective-permute-done.6.rest_3_), channel_id=1, source_target_pairs={{0,1},{1,0},{2,3},{3,2},{4,5},{5,4},{6,7},{7,6},{8,9},{9,8},{10,11... | collective-permute-start | bytes 1572872 | tf_op jit(solution)/shard_map/ppermute | solution.py:55
  82.8 0.8 copy-start.14
  83.5 14.1 %collective-permute-start.11 = (f32[8,128,128]{2,1,0:T(8,128)}, f32[8,128,128]{2,1,0:T(8,128)}, u32[]{:S(2)}, u32[]{:S(2)}) collective-permute-start(f32[8,128,128]{2,1,0:T(8,128)} %collective-permute-done.4.rest_1_), channel_id=1, source_target_pairs={{0,1},{1,0},{2,3},{3,2},{4,5},{5,4},{6,7},{7,6},{8,9},{9,8},{10,11... | collective-permute-start | bytes 1572872 | tf_op jit(solution)/shard_map/ppermute | solution.py:55
  84.2 0.9 copy-start.2
  85.1 0.9 copy-start.4
  86.0 1.1 copy-start.9
  87.1 0.7 copy-start.16
  87.8 0.7 copy-start.17
  88.5 0.7 copy-start.18
  89.2 8.5 %copy-start.11 = (f32[8,128,128]{2,1,0:T(8,128)S(1)}, f32[8,128,128]{2,1,0:T(8,128)}, u32[]{:S(2)}) copy-start(f32[8,128,128]{2,1,0:T(8,128)} %copy-done.10) | copy-start | bytes 1572868
  89.2 8.5 %copy-start.13 = (f32[8,128,128]{2,1,0:T(8,128)S(1)}, f32[8,128,128]{2,1,0:T(8,128)}, u32[]{:S(2)}) copy-start(f32[8,128,128]{2,1,0:T(8,128)} %copy-done.12) | copy-start | bytes 1572868
  89.2 8.5 %copy-start.15 = (f32[8,128,128]{2,1,0:T(8,128)S(1)}, f32[8,128,128]{2,1,0:T(8,128)}, u32[]{:S(2)}) copy-start(f32[8,128,128]{2,1,0:T(8,128)} %copy-done.14) | copy-start | bytes 1572868
  89.2 8.5 %copy-start.19 = (f32[128]{0:T(128)S(1)}, f32[128]{0:T(128)}, u32[]{:S(2)}) copy-start(f32[128]{0:T(128)} %param.17) | copy-start | bytes 1540
  94.4 1.2 %copy-start.20 = (f32[40,72,128]{2,1,0:T(8,128)}, f32[40,72,128]{2,1,0:T(8,128)S(1)}, u32[]{:S(2)}) copy-start(f32[40,72,128]{2,1,0:T(8,128)S(1)} %get-tuple-element.26.ext_hbm) | copy-start | bytes 4423684
  95.6 1.1 copy-start.21
  96.6 1.0 copy-start.22

commit v5 on v4

--- a/solution.py
+++ b/solution.py
@@ -188,6 +188,43 @@
     return (((c + mc) & 1) * 4 + side) * 16 + z * 4 + (y >> 1) * 2 + (x >> 1)
 
 
+def prepare_kernel(
+    taps,
+    code,
+    syndromes,
+    erased,
+    table,
+    lost_vector,
+    first_out,
+    second_out,
+    weights_out,
+    codes,
+    turned,
+):
+    f32 = jnp.float32
+    for a in range(3):
+        for b in range(3):
+            high, low = split(taps[3 * a + b])
+            cols = slice(b * C, (b + 1) * C)
+            lows = slice((3 + b) * C, (4 + b) * C)
+            weights_out[a * C : (a + 1) * C, cols] = high
+            weights_out[a * C : (a + 1) * C, lows] = low
+            weights_out[(3 + a) * C : (4 + a) * C, cols] = high
+            weights_out[(3 + a) * C : (4 + a) * C, lows] = jnp.zeros((C, C), jnp.bfloat16)
+    codes[...] = jnp.zeros((C, C), f32)
+    codes[:TALL, :TC] = code[...]
+    second = repeat_blocks(erased[1].astype(f32), TR)
+    codes[TALL : TALL + TR, :TC] = jnp.where(second > 0.5, 2.0, syndromes[1].astype(f32))
+    turned[...] = codes[...].T
+    values, vector = table[...], lost_vector[...]
+    for r in range(HALO - 1, HALO + TR + 1):
+        column = jnp.broadcast_to(turned[:TC, r : r + 1], (TC, C))
+        first_out[r - HALO + 1] = embed(column, values, vector)
+    for r in range(TR):
+        column = jnp.broadcast_to(turned[:TC, TALL + r : TALL + r + 1], (TC, C))
+        second_out[r] = embed(column, values, vector)
+
+
 def first_kernel(
     me,
     state,
@@ -195,21 +232,14 @@
     bottom,
     right,
     left,
-    taps,
-    code,
+    inputs,
+    weights,
     lost,
     ids,
-    syndromes,
     erased,
-    table,
-    lost_vector,
     ext_out,
     pre_out,
-    inputs_out,
-    weights_out,
     slots_out,
-    codes,
-    turned,
     names,
 ):
     f32 = jnp.float32
@@ -219,16 +249,8 @@
     ext_out[HALO + TR :, :TC] = bottom[:HALO]
     for r in range(TALL):
         ext_out[r, TC:] = jnp.where(sub < 4, right[r], left[r])
-    for a in range(3):
-        for b in range(3):
-            high, low = split(taps[3 * a + b])
-            cols = slice(b * C, (b + 1) * C)
-            lows = slice((3 + b) * C, (4 + b) * C)
-            weights_out[a * C : (a + 1) * C, cols] = high
-            weights_out[a * C : (a + 1) * C, lows] = low
-            weights_out[(3 + a) * C : (4 + a) * C, cols] = high
-            weights_out[(3 + a) * C : (4 + a) * C, lows] = jnp.zeros((C, C), jnp.bfloat16)
-
+
+    names[...] = jnp.zeros((64, C), f32)
     for r in range(BROWS):
         names[r : r + 1] = right[r, 5:6, :]
         names[16 + r : 17 + r] = left[r, 2:3, :]
@@ -248,41 +270,26 @@
             ),
         ).astype(jnp.int32)
 
-    names[BROWS:16] = jnp.zeros((16 - BROWS, C), f32)
-    names[16 + BROWS : 32] = jnp.zeros((16 - BROWS, C), f32)
-    names[32 + BROWS : 48] = jnp.zeros((16 - BROWS, C), f32)
-    names[48 + BROWS :] = jnp.zeros((16 - BROWS, C), f32)
     slots_out[...] = slots_of(widen(ids[...], 32) & 127, me[0], me[1]) + 128 * widen(
         lost[...], 0
     )
     slots_out[1 : 1 + TR // BS, :wide] += 256 * erased[1]
 
-    codes[...] = jnp.zeros((C, C), f32)
-    codes[:TALL, :TC] = code[...]
-    second = repeat_blocks(erased[1].astype(f32), TR)
-    codes[TALL : TALL + TR, :TC] = jnp.where(second > 0.5, 2.0, syndromes[1].astype(f32))
-    turned[...] = codes[...].T
-    values, vector = table[...], lost_vector[...]
     pre_out[0] = jnp.zeros((WIDE, C), f32)
     pre_out[CONV_ROWS - 1] = jnp.zeros((WIDE, C), f32)
+    pre_out[1 : CONV_ROWS - 1, :TC] = inputs[...]
     for r in range(HALO - 1, HALO + TR + 1):
-        column = jnp.broadcast_to(turned[:TC, r : r + 1], (TC, C))
-        pre_out[r - 2, :TC] = embed(column, values, vector)
         pre_out[r - 2, TC:] = jnp.where(
             sub == 0,
             pltpu.roll(right[r], 4, 0),
             jnp.where(sub == 7, pltpu.roll(left[r], 4, 0), 0.0),
         )
-    for r in range(TR):
-        column = jnp.broadcast_to(turned[:TC, TALL + r : TALL + r + 1], (TC, C))
-        inputs_out[r] = embed(column, values, vector)
-
     rows = 12
 
     def step(i, carry):
         start = i * rows
         pre_out[pl.ds(start, rows)] += conv_chunk(
-            lambda a: ext_out[pl.ds(start + 1 + a, rows)], weights_out[...], rows
+            lambda a: ext_out[pl.ds(start + 1 + a, rows)], weights[...], rows
         )
         return carry
 
@@ -478,39 +485,28 @@
     right = lax.ppermute(west_pay, "gy", west)
     pieces = gather_weights(copies)
 
-    ext, pre, inputs, weights, slots = pl.pallas_call(
+    inputs_first, inputs, weights = pl.pallas_call(
+        prepare_kernel,
+        name="prepare",
+        compiler_params=pltpu.CompilerParams(vmem_limit_bytes=60 * 2**20),
+        out_shape=(shape(TR + 2, TC, C), shape(TR, TC, C), shape(6 * C, 6 * C, dtype=jnp.bfloat16)),
+        in_specs=[vmem] * 6,
+        out_specs=(vmem,) * 3,
+        scratch_shapes=[pltpu.VMEM((C, C), f32), pltpu.VMEM((C, C), f32)],
+    )(conv_weight, code, syndromes, erased, syndrome_table, lost_vector)
+
+    ext, pre, slots = pl.pallas_call(
         first_kernel,
         name="conv_first",
-        compiler_params=pltpu.CompilerParams(vmem_limit_bytes=16 * 2**20),
-        out_shape=(
-            shape(TALL, WIDE, C),
-            shape(CONV_ROWS, WIDE, C),
-            shape(TR, TC, C),
-            shape(6 * C, 6 * C, dtype=jnp.bfloat16),
-            shape(16, C, dtype=jnp.int32),
-        ),
-        in_specs=[smem] + [vmem] * 13,
-        out_specs=(vmem,) * 5,
-        scratch_shapes=[pltpu.VMEM((C, C), f32), pltpu.VMEM((C, C), f32), pltpu.VMEM((64, C), f32)],
+        compiler_params=pltpu.CompilerParams(vmem_limit_bytes=60 * 2**20),
+        out_shape=(shape(TALL, WIDE, C), shape(CONV_ROWS, WIDE, C), shape(16, C, dtype=jnp.int32)),
+        in_specs=[smem] + [vmem] * 10,
+        out_specs=(vmem,) * 3,
+        scratch_shapes=[pltpu.VMEM((64, C), f32)],
         cost_estimate=pl.CostEstimate(
             flops=2_000_000_000, bytes_accessed=6_000_000, transcendentals=0
         ),
-    )(
-        me,
-        state,
-        top,
-        bottom,
-        right,
-        left,
-        conv_weight,
-        code,
-        lost,
-        ids,
-        syndromes,
-        erased,
-        syndrome_table,
-        lost_vector,
-    )
+    )(me, state, top, bottom, right, left, inputs_first, weights, lost, ids, erased)
 
     return pl.pallas_call(
         second_kernel,

time: 111 us -> 111 us (level)
  the two profiles are of different devices: /device:TPU:1 before, /device:TPU:27 now
where the time goes in v5:
time: 111 us; the launch traced here: 110 us
  waiting for transfers between devices  39.2 us (35%)
  starting transfers between devices  34.1 us (31%)
  Pallas kernels  28.3 us (25%)
  local copies, waits for them, and re-layouts  8.01 us (7%)
    ppermute x1, waiting for transfers between devices, decode(): bottom = lax.ppermute(up_pay, 'gx', up)  12.5 us
    pallas_call x1, Pallas kernels, decode(): pl.pallas_call(second_kernel, name='read_and_finish', compiler_params=plt...  12.2 us
    all_to_all x1, waiting for transfers between devices, gather_weights(): lax.all_to_all(copies, AX, 0, 0, tiled=True, axis_index_groups=class_grou...  11.5 us
    all_to_all x1, starting transfers between devices, gather_weights(): lax.all_to_all(copies, AX, 0, 0, tiled=True, axis_index_groups=class_grou...  9.28 us
    ppermute x3, waiting for transfers between devices, gather_weights(): pieces.append(lax.ppermute(low, AX, moved(*step)))  8.2 us
    pallas_call x1, Pallas kernels, decode(): pl.pallas_call(first_kernel, name='conv_first', compiler_params=pltpu.Com...  6.95 us
    unnamed x36, local copies, waits for them, and re-layouts  6.94 us
    ppermute x1, starting transfers between devices, decode(): right = lax.ppermute(west_pay, 'gy', west)  5.97 us
  transfers between devices with their start and end apart: 18, of which 5 were waited for; matrix products, arithmetic and copies ran while one was open for 2% of the time, Pallas kernels for 12%

profile of v5, /device:TPU:27, one launch (start us, length us, event | category | flops | bytes accessed | tf_op | source)
XLA Modules:
  0.0 110.3 jit_solution(16423495967023556521)
XLA Ops:
  0.0 3.0 %pack_rows.1 = (f32[5,64,128]{2,1,0:T(8,128)}, f32[5,64,128]{2,1,0:T(8,128)}, f32[16,128,128]{2,1,0:T(8,128)}) custom-call(f32[32,64,128]{2,1,0:T(8,128)} %state.5, f32[128,128]{1,0:T(8,128)} %weight.1, s32[2,32,64]{2,1,0:T(8,128)} %syndromes.5, s32[2,8,16]{2,1,0:T(8,128)} %erased.7, s32[1,128]{1,0:T(1,128)} %bitcast.6), custom_call_target="tpu_custom_call" | custom-call | tf_op jit(solution)/shard_map/pack_rows/pallas_call | solution.py:449
  3.0 0.0 copy-start.17
  3.1 9.3 %all-to-all-start = ((f32[16,128,128]{2,1,0:T(8,128)}), f32[16,128,128]{2,1,0:T(8,128)S(1)}, u32[]{:S(2)}, u32[]{:S(2)}) async-start(f32[16,128,128]{2,1,0:T(8,128)} %get-tuple-element.32), calls=%async_computation | async-start | bytes 2097152 | tf_op jit(solution)/shard_map/all_to_all | solution.py:48
  12.3 0.0 copy-done.17
  12.3 4.1 %collective-permute-start = (f32[5,64,128]{2,1,0:T(8,128)S(1)}, f32[5,64,128]{2,1,0:T(8,128)S(1)}, u32[]{:S(2)}, u32[]{:S(2)}) collective-permute-start(f32[5,64,128]{2,1,0:T(8,128)S(1)} %copy-done.17), channel_id=1, source_target_pairs={{0,8},{8,16},{16,24},{24,32},{32,40},{40,48},{48,56},{56,64},{64,7... | collective-permute-start | bytes 491528 | tf_op jit(solution)/shard_map/ppermute | solution.py:464
  16.5 11.5 %all-to-all-done.rest_0_ = f32[16,128,128]{2,1,0:T(8,128)S(1)} async-done(((f32[16,128,128]{2,1,0:T(8,128)}), f32[16,128,128]{2,1,0:T(8,128)S(1)}, u32[]{:S(2)}, u32[]{:S(2)}) %all-to-all-start) | async-done | bytes 1048608 | tf_op jit(solution)/shard_map/all_to_all | solution.py:48
  27.9 1.1 fusion
  29.0 1.0 collective-permute-start.4
  30.0 0.4 collective-permute-start.5
  30.5 2.1 %collective-permute-start.6 = (f32[8,128,128]{2,1,0:T(8,128)}, f32[8,128,128]{2,1,0:T(8,128)}, u32[]{:S(2)}, u32[]{:S(2)}) collective-permute-start(f32[8,128,128]{2,1,0:T(8,128)} %get-tuple-element.34), channel_id=1, source_target_pairs={{0,8},{1,9},{2,10},{3,11},{4,12},{5,13},{6,14},{7,15},{8,16},{9,17... | collective-permute-start | bytes 1572872 | tf_op jit(solution)/shard_map/ppermute | solution.py:53
  32.6 0.0 collective-permute-start.7
  32.6 0.0 collective-permute-done.top
  32.6 0.0 copy-done.16
  32.6 1.9 %collective-permute-start.1 = (f32[5,64,128]{2,1,0:T(8,128)S(1)}, f32[5,64,128]{2,1,0:T(8,128)S(1)}, u32[]{:S(2)}, u32[]{:S(2)}) collective-permute-start(f32[5,64,128]{2,1,0:T(8,128)S(1)} %copy-done.16), channel_id=1, source_target_pairs={{8,0},{16,8},{24,16},{32,24},{40,32},{48,40},{56,48},{64,56},{72,6... | collective-permute-start | bytes 491528 | tf_op jit(solution)/shard_map/ppermute | solution.py:465
  34.5 12.5 %collective-permute-done.1.bottom = f32[5,64,128]{2,1,0:T(8,128)S(1)} collective-permute-done((f32[5,64,128]{2,1,0:T(8,128)S(1)}, f32[5,64,128]{2,1,0:T(8,128)S(1)}, u32[]{:S(2)}, u32[]{:S(2)}) %collective-permute-start.1) | collective-permute-done | bytes 163872 | tf_op jit(solution)/shard_map/ppermute | solution.py:465
  47.0 0.0 copy-done.12
  47.0 0.7 copy-done.13
  47.7 2.5 %pack_cols.1 = (f32[40,8,128]{2,1,0:T(8,128)}, f32[40,8,128]{2,1,0:T(8,128)}, f32[40,64]{1,0:T(8,128)}, f32[16,128]{1,0:T(8,128)}, f32[16,128]{1,0:T(8,128)}) custom-call(f32[32,64,128]{2,1,0:T(8,128)} %state.5, f32[5,64,128]{2,1,0:T(8,128)} %copy-done.12, f32[5,64,128]{2,1,0:T(8,128)} %copy-done.13, s32[2,32,64]{2,1,0:T(8,128)} %syndromes.5, ...), custom_call_target="tpu_custom_call" | custom-call | tf_op jit(solution)/shard_map/pack_cols/pallas_call | solution.py:467
  50.1 6.0 %collective-permute-start.2 = (f32[40,8,128]{2,1,0:T(8,128)}, f32[40,8,128]{2,1,0:T(8,128)S(1)}, u32[]{:S(2)}, u32[]{:S(2)}) collective-permute-start(f32[40,8,128]{2,1,0:T(8,128)} %get-tuple-element.21), channel_id=1, source_target_pairs={{1,0},{2,1},{3,2},{4,3},{5,4},{6,5},{7,6},{9,8},{10,9},{11,10},{12... | collective-permute-start | bytes 491528 | tf_op jit(solution)/shard_map/ppermute | solution.py:485
  56.1 4.5 %collective-permute-done.2.right = f32[40,8,128]{2,1,0:T(8,128)S(1)} collective-permute-done((f32[40,8,128]{2,1,0:T(8,128)}, f32[40,8,128]{2,1,0:T(8,128)S(1)}, u32[]{:S(2)}, u32[]{:S(2)}) %collective-permute-start.2) | collective-permute-done | bytes 163872 | tf_op jit(solution)/shard_map/ppermute | solution.py:485
  60.6 1.9 %collective-permute-start.3 = (f32[40,8,128]{2,1,0:T(8,128)}, f32[40,8,128]{2,1,0:T(8,128)S(1)}, u32[]{:S(2)}, u32[]{:S(2)}) collective-permute-start(f32[40,8,128]{2,1,0:T(8,128)} %get-tuple-element.22), channel_id=1, source_target_pairs={{0,1},{1,2},{2,3},{3,4},{4,5},{5,6},{6,7},{8,9},{9,10},{10,11},{11... | collective-permute-start | bytes 491528 | tf_op jit(solution)/shard_map/ppermute | solution.py:484
  62.5 2.6 %collective-permute-done.3.left = f32[40,8,128]{2,1,0:T(8,128)S(1)} collective-permute-done((f32[40,8,128]{2,1,0:T(8,128)}, f32[40,8,128]{2,1,0:T(8,128)S(1)}, u32[]{:S(2)}, u32[]{:S(2)}) %collective-permute-start.3) | collective-permute-done | bytes 163872 | tf_op jit(solution)/shard_map/ppermute | solution.py:484
  65.0 0.8 collective-permute-start.8
  65.8 0.0 collective-permute-done.4.rest_1_
  65.8 1.9 %collective-permute-start.9 = (f32[8,128,128]{2,1,0:T(8,128)}, f32[8,128,128]{2,1,0:T(8,128)}, u32[]{:S(2)}, u32[]{:S(2)}) collective-permute-start(f32[8,128,128]{2,1,0:T(8,128)} %get-tuple-element.33), channel_id=1, source_target_pairs={{0,96},{1,97},{2,98},{3,99},{4,100},{5,101},{6,102},{7,103},{8,104... | collective-permute-start | bytes 1572872 | tf_op jit(solution)/shard_map/ppermute | solution.py:54
  67.7 0.0 collective-permute-done.5.rest_2_
  67.7 1.7 %collective-permute-start.11 = (f32[8,128,128]{2,1,0:T(8,128)S(1)}, f32[8,128,128]{2,1,0:T(8,128)S(1)}, u32[]{:S(2)}, u32[]{:S(2)}) collective-permute-start(f32[8,128,128]{2,1,0:T(8,128)S(1)} %collective-permute-done.4.rest_1_), channel_id=1, source_target_pairs={{0,1},{1,0},{2,3},{3,2},{4,5},{5,4},{6,7},{7,6},{8,9},{9,8},{10,11... | collective-permute-start | bytes 1572872 | tf_op jit(solution)/shard_map/ppermute | solution.py:55
  69.4 0.0 collective-permute-done.6.rest_3_
  69.4 0.1 collective-permute-start.12
  69.5 0.8 copy-done.4
  70.3 0.0 collective-permute-done.7.rest_4_
  70.3 0.4 collective-permute-start.10
  70.7 8.2 %collective-permute-done.8.rest_5_ = f32[8,128,128]{2,1,0:T(8,128)} collective-permute-done((f32[8,128,128]{2,1,0:T(8,128)}, f32[8,128,128]{2,1,0:T(8,128)}, u32[]{:S(2)}, u32[]{:S(2)}) %collective-permute-start.8) | collective-permute-done | bytes 524320 | tf_op jit(solution)/shard_map/ppermute | solution.py:53
  78.9 2.0 %collective-permute-start.13 = (f32[8,128,128]{2,1,0:T(8,128)}, f32[8,128,128]{2,1,0:T(8,128)}, u32[]{:S(2)}, u32[]{:S(2)}) collective-permute-start(f32[8,128,128]{2,1,0:T(8,128)} %collective-permute-done.6.rest_3_), channel_id=1, source_target_pairs={{0,1},{1,0},{2,3},{3,2},{4,5},{5,4},{6,7},{7,6},{8,9},{9,8},{10,11... | collective-permute-start | bytes 1572872 | tf_op jit(solution)/shard_map/ppermute | solution.py:55
  80.9 0.0 collective-permute-done.9.rest_6_
  80.9 0.0 collective-permute-start.14
  80.9 0.0 collective-permute-done.11.rest_8_
  80.9 0.0 copy-start.6
  80.9 0.8 copy-done.6
  81.7 0.5 collective-permute-start.15
  82.2 0.0 collective-permute-done.12.rest_9_
  82.2 0.8 copy-done.8
  83.0 0.0 collective-permute-start.16
  83.0 0.6 pad_add_fusion.me
  83.6 3.6 %prepare.1 = (f32[34,64,128]{2,1,0:T(8,128)}, f32[32,64,128]{2,1,0:T(8,128)}, bf16[768,768]{1,0:T(8,128)(2,1)}) custom-call(f32[9,128,128]{2,1,0:T(8,128)} %taps.1, f32[40,64]{1,0:T(8,128)} %get-tuple-element.23.code, s32[2,32,64]{2,1,0:T(8,128)} %syndromes.5, s32[2,8,16]{2,1,0:T(8,128)} %erased.7, f32[2,128]{1,0:T(2,128)} %table.3, f32[1,128]{1,0:T(1,128)} %bitcast.9), custom_call_target="tpu_custom_call" | custom-call | tf_op jit(solution)/shard_map/prepare/pallas_call | solution.py:488
  87.3 0.0 copy-done.2
  87.3 0.0 copy-done.14
  87.3 0.0 copy-done.15
  87.3 0.0 copy-start
  87.3 0.0 copy-start.1
  87.3 0.0 copy-start.3
  87.3 0.0 copy-start.10
  87.3 6.9 %conv_first.1 = (f32[40,72,128]{2,1,0:T(8,128)}, f32[36,72,128]{2,1,0:T(8,128)}, s32[16,128]{1,0:T(8,128)}) custom-call(s32[4]{0:T(128)} %pad_add_fusion.me, f32[32,64,128]{2,1,0:T(8,128)} %state.5, f32[5,64,128]{2,1,0:T(8,128)} %copy-done.12, f32[5,64,128]{2,1,0:T(8,128)} %copy-done.13, f32[40,8,128]{2,1,0:T(8,128)} %copy-done.14, ...), custom_call_target="tpu_custom_call" | custom-call | flops 2000000000 | bytes 6000000 | tf_op jit(solution)/shard_map/conv_first/pallas_call | solution.py:498
  94.3 0.0 collective-permute-done.13.rest_10_
  94.3 0.0 collective-permute-done.14.rest_11_
  94.3 0.0 collective-permute-done.15.rest_12_
  94.3 0.0 collective-permute-done.16.rest_13_
  94.3 0.0 collective-permute-done.10.rest_7_
  94.3 0.0 copy-done
  94.4 1.0 copy-done.5
  95.4 1.0 copy-done.7
  96.4 1.0 copy-done.9
  97.5 0.7 copy-done.11
  98.2 12.2 %read_and_finish.1 = f32[32,64,128]{2,1,0:T(8,128)} custom-call(s32[16,128]{1,0:T(8,128)S(1)} %copy-done.11, s32[4]{0:T(128)S(1)} %copy-done, f32[1,128]{1,0:T(1,128)S(1)} %bitcast.5, f32[40,72,128]{2,1,0:T(8,128)} %get-tuple-element.29.ext_hbm, f32[36,72,128]{2,1,0:T(8,128)} %get-tuple-element.30.pre_hbm, f32[32,64,128]{2,1,0:T(8,128)S(1)} %copy-done.1, ...), custom_call_target="tpu_custom_call" | custom-call | flops 4000000000 | bytes 12000000 | tf_op jit(solution)/shard_map/read_and_finish/pallas_call | solution.py:511
  (15 shorter events, 0.0 us)
Async XLA Ops:
  3.0 9.3 %copy-start.17 = (f32[5,64,128]{2,1,0:T(8,128)S(1)}, f32[5,64,128]{2,1,0:T(8,128)}, u32[]{:S(2)}) copy-start(f32[5,64,128]{2,1,0:T(8,128)} %get-tuple-element.19) | copy-start | bytes 491524
  3.1 24.9 %all-to-all-start = ((f32[16,128,128]{2,1,0:T(8,128)}), f32[16,128,128]{2,1,0:T(8,128)S(1)}, u32[]{:S(2)}, u32[]{:S(2)}) async-start(f32[16,128,128]{2,1,0:T(8,128)} %get-tuple-element.32), calls=%async_computation | async-start | bytes 2097152 | tf_op jit(solution)/shard_map/all_to_all | solution.py:48
  12.3 20.3 %copy-start.16 = (f32[5,64,128]{2,1,0:T(8,128)S(1)}, f32[5,64,128]{2,1,0:T(8,128)}, u32[]{:S(2)}) copy-start(f32[5,64,128]{2,1,0:T(8,128)} %get-tuple-element.20) | copy-start | bytes 491524
  12.3 20.2 %collective-permute-start = (f32[5,64,128]{2,1,0:T(8,128)S(1)}, f32[5,64,128]{2,1,0:T(8,128)S(1)}, u32[]{:S(2)}, u32[]{:S(2)}) collective-permute-start(f32[5,64,128]{2,1,0:T(8,128)S(1)} %copy-done.17), channel_id=1, source_target_pairs={{0,8},{8,16},{16,24},{24,32},{32,40},{40,48},{48,56},{56,64},{64,7... | collective-permute-start | bytes 491528 | tf_op jit(solution)/shard_map/ppermute | solution.py:464
  29.0 36.8 %collective-permute-start.4 = (f32[8,128,128]{2,1,0:T(8,128)}, f32[8,128,128]{2,1,0:T(8,128)S(1)}, u32[]{:S(2)}, u32[]{:S(2)}) collective-permute-start(f32[8,128,128]{2,1,0:T(8,128)} %get-tuple-element.34), channel_id=1, source_target_pairs={{0,2},{1,3},{2,4},{3,5},{4,6},{5,7},{6,0},{7,1},{8,10},{9,11},{10,... | collective-permute-start | bytes 1572872 | tf_op jit(solution)/shard_map/ppermute | solution.py:53
  30.0 37.7 %collective-permute-start.5 = (f32[8,128,128]{2,1,0:T(8,128)}, f32[8,128,128]{2,1,0:T(8,128)S(1)}, u32[]{:S(2)}, u32[]{:S(2)}) collective-permute-start(f32[8,128,128]{2,1,0:T(8,128)} %get-tuple-element.33), channel_id=1, source_target_pairs={{0,6},{1,7},{2,0},{3,1},{4,2},{5,3},{6,4},{7,5},{8,14},{9,15},{10,... | collective-permute-start | bytes 1572872 | tf_op jit(solution)/shard_map/ppermute | solution.py:54
  30.5 38.9 %collective-permute-start.6 = (f32[8,128,128]{2,1,0:T(8,128)}, f32[8,128,128]{2,1,0:T(8,128)}, u32[]{:S(2)}, u32[]{:S(2)}) collective-permute-start(f32[8,128,128]{2,1,0:T(8,128)} %get-tuple-element.34), channel_id=1, source_target_pairs={{0,8},{1,9},{2,10},{3,11},{4,12},{5,13},{6,14},{7,15},{8,16},{9,17... | collective-permute-start | bytes 1572872 | tf_op jit(solution)/shard_map/ppermute | solution.py:53
  32.6 37.7 %collective-permute-start.7 = (f32[8,128,128]{2,1,0:T(8,128)}, f32[8,128,128]{2,1,0:T(8,128)}, u32[]{:S(2)}, u32[]{:S(2)}) collective-permute-start(f32[8,128,128]{2,1,0:T(8,128)} %get-tuple-element.33), channel_id=1, source_target_pairs={{0,24},{1,25},{2,26},{3,27},{4,28},{5,29},{6,30},{7,31},{8,0},{9,1... | collective-permute-start | bytes 1572872 | tf_op jit(solution)/shard_map/ppermute | solution.py:54
  32.6 14.4 %copy-start.12 = (f32[5,64,128]{2,1,0:T(8,128)}, f32[5,64,128]{2,1,0:T(8,128)S(1)}, u32[]{:S(2)}) copy-start(f32[5,64,128]{2,1,0:T(8,128)S(1)} %collective-permute-done.top) | copy-start | bytes 491524
  32.6 14.4 %collective-permute-start.1 = (f32[5,64,128]{2,1,0:T(8,128)S(1)}, f32[5,64,128]{2,1,0:T(8,128)S(1)}, u32[]{:S(2)}, u32[]{:S(2)}) collective-permute-start(f32[5,64,128]{2,1,0:T(8,128)S(1)} %copy-done.16), channel_id=1, source_target_pairs={{8,0},{16,8},{24,16},{32,24},{40,32},{48,40},{56,48},{64,56},{72,6... | collective-permute-start | bytes 491528 | tf_op jit(solution)/shard_map/ppermute | solution.py:465
  47.0 0.7 copy-start.13
  50.1 10.4 %collective-permute-start.2 = (f32[40,8,128]{2,1,0:T(8,128)}, f32[40,8,128]{2,1,0:T(8,128)S(1)}, u32[]{:S(2)}, u32[]{:S(2)}) collective-permute-start(f32[40,8,128]{2,1,0:T(8,128)} %get-tuple-element.21), channel_id=1, source_target_pairs={{1,0},{2,1},{3,2},{4,3},{5,4},{6,5},{7,6},{9,8},{10,9},{11,10},{12... | collective-permute-start | bytes 491528 | tf_op jit(solution)/shard_map/ppermute | solution.py:485
  60.6 26.7 %copy-start.14 = (f32[40,8,128]{2,1,0:T(8,128)}, f32[40,8,128]{2,1,0:T(8,128)S(1)}, u32[]{:S(2)}) copy-start(f32[40,8,128]{2,1,0:T(8,128)S(1)} %collective-permute-done.2.right) | copy-start | bytes 491524
  60.6 4.5 %collective-permute-start.3 = (f32[40,8,128]{2,1,0:T(8,128)}, f32[40,8,128]{2,1,0:T(8,128)S(1)}, u32[]{:S(2)}, u32[]{:S(2)}) collective-permute-start(f32[40,8,128]{2,1,0:T(8,128)} %get-tuple-element.22), channel_id=1, source_target_pairs={{0,1},{1,2},{2,3},{3,4},{4,5},{5,6},{6,7},{8,9},{9,10},{10,11},{11... | collective-permute-start | bytes 491528 | tf_op jit(solution)/shard_map/ppermute | solution.py:484
  65.0 22.2 %copy-start.15 = (f32[40,8,128]{2,1,0:T(8,128)}, f32[40,8,128]{2,1,0:T(8,128)S(1)}, u32[]{:S(2)}) copy-start(f32[40,8,128]{2,1,0:T(8,128)S(1)} %collective-permute-done.3.left) | copy-start | bytes 491524
  65.0 13.9 %collective-permute-start.8 = (f32[8,128,128]{2,1,0:T(8,128)}, f32[8,128,128]{2,1,0:T(8,128)}, u32[]{:S(2)}, u32[]{:S(2)}) collective-permute-start(f32[8,128,128]{2,1,0:T(8,128)} %get-tuple-element.34), channel_id=1, source_target_pairs={{0,32},{1,33},{2,34},{3,35},{4,36},{5,37},{6,38},{7,39},{8,40},{9,... | collective-permute-start | bytes 1572872 | tf_op jit(solution)/shard_map/ppermute | solution.py:53
  65.8 21.4 %copy-start.2 = (f32[8,128,128]{2,1,0:T(8,128)}, f32[8,128,128]{2,1,0:T(8,128)S(1)}, u32[]{:S(2)}) copy-start(f32[8,128,128]{2,1,0:T(8,128)S(1)} %collective-permute-done.4.rest_1_) | copy-start | bytes 1572868
  65.8 15.1 %collective-permute-start.9 = (f32[8,128,128]{2,1,0:T(8,128)}, f32[8,128,128]{2,1,0:T(8,128)}, u32[]{:S(2)}, u32[]{:S(2)}) collective-permute-start(f32[8,128,128]{2,1,0:T(8,128)} %get-tuple-element.33), channel_id=1, source_target_pairs={{0,96},{1,97},{2,98},{3,99},{4,100},{5,101},{6,102},{7,103},{8,104... | collective-permute-start | bytes 1572872 | tf_op jit(solution)/shard_map/ppermute | solution.py:54
  67.7 13.2 %collective-permute-start.11 = (f32[8,128,128]{2,1,0:T(8,128)S(1)}, f32[8,128,128]{2,1,0:T(8,128)S(1)}, u32[]{:S(2)}, u32[]{:S(2)}) collective-permute-start(f32[8,128,128]{2,1,0:T(8,128)S(1)} %collective-permute-done.4.rest_1_), channel_id=1, source_target_pairs={{0,1},{1,0},{2,3},{3,2},{4,5},{5,4},{6,7},{7,6},{8,9},{9,8},{10,11... | collective-permute-start | bytes 1572872 | tf_op jit(solution)/shard_map/ppermute | solution.py:55
  69.4 12.8 %collective-permute-start.12 = (f32[8,128,128]{2,1,0:T(8,128)S(1)}, f32[8,128,128]{2,1,0:T(8,128)S(1)}, u32[]{:S(2)}, u32[]{:S(2)}) collective-permute-start(f32[8,128,128]{2,1,0:T(8,128)S(1)} %collective-permute-done.5.rest_2_), channel_id=1, source_target_pairs={{0,1},{1,0},{2,3},{3,2},{4,5},{5,4},{6,7},{7,6},{8,9},{9,8},{10,11... | collective-permute-start | bytes 1572872 | tf_op jit(solution)/shard_map/ppermute | solution.py:55
  69.5 0.8 copy-start.4
  70.3 24.0 %collective-permute-start.10 = (f32[16,128,128]{2,1,0:T(8,128)S(1)}, f32[16,128,128]{2,1,0:T(8,128)S(1)}, u32[]{:S(2)}, u32[]{:S(2)}) collective-permute-start(f32[16,128,128]{2,1,0:T(8,128)S(1)} %all-to-all-done.rest_0_), channel_id=1, source_target_pairs={{0,1},{1,0},{2,3},{3,2},{4,5},{5,4},{6,7},{7,6},{8,9},{9,8},{10,11... | collective-permute-start | bytes 3145736 | tf_op jit(solution)/shard_map/ppermute | solution.py:55
  78.9 15.3 %collective-permute-start.13 = (f32[8,128,128]{2,1,0:T(8,128)}, f32[8,128,128]{2,1,0:T(8,128)}, u32[]{:S(2)}, u32[]{:S(2)}) collective-permute-start(f32[8,128,128]{2,1,0:T(8,128)} %collective-permute-done.6.rest_3_), channel_id=1, source_target_pairs={{0,1},{1,0},{2,3},{3,2},{4,5},{5,4},{6,7},{7,6},{8,9},{9,8},{10,11... | collective-permute-start | bytes 1572872 | tf_op jit(solution)/shard_map/ppermute | solution.py:55
  80.9 13.4 %collective-permute-start.14 = (f32[8,128,128]{2,1,0:T(8,128)}, f32[8,128,128]{2,1,0:T(8,128)}, u32[]{:S(2)}, u32[]{:S(2)}) collective-permute-start(f32[8,128,128]{2,1,0:T(8,128)} %collective-permute-done.7.rest_4_), channel_id=1, source_target_pairs={{0,1},{1,0},{2,3},{3,2},{4,5},{5,4},{6,7},{7,6},{8,9},{9,8},{10,11... | collective-permute-start | bytes 1572872 | tf_op jit(solution)/shard_map/ppermute | solution.py:55
  80.9 0.8 copy-start.6
  81.7 12.6 %collective-permute-start.15 = (f32[8,128,128]{2,1,0:T(8,128)}, f32[8,128,128]{2,1,0:T(8,128)}, u32[]{:S(2)}, u32[]{:S(2)}) collective-permute-start(f32[8,128,128]{2,1,0:T(8,128)} %collective-permute-done.8.rest_5_), channel_id=1, source_target_pairs={{0,1},{1,0},{2,3},{3,2},{4,5},{5,4},{6,7},{7,6},{8,9},{9,8},{10,11... | collective-permute-start | bytes 1572872 | tf_op jit(solution)/shard_map/ppermute | solution.py:55
  82.2 0.8 copy-start.8
  83.0 11.3 %collective-permute-start.16 = (f32[8,128,128]{2,1,0:T(8,128)}, f32[8,128,128]{2,1,0:T(8,128)}, u32[]{:S(2)}, u32[]{:S(2)}) collective-permute-start(f32[8,128,128]{2,1,0:T(8,128)} %collective-permute-done.9.rest_6_), channel_id=1, source_target_pairs={{0,1},{1,0},{2,3},{3,2},{4,5},{5,4},{6,7},{7,6},{8,9},{9,8},{10,11... | collective-permute-start | bytes 1572872 | tf_op jit(solution)/shard_map/ppermute | solution.py:55
  87.3 7.0 %copy-start = (s32[4]{0:T(128)S(1)}, s32[4]{0:T(128)}, u32[]{:S(2)}) copy-start(s32[4]{0:T(128)} %pad_add_fusion.me) | copy-start | bytes 52
  87.3 7.0 %copy-start.1 = (f32[32,64,128]{2,1,0:T(8,128)S(1)}, f32[32,64,128]{2,1,0:T(8,128)}, u32[]{:S(2)}) copy-start(f32[32,64,128]{2,1,0:T(8,128)} %get-tuple-element.31.inputs_hbm) | copy-start | bytes 3145732
  87.3 7.0 %copy-start.3 = (f32[8,128,128]{2,1,0:T(8,128)S(1)}, f32[8,128,128]{2,1,0:T(8,128)}, u32[]{:S(2)}) copy-start(f32[8,128,128]{2,1,0:T(8,128)} %copy-done.2) | copy-start | bytes 1572868
  87.3 7.0 %copy-start.10 = (f32[128]{0:T(128)S(1)}, f32[128]{0:T(128)}, u32[]{:S(2)}) copy-start(f32[128]{0:T(128)} %param.17) | copy-start | bytes 1540
  94.3 1.0 copy-start.5
  95.4 1.0 copy-start.7
  96.4 1.0 copy-start.9
  97.5 0.7 copy-start.11

commit v6 on v5

--- a/solution.py
+++ b/solution.py
@@ -61,21 +61,28 @@
     return high, (value - high.astype(jnp.float32)).astype(jnp.bfloat16)
 
 
-def conv_chunk(read, weights, rows):
-    highs, lows = [], []
-    for a in range(3):
-        high, low = split(read(a).reshape(rows * WIDE, C))
-        highs.append(high)
-        lows.append(low)
-    left = jnp.concatenate(highs + lows, axis=1)
-    near = jnp.dot(left, weights[:, : 4 * C], preferred_element_type=jnp.float32)
-    far = jnp.dot(left[:, : 4 * C], weights[: 4 * C, 4 * C :], preferred_element_type=jnp.float32)
-    sums = [
-        (near[:, :C] + near[:, 3 * C :]).reshape(rows, WIDE, C),
-        (near[:, C : 2 * C] + far[:, :C]).reshape(rows, WIDE, C),
-        (near[:, 2 * C : 3 * C] + far[:, C:]).reshape(rows, WIDE, C),
-    ]
-    return pltpu.roll(sums[0], 1, 1) + sums[1] + pltpu.roll(sums[2], WIDE - 1, 1)
+def conv_chunk(cells, weights, rows):
+    half = rows // 2
+    paired = cells.reshape(half + 1, 2, WIDE, C)
+    d0, d1, d2, d3 = paired[:half, 0], paired[:half, 1], paired[1:, 0], paired[1:, 1]
+    parts = []
+    for q, plane in enumerate((d0 - d2, d1 + d2, d2 - d1, d1 - d3)):
+        left = jnp.concatenate(split(plane.reshape(half * WIDE, C)), axis=1)
+        sums = jnp.dot(
+            left, weights[q * 2 * C : (q + 1) * 2 * C], preferred_element_type=jnp.float32
+        )
+        parts.append((sums[:, : 3 * C] + sums[:, 3 * C :]).reshape(half, WIDE, 3 * C))
+    m1, m2, m3, m4 = parts
+
+    def join(sums):
+        return (
+            pltpu.roll(sums[:, :, :C], 1, 1)
+            + sums[:, :, C : 2 * C]
+            + pltpu.roll(sums[:, :, 2 * C :], WIDE - 1, 1)
+        )
+
+    pair = [join(m1 + m2 + m3)[:, None], join(m2 - m3 - m4)[:, None]]
+    return jnp.concatenate(pair, axis=1).reshape(rows, WIDE, C)
 
 
 def rows_kernel(
@@ -189,6 +196,7 @@
 
 
 def prepare_kernel(
+    me,
     taps,
     code,
     syndromes,
@@ -202,15 +210,18 @@
     turned,
 ):
     f32 = jnp.float32
-    for a in range(3):
-        for b in range(3):
-            high, low = split(taps[3 * a + b])
+    for b in range(3):
+        g0, g1, g2 = taps[b], taps[3 + b], taps[6 + b]
+        mixed = (g0, (g0 + g1 + g2) * 0.5, (g0 - g1 + g2) * 0.5, g2)
+        for q in range(4):
+            high, low = split(mixed[q])
+            top, mid, end = 2 * q * C, (2 * q + 1) * C, (2 * q + 2) * C
             cols = slice(b * C, (b + 1) * C)
             lows = slice((3 + b) * C, (4 + b) * C)
-            weights_out[a * C : (a + 1) * C, cols] = high
-            weights_out[a * C : (a + 1) * C, lows] = low
-            weights_out[(3 + a) * C : (4 + a) * C, cols] = high
-            weights_out[(3 + a) * C : (4 + a) * C, lows] = jnp.zeros((C, C), jnp.bfloat16)
+            weights_out[top:mid, cols] = high
+            weights_out[top:mid, lows] = low
+            weights_out[mid:end, cols] = high
+            weights_out[mid:end, lows] = jnp.zeros((C, C), jnp.bfloat16)
     codes[...] = jnp.zeros((C, C), f32)
     codes[:TALL, :TC] = code[...]
     second = repeat_blocks(erased[1].astype(f32), TR)
@@ -289,7 +300,7 @@
     def step(i, carry):
         start = i * rows
         pre_out[pl.ds(start, rows)] += conv_chunk(
-            lambda a: ext_out[pl.ds(start + 1 + a, rows)], weights[...], rows
+            ext_out[pl.ds(start + 1, rows + 2)], weights, rows
         )
         return carry
 
@@ -402,13 +413,11 @@
     lax.fori_loop(0, TR // BS // 4, read_second, 0)
     later[2].wait()
     later[3].wait()
-    rows = 8
+    rows = 16
 
     def finish(i, carry):
         start = i * rows
-        sums = conv_chunk(
-            lambda a: field[pl.ds(start + a, rows)], weights[...], rows
-        )[:, :TC]
+        sums = conv_chunk(field[pl.ds(start, rows + 2)], weights, rows)[:, :TC]
         for half in range(rows // BS):
             at = start + half * BS
             out[pl.ds(at, BS)] = 0.5 * field[pl.ds(at + 1, BS), :TC] + jnp.tanh(
@@ -489,11 +498,11 @@
         prepare_kernel,
         name="prepare",
         compiler_params=pltpu.CompilerParams(vmem_limit_bytes=60 * 2**20),
-        out_shape=(shape(TR + 2, TC, C), shape(TR, TC, C), shape(6 * C, 6 * C, dtype=jnp.bfloat16)),
-        in_specs=[vmem] * 6,
+        out_shape=(shape(TR + 2, TC, C), shape(TR, TC, C), shape(8 * C, 6 * C, dtype=jnp.bfloat16)),
+        in_specs=[smem] + [vmem] * 6,
         out_specs=(vmem,) * 3,
         scratch_shapes=[pltpu.VMEM((C, C), f32), pltpu.VMEM((C, C), f32)],
-    )(conv_weight, code, syndromes, erased, syndrome_table, lost_vector)
+    )(me, conv_weight, code, syndromes, erased, syndrome_table, lost_vector)
 
     ext, pre, slots = pl.pallas_call(
         first_kernel,
@@ -523,7 +532,7 @@
             pltpu.VMEM((TALL, WIDE, C), f32),
             pltpu.VMEM((CONV_ROWS, WIDE, C), f32),
             pltpu.VMEM((TR, TC, C), f32),
-            pltpu.VMEM((6 * C, 6 * C), jnp.bfloat16),
+            pltpu.VMEM((8 * C, 6 * C), jnp.bfloat16),
             pltpu.SemaphoreType.DMA((4,)),
         ],
         cost_estimate=pl.CostEstimate(

time: 111 us -> 110 us (level)
  no operation moved by 1% of the time
where the time goes in v6:
time: 110 us; the launch traced here: 109 us
  waiting for transfers between devices  39.2 us (36%)
  starting transfers between devices  34.1 us (31%)
  Pallas kernels  27.2 us (25%)
  local copies, waits for them, and re-layouts  7.97 us (7%)
    ppermute x1, waiting for transfers between devices, decode(): bottom = lax.ppermute(up_pay, 'gx', up)  12.5 us
    all_to_all x1, waiting for transfers between devices, gather_weights(): lax.all_to_all(copies, AX, 0, 0, tiled=True, axis_index_groups=class_grou...  11.5 us
    pallas_call x1, Pallas kernels, decode(): pl.pallas_call(second_kernel, name='read_and_finish', compiler_params=plt...  11.4 us
    all_to_all x1, starting transfers between devices, gather_weights(): lax.all_to_all(copies, AX, 0, 0, tiled=True, axis_index_groups=class_grou...  9.28 us
    ppermute x3, waiting for transfers between devices, gather_weights(): pieces.append(lax.ppermute(low, AX, moved(*step)))  8.22 us
    unnamed x36, local copies, waits for them, and re-layouts  6.89 us
    pallas_call x1, Pallas kernels, decode(): pl.pallas_call(first_kernel, name='conv_first', compiler_params=pltpu.Com...  6.49 us
    ppermute x1, starting transfers between devices, decode(): right = lax.ppermute(west_pay, 'gy', west)  5.97 us
  transfers between devices with their start and end apart: 18, of which 5 were waited for; matrix products, arithmetic and copies ran while one was open for 2% of the time, Pallas kernels for 12%

profile of v6, /device:TPU:27, one launch (start us, length us, event | category | flops | bytes accessed | tf_op | source)
XLA Modules:
  0.0 109.4 jit_solution(10301307075949488869)
XLA Ops:
  0.0 3.0 %pack_rows.1 = (f32[5,64,128]{2,1,0:T(8,128)}, f32[5,64,128]{2,1,0:T(8,128)}, f32[16,128,128]{2,1,0:T(8,128)}) custom-call(f32[32,64,128]{2,1,0:T(8,128)} %state.5, f32[128,128]{1,0:T(8,128)} %weight.1, s32[2,32,64]{2,1,0:T(8,128)} %syndromes.5, s32[2,8,16]{2,1,0:T(8,128)} %erased.7, s32[1,128]{1,0:T(1,128)} %bitcast.6), custom_call_target="tpu_custom_call" | custom-call | tf_op jit(solution)/shard_map/pack_rows/pallas_call | solution.py:458
  3.0 0.0 copy-start.17
  3.1 9.3 %all-to-all-start = ((f32[16,128,128]{2,1,0:T(8,128)}), f32[16,128,128]{2,1,0:T(8,128)S(1)}, u32[]{:S(2)}, u32[]{:S(2)}) async-start(f32[16,128,128]{2,1,0:T(8,128)} %get-tuple-element.32), calls=%async_computation | async-start | bytes 2097152 | tf_op jit(solution)/shard_map/all_to_all | solution.py:48
  12.3 0.0 copy-done.17
  12.3 4.1 %collective-permute-start = (f32[5,64,128]{2,1,0:T(8,128)S(1)}, f32[5,64,128]{2,1,0:T(8,128)S(1)}, u32[]{:S(2)}, u32[]{:S(2)}) collective-permute-start(f32[5,64,128]{2,1,0:T(8,128)S(1)} %copy-done.17), channel_id=1, source_target_pairs={{0,8},{8,16},{16,24},{24,32},{32,40},{40,48},{48,56},{56,64},{64,7... | collective-permute-start | bytes 491528 | tf_op jit(solution)/shard_map/ppermute | solution.py:473
  16.4 11.5 %all-to-all-done.rest_0_ = f32[16,128,128]{2,1,0:T(8,128)S(1)} async-done(((f32[16,128,128]{2,1,0:T(8,128)}), f32[16,128,128]{2,1,0:T(8,128)S(1)}, u32[]{:S(2)}, u32[]{:S(2)}) %all-to-all-start) | async-done | bytes 1048608 | tf_op jit(solution)/shard_map/all_to_all | solution.py:48
  27.9 1.1 fusion
  29.0 1.0 collective-permute-start.4
  30.0 0.4 collective-permute-start.5
  30.5 2.1 %collective-permute-start.6 = (f32[8,128,128]{2,1,0:T(8,128)}, f32[8,128,128]{2,1,0:T(8,128)}, u32[]{:S(2)}, u32[]{:S(2)}) collective-permute-start(f32[8,128,128]{2,1,0:T(8,128)} %get-tuple-element.34), channel_id=1, source_target_pairs={{0,8},{1,9},{2,10},{3,11},{4,12},{5,13},{6,14},{7,15},{8,16},{9,17... | collective-permute-start | bytes 1572872 | tf_op jit(solution)/shard_map/ppermute | solution.py:53
  32.6 0.0 collective-permute-start.7
  32.6 0.0 collective-permute-done.top
  32.6 0.0 copy-done.16
  32.6 1.9 %collective-permute-start.1 = (f32[5,64,128]{2,1,0:T(8,128)S(1)}, f32[5,64,128]{2,1,0:T(8,128)S(1)}, u32[]{:S(2)}, u32[]{:S(2)}) collective-permute-start(f32[5,64,128]{2,1,0:T(8,128)S(1)} %copy-done.16), channel_id=1, source_target_pairs={{8,0},{16,8},{24,16},{32,24},{40,32},{48,40},{56,48},{64,56},{72,6... | collective-permute-start | bytes 491528 | tf_op jit(solution)/shard_map/ppermute | solution.py:474
  34.5 12.5 %collective-permute-done.1.bottom = f32[5,64,128]{2,1,0:T(8,128)S(1)} collective-permute-done((f32[5,64,128]{2,1,0:T(8,128)S(1)}, f32[5,64,128]{2,1,0:T(8,128)S(1)}, u32[]{:S(2)}, u32[]{:S(2)}) %collective-permute-start.1) | collective-permute-done | bytes 163872 | tf_op jit(solution)/shard_map/ppermute | solution.py:474
  47.0 0.0 copy-done.12
  47.0 0.7 copy-done.13
  47.7 2.5 %pack_cols.1 = (f32[40,8,128]{2,1,0:T(8,128)}, f32[40,8,128]{2,1,0:T(8,128)}, f32[40,64]{1,0:T(8,128)}, f32[16,128]{1,0:T(8,128)}, f32[16,128]{1,0:T(8,128)}) custom-call(f32[32,64,128]{2,1,0:T(8,128)} %state.5, f32[5,64,128]{2,1,0:T(8,128)} %copy-done.12, f32[5,64,128]{2,1,0:T(8,128)} %copy-done.13, s32[2,32,64]{2,1,0:T(8,128)} %syndromes.5, ...), custom_call_target="tpu_custom_call" | custom-call | tf_op jit(solution)/shard_map/pack_cols/pallas_call | solution.py:476
  50.1 6.0 %collective-permute-start.2 = (f32[40,8,128]{2,1,0:T(8,128)}, f32[40,8,128]{2,1,0:T(8,128)S(1)}, u32[]{:S(2)}, u32[]{:S(2)}) collective-permute-start(f32[40,8,128]{2,1,0:T(8,128)} %get-tuple-element.21), channel_id=1, source_target_pairs={{1,0},{2,1},{3,2},{4,3},{5,4},{6,5},{7,6},{9,8},{10,9},{11,10},{12... | collective-permute-start | bytes 491528 | tf_op jit(solution)/shard_map/ppermute | solution.py:494
  56.1 4.5 %collective-permute-done.2.right = f32[40,8,128]{2,1,0:T(8,128)S(1)} collective-permute-done((f32[40,8,128]{2,1,0:T(8,128)}, f32[40,8,128]{2,1,0:T(8,128)S(1)}, u32[]{:S(2)}, u32[]{:S(2)}) %collective-permute-start.2) | collective-permute-done | bytes 163872 | tf_op jit(solution)/shard_map/ppermute | solution.py:494
  60.6 1.9 %collective-permute-start.3 = (f32[40,8,128]{2,1,0:T(8,128)}, f32[40,8,128]{2,1,0:T(8,128)S(1)}, u32[]{:S(2)}, u32[]{:S(2)}) collective-permute-start(f32[40,8,128]{2,1,0:T(8,128)} %get-tuple-element.22), channel_id=1, source_target_pairs={{0,1},{1,2},{2,3},{3,4},{4,5},{5,6},{6,7},{8,9},{9,10},{10,11},{11... | collective-permute-start | bytes 491528 | tf_op jit(solution)/shard_map/ppermute | solution.py:493
  62.5 2.6 %collective-permute-done.3.left = f32[40,8,128]{2,1,0:T(8,128)S(1)} collective-permute-done((f32[40,8,128]{2,1,0:T(8,128)}, f32[40,8,128]{2,1,0:T(8,128)S(1)}, u32[]{:S(2)}, u32[]{:S(2)}) %collective-permute-start.3) | collective-permute-done | bytes 163872 | tf_op jit(solution)/shard_map/ppermute | solution.py:493
  65.0 0.8 collective-permute-start.8
  65.8 0.0 collective-permute-done.4.rest_1_
  65.8 1.9 %collective-permute-start.9 = (f32[8,128,128]{2,1,0:T(8,128)}, f32[8,128,128]{2,1,0:T(8,128)}, u32[]{:S(2)}, u32[]{:S(2)}) collective-permute-start(f32[8,128,128]{2,1,0:T(8,128)} %get-tuple-element.33), channel_id=1, source_target_pairs={{0,96},{1,97},{2,98},{3,99},{4,100},{5,101},{6,102},{7,103},{8,104... | collective-permute-start | bytes 1572872 | tf_op jit(solution)/shard_map/ppermute | solution.py:54
  67.7 0.0 collective-permute-done.5.rest_2_
  67.7 1.7 %collective-permute-start.11 = (f32[8,128,128]{2,1,0:T(8,128)S(1)}, f32[8,128,128]{2,1,0:T(8,128)S(1)}, u32[]{:S(2)}, u32[]{:S(2)}) collective-permute-start(f32[8,128,128]{2,1,0:T(8,128)S(1)} %collective-permute-done.4.rest_1_), channel_id=1, source_target_pairs={{0,1},{1,0},{2,3},{3,2},{4,5},{5,4},{6,7},{7,6},{8,9},{9,8},{10,11... | collective-permute-start | bytes 1572872 | tf_op jit(solution)/shard_map/ppermute | solution.py:55
  69.4 0.0 collective-permute-done.6.rest_3_
  69.4 0.1 collective-permute-start.12
  69.5 0.8 copy-done.3
  70.3 0.0 collective-permute-done.7.rest_4_
  70.3 0.4 collective-permute-start.10
  70.7 8.2 %collective-permute-done.8.rest_5_ = f32[8,128,128]{2,1,0:T(8,128)} collective-permute-done((f32[8,128,128]{2,1,0:T(8,128)}, f32[8,128,128]{2,1,0:T(8,128)}, u32[]{:S(2)}, u32[]{:S(2)}) %collective-permute-start.8) | collective-permute-done | bytes 524320 | tf_op jit(solution)/shard_map/ppermute | solution.py:53
  78.9 2.0 %collective-permute-start.13 = (f32[8,128,128]{2,1,0:T(8,128)}, f32[8,128,128]{2,1,0:T(8,128)}, u32[]{:S(2)}, u32[]{:S(2)}) collective-permute-start(f32[8,128,128]{2,1,0:T(8,128)} %collective-permute-done.6.rest_3_), channel_id=1, source_target_pairs={{0,1},{1,0},{2,3},{3,2},{4,5},{5,4},{6,7},{7,6},{8,9},{9,8},{10,11... | collective-permute-start | bytes 1572872 | tf_op jit(solution)/shard_map/ppermute | solution.py:55
  80.9 0.0 collective-permute-done.9.rest_6_
  80.9 0.0 collective-permute-start.14
  80.9 0.0 collective-permute-done.11.rest_8_
  80.9 0.0 copy-start.5
  80.9 0.8 copy-done.5
  81.7 0.5 collective-permute-start.15
  82.2 0.0 collective-permute-done.12.rest_9_
  82.2 0.8 copy-done.7
  83.0 0.0 collective-permute-start.16
  83.0 0.7 pad_add_fusion.me
  83.7 3.8 %prepare.1 = (f32[34,64,128]{2,1,0:T(8,128)}, f32[32,64,128]{2,1,0:T(8,128)}, bf16[1024,768]{1,0:T(8,128)(2,1)}) custom-call(s32[4]{0:T(128)} %pad_add_fusion.me, f32[9,128,128]{2,1,0:T(8,128)} %taps.1, f32[40,64]{1,0:T(8,128)} %get-tuple-element.23.code, s32[2,32,64]{2,1,0:T(8,128)} %syndromes.5, s32[2,8,16]{2,1,0:T(8,128)} %erased.7, f32[2,128]{1,0:T(2,128)} %table.3, ...), custom_call_target="tpu_custom_call" | custom-call | tf_op jit(solution)/shard_map/prepare/pallas_call | solution.py:497
  87.5 0.0 copy-done.1
  87.5 0.0 copy-done.14
  87.5 0.0 copy-done.15
  87.5 0.0 copy-start
  87.5 0.0 copy-start.2
  87.6 0.0 copy-start.10
  87.6 0.0 copy-start.11
  87.6 6.5 %conv_first.1 = (f32[40,72,128]{2,1,0:T(8,128)}, f32[36,72,128]{2,1,0:T(8,128)}, s32[16,128]{1,0:T(8,128)}) custom-call(s32[4]{0:T(128)} %pad_add_fusion.me, f32[32,64,128]{2,1,0:T(8,128)} %state.5, f32[5,64,128]{2,1,0:T(8,128)} %copy-done.12, f32[5,64,128]{2,1,0:T(8,128)} %copy-done.13, f32[40,8,128]{2,1,0:T(8,128)} %copy-done.14, ...), custom_call_target="tpu_custom_call" | custom-call | flops 2000000000 | bytes 6000000 | tf_op jit(solution)/shard_map/conv_first/pallas_call | solution.py:507
  94.1 0.0 collective-permute-done.13.rest_10_
  94.1 0.0 collective-permute-done.14.rest_11_
  94.1 0.0 collective-permute-done.15.rest_12_
  94.1 0.0 collective-permute-done.16.rest_13_
  94.1 0.0 collective-permute-done.10.rest_7_
  94.1 0.0 copy-done
  94.2 1.0 copy-done.4
  95.2 1.0 copy-done.6
  96.2 1.0 copy-done.8
  97.3 0.7 copy-done.9
  98.0 11.4 %read_and_finish.1 = f32[32,64,128]{2,1,0:T(8,128)} custom-call(s32[16,128]{1,0:T(8,128)S(1)} %copy-done.9, s32[4]{0:T(128)S(1)} %copy-done.10, f32[1,128]{1,0:T(1,128)S(1)} %bitcast.5, f32[40,72,128]{2,1,0:T(8,128)} %get-tuple-element.29.ext_hbm, f32[36,72,128]{2,1,0:T(8,128)} %get-tuple-element.30.pre_hbm, f32[32,64,128]{2,1,0:T(8,128)S(1)} %copy-done, ...), custom_call_target="tpu_custom_call" | custom-call | flops 4000000000 | bytes 12000000 | tf_op jit(solution)/shard_map/read_and_finish/pallas_call | solution.py:520
  (15 shorter events, 0.0 us)
Async XLA Ops:
  3.0 9.3 %copy-start.17 = (f32[5,64,128]{2,1,0:T(8,128)S(1)}, f32[5,64,128]{2,1,0:T(8,128)}, u32[]{:S(2)}) copy-start(f32[5,64,128]{2,1,0:T(8,128)} %get-tuple-element.19) | copy-start | bytes 491524
  3.1 24.9 %all-to-all-start = ((f32[16,128,128]{2,1,0:T(8,128)}), f32[16,128,128]{2,1,0:T(8,128)S(1)}, u32[]{:S(2)}, u32[]{:S(2)}) async-start(f32[16,128,128]{2,1,0:T(8,128)} %get-tuple-element.32), calls=%async_computation | async-start | bytes 2097152 | tf_op jit(solution)/shard_map/all_to_all | solution.py:48
  12.3 20.3 %copy-start.16 = (f32[5,64,128]{2,1,0:T(8,128)S(1)}, f32[5,64,128]{2,1,0:T(8,128)}, u32[]{:S(2)}) copy-start(f32[5,64,128]{2,1,0:T(8,128)} %get-tuple-element.20) | copy-start | bytes 491524
  12.3 20.3 %collective-permute-start = (f32[5,64,128]{2,1,0:T(8,128)S(1)}, f32[5,64,128]{2,1,0:T(8,128)S(1)}, u32[]{:S(2)}, u32[]{:S(2)}) collective-permute-start(f32[5,64,128]{2,1,0:T(8,128)S(1)} %copy-done.17), channel_id=1, source_target_pairs={{0,8},{8,16},{16,24},{24,32},{32,40},{40,48},{48,56},{56,64},{64,7... | collective-permute-start | bytes 491528 | tf_op jit(solution)/shard_map/ppermute | solution.py:473
  29.0 36.8 %collective-permute-start.4 = (f32[8,128,128]{2,1,0:T(8,128)}, f32[8,128,128]{2,1,0:T(8,128)S(1)}, u32[]{:S(2)}, u32[]{:S(2)}) collective-permute-start(f32[8,128,128]{2,1,0:T(8,128)} %get-tuple-element.34), channel_id=1, source_target_pairs={{0,2},{1,3},{2,4},{3,5},{4,6},{5,7},{6,0},{7,1},{8,10},{9,11},{10,... | collective-permute-start | bytes 1572872 | tf_op jit(solution)/shard_map/ppermute | solution.py:53
  30.0 37.7 %collective-permute-start.5 = (f32[8,128,128]{2,1,0:T(8,128)}, f32[8,128,128]{2,1,0:T(8,128)S(1)}, u32[]{:S(2)}, u32[]{:S(2)}) collective-permute-start(f32[8,128,128]{2,1,0:T(8,128)} %get-tuple-element.33), channel_id=1, source_target_pairs={{0,6},{1,7},{2,0},{3,1},{4,2},{5,3},{6,4},{7,5},{8,14},{9,15},{10,... | collective-permute-start | bytes 1572872 | tf_op jit(solution)/shard_map/ppermute | solution.py:54
  30.5 38.9 %collective-permute-start.6 = (f32[8,128,128]{2,1,0:T(8,128)}, f32[8,128,128]{2,1,0:T(8,128)}, u32[]{:S(2)}, u32[]{:S(2)}) collective-permute-start(f32[8,128,128]{2,1,0:T(8,128)} %get-tuple-element.34), channel_id=1, source_target_pairs={{0,8},{1,9},{2,10},{3,11},{4,12},{5,13},{6,14},{7,15},{8,16},{9,17... | collective-permute-start | bytes 1572872 | tf_op jit(solution)/shard_map/ppermute | solution.py:53
  32.6 37.7 %collective-permute-start.7 = (f32[8,128,128]{2,1,0:T(8,128)}, f32[8,128,128]{2,1,0:T(8,128)}, u32[]{:S(2)}, u32[]{:S(2)}) collective-permute-start(f32[8,128,128]{2,1,0:T(8,128)} %get-tuple-element.33), channel_id=1, source_target_pairs={{0,24},{1,25},{2,26},{3,27},{4,28},{5,29},{6,30},{7,31},{8,0},{9,1... | collective-permute-start | bytes 1572872 | tf_op jit(solution)/shard_map/ppermute | solution.py:54
  32.6 14.4 %copy-start.12 = (f32[5,64,128]{2,1,0:T(8,128)}, f32[5,64,128]{2,1,0:T(8,128)S(1)}, u32[]{:S(2)}) copy-start(f32[5,64,128]{2,1,0:T(8,128)S(1)} %collective-permute-done.top) | copy-start | bytes 491524
  32.6 14.4 %collective-permute-start.1 = (f32[5,64,128]{2,1,0:T(8,128)S(1)}, f32[5,64,128]{2,1,0:T(8,128)S(1)}, u32[]{:S(2)}, u32[]{:S(2)}) collective-permute-start(f32[5,64,128]{2,1,0:T(8,128)S(1)} %copy-done.16), channel_id=1, source_target_pairs={{8,0},{16,8},{24,16},{32,24},{40,32},{48,40},{56,48},{64,56},{72,6... | collective-permute-start | bytes 491528 | tf_op jit(solution)/shard_map/ppermute | solution.py:474
  47.0 0.7 copy-start.13
  50.1 10.4 %collective-permute-start.2 = (f32[40,8,128]{2,1,0:T(8,128)}, f32[40,8,128]{2,1,0:T(8,128)S(1)}, u32[]{:S(2)}, u32[]{:S(2)}) collective-permute-start(f32[40,8,128]{2,1,0:T(8,128)} %get-tuple-element.21), channel_id=1, source_target_pairs={{1,0},{2,1},{3,2},{4,3},{5,4},{6,5},{7,6},{9,8},{10,9},{11,10},{12... | collective-permute-start | bytes 491528 | tf_op jit(solution)/shard_map/ppermute | solution.py:494
  60.6 27.0 %copy-start.14 = (f32[40,8,128]{2,1,0:T(8,128)}, f32[40,8,128]{2,1,0:T(8,128)S(1)}, u32[]{:S(2)}) copy-start(f32[40,8,128]{2,1,0:T(8,128)S(1)} %collective-permute-done.2.right) | copy-start | bytes 491524
  60.6 4.5 %collective-permute-start.3 = (f32[40,8,128]{2,1,0:T(8,128)}, f32[40,8,128]{2,1,0:T(8,128)S(1)}, u32[]{:S(2)}, u32[]{:S(2)}) collective-permute-start(f32[40,8,128]{2,1,0:T(8,128)} %get-tuple-element.22), channel_id=1, source_target_pairs={{0,1},{1,2},{2,3},{3,4},{4,5},{5,6},{6,7},{8,9},{9,10},{10,11},{11... | collective-permute-start | bytes 491528 | tf_op jit(solution)/shard_map/ppermute | solution.py:493
  65.0 22.5 %copy-start.15 = (f32[40,8,128]{2,1,0:T(8,128)}, f32[40,8,128]{2,1,0:T(8,128)S(1)}, u32[]{:S(2)}) copy-start(f32[40,8,128]{2,1,0:T(8,128)S(1)} %collective-permute-done.3.left) | copy-start | bytes 491524
  65.0 13.9 %collective-permute-start.8 = (f32[8,128,128]{2,1,0:T(8,128)}, f32[8,128,128]{2,1,0:T(8,128)}, u32[]{:S(2)}, u32[]{:S(2)}) collective-permute-start(f32[8,128,128]{2,1,0:T(8,128)} %get-tuple-element.34), channel_id=1, source_target_pairs={{0,32},{1,33},{2,34},{3,35},{4,36},{5,37},{6,38},{7,39},{8,40},{9,... | collective-permute-start | bytes 1572872 | tf_op jit(solution)/shard_map/ppermute | solution.py:53
  65.8 21.7 %copy-start.1 = (f32[8,128,128]{2,1,0:T(8,128)}, f32[8,128,128]{2,1,0:T(8,128)S(1)}, u32[]{:S(2)}) copy-start(f32[8,128,128]{2,1,0:T(8,128)S(1)} %collective-permute-done.4.rest_1_) | copy-start | bytes 1572868
  65.8 15.1 %collective-permute-start.9 = (f32[8,128,128]{2,1,0:T(8,128)}, f32[8,128,128]{2,1,0:T(8,128)}, u32[]{:S(2)}, u32[]{:S(2)}) collective-permute-start(f32[8,128,128]{2,1,0:T(8,128)} %get-tuple-element.33), channel_id=1, source_target_pairs={{0,96},{1,97},{2,98},{3,99},{4,100},{5,101},{6,102},{7,103},{8,104... | collective-permute-start | bytes 1572872 | tf_op jit(solution)/shard_map/ppermute | solution.py:54
  67.7 13.2 %collective-permute-start.11 = (f32[8,128,128]{2,1,0:T(8,128)S(1)}, f32[8,128,128]{2,1,0:T(8,128)S(1)}, u32[]{:S(2)}, u32[]{:S(2)}) collective-permute-start(f32[8,128,128]{2,1,0:T(8,128)S(1)} %collective-permute-done.4.rest_1_), channel_id=1, source_target_pairs={{0,1},{1,0},{2,3},{3,2},{4,5},{5,4},{6,7},{7,6},{8,9},{9,8},{10,11... | collective-permute-start | bytes 1572872 | tf_op jit(solution)/shard_map/ppermute | solution.py:55
  69.4 12.8 %collective-permute-start.12 = (f32[8,128,128]{2,1,0:T(8,128)S(1)}, f32[8,128,128]{2,1,0:T(8,128)S(1)}, u32[]{:S(2)}, u32[]{:S(2)}) collective-permute-start(f32[8,128,128]{2,1,0:T(8,128)S(1)} %collective-permute-done.5.rest_2_), channel_id=1, source_target_pairs={{0,1},{1,0},{2,3},{3,2},{4,5},{5,4},{6,7},{7,6},{8,9},{9,8},{10,11... | collective-permute-start | bytes 1572872 | tf_op jit(solution)/shard_map/ppermute | solution.py:55
  69.5 0.8 copy-start.3
  70.3 23.8 %collective-permute-start.10 = (f32[16,128,128]{2,1,0:T(8,128)S(1)}, f32[16,128,128]{2,1,0:T(8,128)S(1)}, u32[]{:S(2)}, u32[]{:S(2)}) collective-permute-start(f32[16,128,128]{2,1,0:T(8,128)S(1)} %all-to-all-done.rest_0_), channel_id=1, source_target_pairs={{0,1},{1,0},{2,3},{3,2},{4,5},{5,4},{6,7},{7,6},{8,9},{9,8},{10,11... | collective-permute-start | bytes 3145736 | tf_op jit(solution)/shard_map/ppermute | solution.py:55
  78.9 15.1 %collective-permute-start.13 = (f32[8,128,128]{2,1,0:T(8,128)}, f32[8,128,128]{2,1,0:T(8,128)}, u32[]{:S(2)}, u32[]{:S(2)}) collective-permute-start(f32[8,128,128]{2,1,0:T(8,128)} %collective-permute-done.6.rest_3_), channel_id=1, source_target_pairs={{0,1},{1,0},{2,3},{3,2},{4,5},{5,4},{6,7},{7,6},{8,9},{9,8},{10,11... | collective-permute-start | bytes 1572872 | tf_op jit(solution)/shard_map/ppermute | solution.py:55
  80.9 13.2 %collective-permute-start.14 = (f32[8,128,128]{2,1,0:T(8,128)}, f32[8,128,128]{2,1,0:T(8,128)}, u32[]{:S(2)}, u32[]{:S(2)}) collective-permute-start(f32[8,128,128]{2,1,0:T(8,128)} %collective-permute-done.7.rest_4_), channel_id=1, source_target_pairs={{0,1},{1,0},{2,3},{3,2},{4,5},{5,4},{6,7},{7,6},{8,9},{9,8},{10,11... | collective-permute-start | bytes 1572872 | tf_op jit(solution)/shard_map/ppermute | solution.py:55
  80.9 0.8 copy-start.5
  81.7 12.4 %collective-permute-start.15 = (f32[8,128,128]{2,1,0:T(8,128)}, f32[8,128,128]{2,1,0:T(8,128)}, u32[]{:S(2)}, u32[]{:S(2)}) collective-permute-start(f32[8,128,128]{2,1,0:T(8,128)} %collective-permute-done.8.rest_5_), channel_id=1, source_target_pairs={{0,1},{1,0},{2,3},{3,2},{4,5},{5,4},{6,7},{7,6},{8,9},{9,8},{10,11... | collective-permute-start | bytes 1572872 | tf_op jit(solution)/shard_map/ppermute | solution.py:55
  82.2 0.8 copy-start.7
  83.0 11.1 %collective-permute-start.16 = (f32[8,128,128]{2,1,0:T(8,128)}, f32[8,128,128]{2,1,0:T(8,128)}, u32[]{:S(2)}, u32[]{:S(2)}) collective-permute-start(f32[8,128,128]{2,1,0:T(8,128)} %collective-permute-done.9.rest_6_), channel_id=1, source_target_pairs={{0,1},{1,0},{2,3},{3,2},{4,5},{5,4},{6,7},{7,6},{8,9},{9,8},{10,11... | collective-permute-start | bytes 1572872 | tf_op jit(solution)/shard_map/ppermute | solution.py:55
  87.5 6.6 %copy-start = (f32[32,64,128]{2,1,0:T(8,128)S(1)}, f32[32,64,128]{2,1,0:T(8,128)}, u32[]{:S(2)}) copy-start(f32[32,64,128]{2,1,0:T(8,128)} %get-tuple-element.31.inputs_hbm) | copy-start | bytes 3145732
  87.5 6.6 %copy-start.2 = (f32[8,128,128]{2,1,0:T(8,128)S(1)}, f32[8,128,128]{2,1,0:T(8,128)}, u32[]{:S(2)}) copy-start(f32[8,128,128]{2,1,0:T(8,128)} %copy-done.1) | copy-start | bytes 1572868
  87.6 6.6 %copy-start.10 = (s32[4]{0:T(128)S(1)}, s32[4]{0:T(128)}, u32[]{:S(2)}) copy-start(s32[4]{0:T(128)} %pad_add_fusion.me) | copy-start | bytes 52
  87.6 6.6 %copy-start.11 = (f32[128]{0:T(128)S(1)}, f32[128]{0:T(128)}, u32[]{:S(2)}) copy-start(f32[128]{0:T(128)} %param.17) | copy-start | bytes 1540
  94.1 1.0 copy-start.4
  95.2 1.0 copy-start.6
  96.2 1.0 copy-start.8
  97.3 0.7 copy-start.9

commit v7 on v6

--- a/solution.py
+++ b/solution.py
@@ -295,7 +295,7 @@
             pltpu.roll(right[r], 4, 0),
             jnp.where(sub == 7, pltpu.roll(left[r], 4, 0), 0.0),
         )
-    rows = 12
+    rows = CONV_ROWS
 
     def step(i, carry):
         start = i * rows
@@ -361,7 +361,7 @@
     shift = offset[...]
 
     def read_first(step, carry):
-        for br, g in [(5 * step + k, g) for k in range(5) for g in range(GROUPS)]:
+        for br, g in [(10 * step + k, g) for k in range(10) for g in range(GROUPS)]:
             one, two = slots[br, 2 * g], slots[br, 2 * g + 1]
             first[br, 8 * g : 8 * g + 8] = readout(
                 ext[pl.ds(br * BS, BS), 8 * g : 8 * g + 8],
@@ -373,7 +373,7 @@
             )
         return carry
 
-    lax.fori_loop(0, BROWS // 5, read_first, 0)
+    read_first(0, 0)
 
     later[1].wait()
 
@@ -398,7 +398,7 @@
     field[:, TC:] = field[:, TC:] * kept
 
     def read_second(step, carry):
-        for br, g in [(4 * step + k, g) for k in range(4) for g in range(TC // 8)]:
+        for br, g in [(8 * step + k, g) for k in range(8) for g in range(TC // 8)]:
             one, two = slots[br + 1, 2 * g], slots[br + 1, 2 * g + 1]
             second[br, 8 * g : 8 * g + 8] = readout(
                 field[pl.ds(br * BS + 1, BS), 8 * g : 8 * g + 8],
@@ -410,10 +410,10 @@
             )
         return carry
 
-    lax.fori_loop(0, TR // BS // 4, read_second, 0)
+    read_second(0, 0)
     later[2].wait()
     later[3].wait()
-    rows = 16
+    rows = TR
 
     def finish(i, carry):
         start = i * rows

time: 110 us -> 109 us (level)
  no operation moved by 1% of the time
where the time goes in v7:
time: 109 us
  waiting for transfers between devices  39.2 us (36%)
  starting transfers between devices  34.1 us (31%)
  Pallas kernels  26.4 us (24%)
  local copies, waits for them, and re-layouts  7.97 us (7%)
    ppermute x1, waiting for transfers between devices, decode(): bottom = lax.ppermute(up_pay, 'gx', up)  12.5 us
    all_to_all x1, waiting for transfers between devices, gather_weights(): lax.all_to_all(copies, AX, 0, 0, tiled=True, axis_index_groups=class_grou...  11.5 us
    pallas_call x1, Pallas kernels, decode(): pl.pallas_call(second_kernel, name='read_and_finish', compiler_params=plt...  10.8 us
    all_to_all x1, starting transfers between devices, gather_weights(): lax.all_to_all(copies, AX, 0, 0, tiled=True, axis_index_groups=class_grou...  9.28 us
    ppermute x3, waiting for transfers between devices, gather_weights(): pieces.append(lax.ppermute(low, AX, moved(*step)))  8.22 us
    unnamed x36, local copies, waits for them, and re-layouts  6.89 us
    pallas_call x1, Pallas kernels, decode(): pl.pallas_call(first_kernel, name='conv_first', compiler_params=pltpu.Com...  6.31 us
    ppermute x1, starting transfers between devices, decode(): right = lax.ppermute(west_pay, 'gy', west)  5.97 us
  transfers between devices with their start and end apart: 18, of which 5 were waited for; matrix products, arithmetic and copies ran while one was open for 2% of the time, Pallas kernels for 12%

profile of v7, /device:TPU:27, one launch (start us, length us, event | category | flops | bytes accessed | tf_op | source)
XLA Modules:
  0.0 108.7 jit_solution(6525505833062061603)
XLA Ops:
  0.0 3.0 %pack_rows.1 = (f32[5,64,128]{2,1,0:T(8,128)}, f32[5,64,128]{2,1,0:T(8,128)}, f32[16,128,128]{2,1,0:T(8,128)}) custom-call(f32[32,64,128]{2,1,0:T(8,128)} %state.5, f32[128,128]{1,0:T(8,128)} %weight.1, s32[2,32,64]{2,1,0:T(8,128)} %syndromes.5, s32[2,8,16]{2,1,0:T(8,128)} %erased.7, s32[1,128]{1,0:T(1,128)} %bitcast.6), custom_call_target="tpu_custom_call" | custom-call | tf_op jit(solution)/shard_map/pack_rows/pallas_call | solution.py:458
  3.0 0.0 copy-start.17
  3.1 9.3 %all-to-all-start = ((f32[16,128,128]{2,1,0:T(8,128)}), f32[16,128,128]{2,1,0:T(8,128)S(1)}, u32[]{:S(2)}, u32[]{:S(2)}) async-start(f32[16,128,128]{2,1,0:T(8,128)} %get-tuple-element.32), calls=%async_computation | async-start | bytes 2097152 | tf_op jit(solution)/shard_map/all_to_all | solution.py:48
  12.3 0.0 copy-done.17
  12.3 4.1 %collective-permute-start = (f32[5,64,128]{2,1,0:T(8,128)S(1)}, f32[5,64,128]{2,1,0:T(8,128)S(1)}, u32[]{:S(2)}, u32[]{:S(2)}) collective-permute-start(f32[5,64,128]{2,1,0:T(8,128)S(1)} %copy-done.17), channel_id=1, source_target_pairs={{0,8},{8,16},{16,24},{24,32},{32,40},{40,48},{48,56},{56,64},{64,7... | collective-permute-start | bytes 491528 | tf_op jit(solution)/shard_map/ppermute | solution.py:473
  16.4 11.5 %all-to-all-done.rest_0_ = f32[16,128,128]{2,1,0:T(8,128)S(1)} async-done(((f32[16,128,128]{2,1,0:T(8,128)}), f32[16,128,128]{2,1,0:T(8,128)S(1)}, u32[]{:S(2)}, u32[]{:S(2)}) %all-to-all-start) | async-done | bytes 1048608 | tf_op jit(solution)/shard_map/all_to_all | solution.py:48
  27.9 1.1 fusion
  29.0 1.0 collective-permute-start.4
  30.0 0.4 collective-permute-start.5
  30.5 2.1 %collective-permute-start.6 = (f32[8,128,128]{2,1,0:T(8,128)}, f32[8,128,128]{2,1,0:T(8,128)}, u32[]{:S(2)}, u32[]{:S(2)}) collective-permute-start(f32[8,128,128]{2,1,0:T(8,128)} %get-tuple-element.34), channel_id=1, source_target_pairs={{0,8},{1,9},{2,10},{3,11},{4,12},{5,13},{6,14},{7,15},{8,16},{9,17... | collective-permute-start | bytes 1572872 | tf_op jit(solution)/shard_map/ppermute | solution.py:53
  32.6 0.0 collective-permute-start.7
  32.6 0.0 collective-permute-done.top
  32.6 0.0 copy-done.16
  32.6 1.9 %collective-permute-start.1 = (f32[5,64,128]{2,1,0:T(8,128)S(1)}, f32[5,64,128]{2,1,0:T(8,128)S(1)}, u32[]{:S(2)}, u32[]{:S(2)}) collective-permute-start(f32[5,64,128]{2,1,0:T(8,128)S(1)} %copy-done.16), channel_id=1, source_target_pairs={{8,0},{16,8},{24,16},{32,24},{40,32},{48,40},{56,48},{64,56},{72,6... | collective-permute-start | bytes 491528 | tf_op jit(solution)/shard_map/ppermute | solution.py:474
  34.5 12.5 %collective-permute-done.1.bottom = f32[5,64,128]{2,1,0:T(8,128)S(1)} collective-permute-done((f32[5,64,128]{2,1,0:T(8,128)S(1)}, f32[5,64,128]{2,1,0:T(8,128)S(1)}, u32[]{:S(2)}, u32[]{:S(2)}) %collective-permute-start.1) | collective-permute-done | bytes 163872 | tf_op jit(solution)/shard_map/ppermute | solution.py:474
  47.0 0.0 copy-done.12
  47.0 0.7 copy-done.13
  47.7 2.5 %pack_cols.1 = (f32[40,8,128]{2,1,0:T(8,128)}, f32[40,8,128]{2,1,0:T(8,128)}, f32[40,64]{1,0:T(8,128)}, f32[16,128]{1,0:T(8,128)}, f32[16,128]{1,0:T(8,128)}) custom-call(f32[32,64,128]{2,1,0:T(8,128)} %state.5, f32[5,64,128]{2,1,0:T(8,128)} %copy-done.12, f32[5,64,128]{2,1,0:T(8,128)} %copy-done.13, s32[2,32,64]{2,1,0:T(8,128)} %syndromes.5, ...), custom_call_target="tpu_custom_call" | custom-call | tf_op jit(solution)/shard_map/pack_cols/pallas_call | solution.py:476
  50.1 6.0 %collective-permute-start.2 = (f32[40,8,128]{2,1,0:T(8,128)}, f32[40,8,128]{2,1,0:T(8,128)S(1)}, u32[]{:S(2)}, u32[]{:S(2)}) collective-permute-start(f32[40,8,128]{2,1,0:T(8,128)} %get-tuple-element.21), channel_id=1, source_target_pairs={{1,0},{2,1},{3,2},{4,3},{5,4},{6,5},{7,6},{9,8},{10,9},{11,10},{12... | collective-permute-start | bytes 491528 | tf_op jit(solution)/shard_map/ppermute | solution.py:494
  56.1 4.5 %collective-permute-done.2.right = f32[40,8,128]{2,1,0:T(8,128)S(1)} collective-permute-done((f32[40,8,128]{2,1,0:T(8,128)}, f32[40,8,128]{2,1,0:T(8,128)S(1)}, u32[]{:S(2)}, u32[]{:S(2)}) %collective-permute-start.2) | collective-permute-done | bytes 163872 | tf_op jit(solution)/shard_map/ppermute | solution.py:494
  60.6 1.9 %collective-permute-start.3 = (f32[40,8,128]{2,1,0:T(8,128)}, f32[40,8,128]{2,1,0:T(8,128)S(1)}, u32[]{:S(2)}, u32[]{:S(2)}) collective-permute-start(f32[40,8,128]{2,1,0:T(8,128)} %get-tuple-element.22), channel_id=1, source_target_pairs={{0,1},{1,2},{2,3},{3,4},{4,5},{5,6},{6,7},{8,9},{9,10},{10,11},{11... | collective-permute-start | bytes 491528 | tf_op jit(solution)/shard_map/ppermute | solution.py:493
  62.5 2.6 %collective-permute-done.3.left = f32[40,8,128]{2,1,0:T(8,128)S(1)} collective-permute-done((f32[40,8,128]{2,1,0:T(8,128)}, f32[40,8,128]{2,1,0:T(8,128)S(1)}, u32[]{:S(2)}, u32[]{:S(2)}) %collective-permute-start.3) | collective-permute-done | bytes 163872 | tf_op jit(solution)/shard_map/ppermute | solution.py:493
  65.0 0.8 collective-permute-start.8
  65.8 0.0 collective-permute-done.4.rest_1_
  65.8 1.9 %collective-permute-start.9 = (f32[8,128,128]{2,1,0:T(8,128)}, f32[8,128,128]{2,1,0:T(8,128)}, u32[]{:S(2)}, u32[]{:S(2)}) collective-permute-start(f32[8,128,128]{2,1,0:T(8,128)} %get-tuple-element.33), channel_id=1, source_target_pairs={{0,96},{1,97},{2,98},{3,99},{4,100},{5,101},{6,102},{7,103},{8,104... | collective-permute-start | bytes 1572872 | tf_op jit(solution)/shard_map/ppermute | solution.py:54
  67.7 0.0 collective-permute-done.5.rest_2_
  67.7 1.7 %collective-permute-start.11 = (f32[8,128,128]{2,1,0:T(8,128)S(1)}, f32[8,128,128]{2,1,0:T(8,128)S(1)}, u32[]{:S(2)}, u32[]{:S(2)}) collective-permute-start(f32[8,128,128]{2,1,0:T(8,128)S(1)} %collective-permute-done.4.rest_1_), channel_id=1, source_target_pairs={{0,1},{1,0},{2,3},{3,2},{4,5},{5,4},{6,7},{7,6},{8,9},{9,8},{10,11... | collective-permute-start | bytes 1572872 | tf_op jit(solution)/shard_map/ppermute | solution.py:55
  69.4 0.0 collective-permute-done.6.rest_3_
  69.4 0.1 collective-permute-start.12
  69.5 0.8 copy-done.3
  70.3 0.0 collective-permute-done.7.rest_4_
  70.3 0.4 collective-permute-start.10
  70.7 8.2 %collective-permute-done.8.rest_5_ = f32[8,128,128]{2,1,0:T(8,128)} collective-permute-done((f32[8,128,128]{2,1,0:T(8,128)}, f32[8,128,128]{2,1,0:T(8,128)}, u32[]{:S(2)}, u32[]{:S(2)}) %collective-permute-start.8) | collective-permute-done | bytes 524320 | tf_op jit(solution)/shard_map/ppermute | solution.py:53
  78.9 2.0 %collective-permute-start.13 = (f32[8,128,128]{2,1,0:T(8,128)}, f32[8,128,128]{2,1,0:T(8,128)}, u32[]{:S(2)}, u32[]{:S(2)}) collective-permute-start(f32[8,128,128]{2,1,0:T(8,128)} %collective-permute-done.6.rest_3_), channel_id=1, source_target_pairs={{0,1},{1,0},{2,3},{3,2},{4,5},{5,4},{6,7},{7,6},{8,9},{9,8},{10,11... | collective-permute-start | bytes 1572872 | tf_op jit(solution)/shard_map/ppermute | solution.py:55
  80.9 0.0 collective-permute-done.9.rest_6_
  80.9 0.0 collective-permute-start.14
  80.9 0.0 collective-permute-done.11.rest_8_
  80.9 0.0 copy-start.5
  80.9 0.8 copy-done.5
  81.7 0.5 collective-permute-start.15
  82.2 0.0 collective-permute-done.12.rest_9_
  82.2 0.8 copy-done.7
  83.0 0.0 collective-permute-start.16
  83.0 0.7 pad_add_fusion.me
  83.7 3.8 %prepare.1 = (f32[34,64,128]{2,1,0:T(8,128)}, f32[32,64,128]{2,1,0:T(8,128)}, bf16[1024,768]{1,0:T(8,128)(2,1)}) custom-call(s32[4]{0:T(128)} %pad_add_fusion.me, f32[9,128,128]{2,1,0:T(8,128)} %taps.1, f32[40,64]{1,0:T(8,128)} %get-tuple-element.23.code, s32[2,32,64]{2,1,0:T(8,128)} %syndromes.5, s32[2,8,16]{2,1,0:T(8,128)} %erased.7, f32[2,128]{1,0:T(2,128)} %table.3, ...), custom_call_target="tpu_custom_call" | custom-call | tf_op jit(solution)/shard_map/prepare/pallas_call | solution.py:497
  87.5 0.0 copy-done.1
  87.5 0.0 copy-done.14
  87.5 0.0 copy-done.15
  87.5 0.0 copy-start
  87.5 0.0 copy-start.2
  87.6 0.0 copy-start.10
  87.6 0.0 copy-start.11
  87.6 6.3 %conv_first.1 = (f32[40,72,128]{2,1,0:T(8,128)}, f32[36,72,128]{2,1,0:T(8,128)}, s32[16,128]{1,0:T(8,128)}) custom-call(s32[4]{0:T(128)} %pad_add_fusion.me, f32[32,64,128]{2,1,0:T(8,128)} %state.5, f32[5,64,128]{2,1,0:T(8,128)} %copy-done.12, f32[5,64,128]{2,1,0:T(8,128)} %copy-done.13, f32[40,8,128]{2,1,0:T(8,128)} %copy-done.14, ...), custom_call_target="tpu_custom_call" | custom-call | flops 2000000000 | bytes 6000000 | tf_op jit(solution)/shard_map/conv_first/pallas_call | solution.py:507
  93.9 0.0 collective-permute-done.13.rest_10_
  93.9 0.0 collective-permute-done.14.rest_11_
  93.9 0.0 collective-permute-done.15.rest_12_
  93.9 0.0 collective-permute-done.16.rest_13_
  93.9 0.0 collective-permute-done.10.rest_7_
  93.9 0.0 copy-done
  94.0 1.0 copy-done.4
  95.0 1.0 copy-done.6
  96.0 1.0 copy-done.8
  97.1 0.7 copy-done.9
  97.8 10.8 %read_and_finish.1 = f32[32,64,128]{2,1,0:T(8,128)} custom-call(s32[16,128]{1,0:T(8,128)S(1)} %copy-done.9, s32[4]{0:T(128)S(1)} %copy-done.10, f32[1,128]{1,0:T(1,128)S(1)} %bitcast.5, f32[40,72,128]{2,1,0:T(8,128)} %get-tuple-element.29.ext_hbm, f32[36,72,128]{2,1,0:T(8,128)} %get-tuple-element.30.pre_hbm, f32[32,64,128]{2,1,0:T(8,128)S(1)} %copy-done, ...), custom_call_target="tpu_custom_call" | custom-call | flops 4000000000 | bytes 12000000 | tf_op jit(solution)/shard_map/read_and_finish/pallas_call | solution.py:520
  (15 shorter events, 0.0 us)
Async XLA Ops:
  3.0 9.3 %copy-start.17 = (f32[5,64,128]{2,1,0:T(8,128)S(1)}, f32[5,64,128]{2,1,0:T(8,128)}, u32[]{:S(2)}) copy-start(f32[5,64,128]{2,1,0:T(8,128)} %get-tuple-element.19) | copy-start | bytes 491524
  3.1 24.9 %all-to-all-start = ((f32[16,128,128]{2,1,0:T(8,128)}), f32[16,128,128]{2,1,0:T(8,128)S(1)}, u32[]{:S(2)}, u32[]{:S(2)}) async-start(f32[16,128,128]{2,1,0:T(8,128)} %get-tuple-element.32), calls=%async_computation | async-start | bytes 2097152 | tf_op jit(solution)/shard_map/all_to_all | solution.py:48
  12.3 20.3 %copy-start.16 = (f32[5,64,128]{2,1,0:T(8,128)S(1)}, f32[5,64,128]{2,1,0:T(8,128)}, u32[]{:S(2)}) copy-start(f32[5,64,128]{2,1,0:T(8,128)} %get-tuple-element.20) | copy-start | bytes 491524
  12.3 20.3 %collective-permute-start = (f32[5,64,128]{2,1,0:T(8,128)S(1)}, f32[5,64,128]{2,1,0:T(8,128)S(1)}, u32[]{:S(2)}, u32[]{:S(2)}) collective-permute-start(f32[5,64,128]{2,1,0:T(8,128)S(1)} %copy-done.17), channel_id=1, source_target_pairs={{0,8},{8,16},{16,24},{24,32},{32,40},{40,48},{48,56},{56,64},{64,7... | collective-permute-start | bytes 491528 | tf_op jit(solution)/shard_map/ppermute | solution.py:473
  29.0 36.8 %collective-permute-start.4 = (f32[8,128,128]{2,1,0:T(8,128)}, f32[8,128,128]{2,1,0:T(8,128)S(1)}, u32[]{:S(2)}, u32[]{:S(2)}) collective-permute-start(f32[8,128,128]{2,1,0:T(8,128)} %get-tuple-element.34), channel_id=1, source_target_pairs={{0,2},{1,3},{2,4},{3,5},{4,6},{5,7},{6,0},{7,1},{8,10},{9,11},{10,... | collective-permute-start | bytes 1572872 | tf_op jit(solution)/shard_map/ppermute | solution.py:53
  30.0 37.7 %collective-permute-start.5 = (f32[8,128,128]{2,1,0:T(8,128)}, f32[8,128,128]{2,1,0:T(8,128)S(1)}, u32[]{:S(2)}, u32[]{:S(2)}) collective-permute-start(f32[8,128,128]{2,1,0:T(8,128)} %get-tuple-element.33), channel_id=1, source_target_pairs={{0,6},{1,7},{2,0},{3,1},{4,2},{5,3},{6,4},{7,5},{8,14},{9,15},{10,... | collective-permute-start | bytes 1572872 | tf_op jit(solution)/shard_map/ppermute | solution.py:54
  30.5 38.9 %collective-permute-start.6 = (f32[8,128,128]{2,1,0:T(8,128)}, f32[8,128,128]{2,1,0:T(8,128)}, u32[]{:S(2)}, u32[]{:S(2)}) collective-permute-start(f32[8,128,128]{2,1,0:T(8,128)} %get-tuple-element.34), channel_id=1, source_target_pairs={{0,8},{1,9},{2,10},{3,11},{4,12},{5,13},{6,14},{7,15},{8,16},{9,17... | collective-permute-start | bytes 1572872 | tf_op jit(solution)/shard_map/ppermute | solution.py:53
  32.6 37.7 %collective-permute-start.7 = (f32[8,128,128]{2,1,0:T(8,128)}, f32[8,128,128]{2,1,0:T(8,128)}, u32[]{:S(2)}, u32[]{:S(2)}) collective-permute-start(f32[8,128,128]{2,1,0:T(8,128)} %get-tuple-element.33), channel_id=1, source_target_pairs={{0,24},{1,25},{2,26},{3,27},{4,28},{5,29},{6,30},{7,31},{8,0},{9,1... | collective-permute-start | bytes 1572872 | tf_op jit(solution)/shard_map/ppermute | solution.py:54
  32.6 14.4 %copy-start.12 = (f32[5,64,128]{2,1,0:T(8,128)}, f32[5,64,128]{2,1,0:T(8,128)S(1)}, u32[]{:S(2)}) copy-start(f32[5,64,128]{2,1,0:T(8,128)S(1)} %collective-permute-done.top) | copy-start | bytes 491524
  32.6 14.4 %collective-permute-start.1 = (f32[5,64,128]{2,1,0:T(8,128)S(1)}, f32[5,64,128]{2,1,0:T(8,128)S(1)}, u32[]{:S(2)}, u32[]{:S(2)}) collective-permute-start(f32[5,64,128]{2,1,0:T(8,128)S(1)} %copy-done.16), channel_id=1, source_target_pairs={{8,0},{16,8},{24,16},{32,24},{40,32},{48,40},{56,48},{64,56},{72,6... | collective-permute-start | bytes 491528 | tf_op jit(solution)/shard_map/ppermute | solution.py:474
  47.0 0.7 copy-start.13
  50.1 10.4 %collective-permute-start.2 = (f32[40,8,128]{2,1,0:T(8,128)}, f32[40,8,128]{2,1,0:T(8,128)S(1)}, u32[]{:S(2)}, u32[]{:S(2)}) collective-permute-start(f32[40,8,128]{2,1,0:T(8,128)} %get-tuple-element.21), channel_id=1, source_target_pairs={{1,0},{2,1},{3,2},{4,3},{5,4},{6,5},{7,6},{9,8},{10,9},{11,10},{12... | collective-permute-start | bytes 491528 | tf_op jit(solution)/shard_map/ppermute | solution.py:494
  60.6 27.0 %copy-start.14 = (f32[40,8,128]{2,1,0:T(8,128)}, f32[40,8,128]{2,1,0:T(8,128)S(1)}, u32[]{:S(2)}) copy-start(f32[40,8,128]{2,1,0:T(8,128)S(1)} %collective-permute-done.2.right) | copy-start | bytes 491524
  60.6 4.5 %collective-permute-start.3 = (f32[40,8,128]{2,1,0:T(8,128)}, f32[40,8,128]{2,1,0:T(8,128)S(1)}, u32[]{:S(2)}, u32[]{:S(2)}) collective-permute-start(f32[40,8,128]{2,1,0:T(8,128)} %get-tuple-element.22), channel_id=1, source_target_pairs={{0,1},{1,2},{2,3},{3,4},{4,5},{5,6},{6,7},{8,9},{9,10},{10,11},{11... | collective-permute-start | bytes 491528 | tf_op jit(solution)/shard_map/ppermute | solution.py:493
  65.0 22.5 %copy-start.15 = (f32[40,8,128]{2,1,0:T(8,128)}, f32[40,8,128]{2,1,0:T(8,128)S(1)}, u32[]{:S(2)}) copy-start(f32[40,8,128]{2,1,0:T(8,128)S(1)} %collective-permute-done.3.left) | copy-start | bytes 491524
  65.0 13.9 %collective-permute-start.8 = (f32[8,128,128]{2,1,0:T(8,128)}, f32[8,128,128]{2,1,0:T(8,128)}, u32[]{:S(2)}, u32[]{:S(2)}) collective-permute-start(f32[8,128,128]{2,1,0:T(8,128)} %get-tuple-element.34), channel_id=1, source_target_pairs={{0,32},{1,33},{2,34},{3,35},{4,36},{5,37},{6,38},{7,39},{8,40},{9,... | collective-permute-start | bytes 1572872 | tf_op jit(solution)/shard_map/ppermute | solution.py:53
  65.8 21.7 %copy-start.1 = (f32[8,128,128]{2,1,0:T(8,128)}, f32[8,128,128]{2,1,0:T(8,128)S(1)}, u32[]{:S(2)}) copy-start(f32[8,128,128]{2,1,0:T(8,128)S(1)} %collective-permute-done.4.rest_1_) | copy-start | bytes 1572868
  65.8 15.1 %collective-permute-start.9 = (f32[8,128,128]{2,1,0:T(8,128)}, f32[8,128,128]{2,1,0:T(8,128)}, u32[]{:S(2)}, u32[]{:S(2)}) collective-permute-start(f32[8,128,128]{2,1,0:T(8,128)} %get-tuple-element.33), channel_id=1, source_target_pairs={{0,96},{1,97},{2,98},{3,99},{4,100},{5,101},{6,102},{7,103},{8,104... | collective-permute-start | bytes 1572872 | tf_op jit(solution)/shard_map/ppermute | solution.py:54
  67.7 13.2 %collective-permute-start.11 = (f32[8,128,128]{2,1,0:T(8,128)S(1)}, f32[8,128,128]{2,1,0:T(8,128)S(1)}, u32[]{:S(2)}, u32[]{:S(2)}) collective-permute-start(f32[8,128,128]{2,1,0:T(8,128)S(1)} %collective-permute-done.4.rest_1_), channel_id=1, source_target_pairs={{0,1},{1,0},{2,3},{3,2},{4,5},{5,4},{6,7},{7,6},{8,9},{9,8},{10,11... | collective-permute-start | bytes 1572872 | tf_op jit(solution)/shard_map/ppermute | solution.py:55
  69.4 12.8 %collective-permute-start.12 = (f32[8,128,128]{2,1,0:T(8,128)S(1)}, f32[8,128,128]{2,1,0:T(8,128)S(1)}, u32[]{:S(2)}, u32[]{:S(2)}) collective-permute-start(f32[8,128,128]{2,1,0:T(8,128)S(1)} %collective-permute-done.5.rest_2_), channel_id=1, source_target_pairs={{0,1},{1,0},{2,3},{3,2},{4,5},{5,4},{6,7},{7,6},{8,9},{9,8},{10,11... | collective-permute-start | bytes 1572872 | tf_op jit(solution)/shard_map/ppermute | solution.py:55
  69.5 0.8 copy-start.3
  70.3 23.6 %collective-permute-start.10 = (f32[16,128,128]{2,1,0:T(8,128)S(1)}, f32[16,128,128]{2,1,0:T(8,128)S(1)}, u32[]{:S(2)}, u32[]{:S(2)}) collective-permute-start(f32[16,128,128]{2,1,0:T(8,128)S(1)} %all-to-all-done.rest_0_), channel_id=1, source_target_pairs={{0,1},{1,0},{2,3},{3,2},{4,5},{5,4},{6,7},{7,6},{8,9},{9,8},{10,11... | collective-permute-start | bytes 3145736 | tf_op jit(solution)/shard_map/ppermute | solution.py:55
  78.9 14.9 %collective-permute-start.13 = (f32[8,128,128]{2,1,0:T(8,128)}, f32[8,128,128]{2,1,0:T(8,128)}, u32[]{:S(2)}, u32[]{:S(2)}) collective-permute-start(f32[8,128,128]{2,1,0:T(8,128)} %collective-permute-done.6.rest_3_), channel_id=1, source_target_pairs={{0,1},{1,0},{2,3},{3,2},{4,5},{5,4},{6,7},{7,6},{8,9},{9,8},{10,11... | collective-permute-start | bytes 1572872 | tf_op jit(solution)/shard_map/ppermute | solution.py:55
  80.9 13.0 %collective-permute-start.14 = (f32[8,128,128]{2,1,0:T(8,128)}, f32[8,128,128]{2,1,0:T(8,128)}, u32[]{:S(2)}, u32[]{:S(2)}) collective-permute-start(f32[8,128,128]{2,1,0:T(8,128)} %collective-permute-done.7.rest_4_), channel_id=1, source_target_pairs={{0,1},{1,0},{2,3},{3,2},{4,5},{5,4},{6,7},{7,6},{8,9},{9,8},{10,11... | collective-permute-start | bytes 1572872 | tf_op jit(solution)/shard_map/ppermute | solution.py:55
  80.9 0.8 copy-start.5
  81.7 12.2 %collective-permute-start.15 = (f32[8,128,128]{2,1,0:T(8,128)}, f32[8,128,128]{2,1,0:T(8,128)}, u32[]{:S(2)}, u32[]{:S(2)}) collective-permute-start(f32[8,128,128]{2,1,0:T(8,128)} %collective-permute-done.8.rest_5_), channel_id=1, source_target_pairs={{0,1},{1,0},{2,3},{3,2},{4,5},{5,4},{6,7},{7,6},{8,9},{9,8},{10,11... | collective-permute-start | bytes 1572872 | tf_op jit(solution)/shard_map/ppermute | solution.py:55
  82.2 0.8 copy-start.7
  83.0 10.9 %collective-permute-start.16 = (f32[8,128,128]{2,1,0:T(8,128)}, f32[8,128,128]{2,1,0:T(8,128)}, u32[]{:S(2)}, u32[]{:S(2)}) collective-permute-start(f32[8,128,128]{2,1,0:T(8,128)} %collective-permute-done.9.rest_6_), channel_id=1, source_target_pairs={{0,1},{1,0},{2,3},{3,2},{4,5},{5,4},{6,7},{7,6},{8,9},{9,8},{10,11... | collective-permute-start | bytes 1572872 | tf_op jit(solution)/shard_map/ppermute | solution.py:55
  87.5 6.4 %copy-start = (f32[32,64,128]{2,1,0:T(8,128)S(1)}, f32[32,64,128]{2,1,0:T(8,128)}, u32[]{:S(2)}) copy-start(f32[32,64,128]{2,1,0:T(8,128)} %get-tuple-element.31.inputs_hbm) | copy-start | bytes 3145732
  87.5 6.4 %copy-start.2 = (f32[8,128,128]{2,1,0:T(8,128)S(1)}, f32[8,128,128]{2,1,0:T(8,128)}, u32[]{:S(2)}) copy-start(f32[8,128,128]{2,1,0:T(8,128)} %copy-done.1) | copy-start | bytes 1572868
  87.6 6.4 %copy-start.10 = (s32[4]{0:T(128)S(1)}, s32[4]{0:T(128)}, u32[]{:S(2)}) copy-start(s32[4]{0:T(128)} %pad_add_fusion.me) | copy-start | bytes 52
  87.6 6.4 %copy-start.11 = (f32[128]{0:T(128)S(1)}, f32[128]{0:T(128)}, u32[]{:S(2)}) copy-start(f32[128]{0:T(128)} %param.17) | copy-start | bytes 1540
  94.0 1.0 copy-start.4
  95.0 1.0 copy-start.6
  96.0 1.0 copy-start.8
  97.1 0.7 copy-start.9

commit v8 on v7

--- a/solution.py
+++ b/solution.py
@@ -52,8 +52,9 @@
         back = tuple(-s for s in step)
         pieces.append(lax.ppermute(low, AX, moved(*step)))
         pieces.append(lax.ppermute(high, AX, moved(*back)))
-    pieces += [lax.ppermute(piece, AX, PARTNER) for piece in pieces]
-    return pieces
+    swapped = [lax.ppermute(own, AX, PARTNER)]
+    swapped += [lax.ppermute(piece, AX, PARTNER) for piece in pieces[1:]]
+    return pieces + swapped
 
 
 def split(value):

time: 109 us -> 109 us (level)
  no operation moved by 1% of the time
where the time goes in v8:
time: 109 us
  waiting for transfers between devices  39.2 us (36%)
  starting transfers between devices  34.1 us (31%)
  Pallas kernels  26.4 us (24%)
  local copies, waits for them, and re-layouts  7.97 us (7%)
    ppermute x1, waiting for transfers between devices, decode(): bottom = lax.ppermute(up_pay, 'gx', up)  12.5 us
    all_to_all x1, waiting for transfers between devices, gather_weights(): lax.all_to_all(copies, AX, 0, 0, tiled=True, axis_index_groups=class_grou...  11.5 us
    pallas_call x1, Pallas kernels, decode(): pl.pallas_call(second_kernel, name='read_and_finish', compiler_params=plt...  10.8 us
    all_to_all x1, starting transfers between devices, gather_weights(): lax.all_to_all(copies, AX, 0, 0, tiled=True, axis_index_groups=class_grou...  9.28 us
    ppermute x3, waiting for transfers between devices, gather_weights(): pieces.append(lax.ppermute(low, AX, moved(*step)))  8.22 us
    unnamed x36, local copies, waits for them, and re-layouts  6.89 us
    pallas_call x1, Pallas kernels, decode(): pl.pallas_call(first_kernel, name='conv_first', compiler_params=pltpu.Com...  6.31 us
    ppermute x1, starting transfers between devices, decode(): right = lax.ppermute(west_pay, 'gy', west)  5.97 us
  transfers between devices with their start and end apart: 18, of which 5 were waited for; matrix products, arithmetic and copies ran while one was open for 2% of the time, Pallas kernels for 12%

profile of v8, /device:TPU:27, one launch (start us, length us, event | category | flops | bytes accessed | tf_op | source)
XLA Modules:
  0.0 108.7 jit_solution(6525505833062061603)
XLA Ops:
  0.0 3.0 %pack_rows.1 = (f32[5,64,128]{2,1,0:T(8,128)}, f32[5,64,128]{2,1,0:T(8,128)}, f32[16,128,128]{2,1,0:T(8,128)}) custom-call(f32[32,64,128]{2,1,0:T(8,128)} %state.5, f32[128,128]{1,0:T(8,128)} %weight.1, s32[2,32,64]{2,1,0:T(8,128)} %syndromes.5, s32[2,8,16]{2,1,0:T(8,128)} %erased.7, s32[1,128]{1,0:T(1,128)} %bitcast.6), custom_call_target="tpu_custom_call" | custom-call | tf_op jit(solution)/shard_map/pack_rows/pallas_call | solution.py:459
  3.0 0.0 copy-start.17
  3.1 9.3 %all-to-all-start = ((f32[16,128,128]{2,1,0:T(8,128)}), f32[16,128,128]{2,1,0:T(8,128)S(1)}, u32[]{:S(2)}, u32[]{:S(2)}) async-start(f32[16,128,128]{2,1,0:T(8,128)} %get-tuple-element.32), calls=%async_computation | async-start | bytes 2097152 | tf_op jit(solution)/shard_map/all_to_all | solution.py:48
  12.3 0.0 copy-done.17
  12.3 4.1 %collective-permute-start = (f32[5,64,128]{2,1,0:T(8,128)S(1)}, f32[5,64,128]{2,1,0:T(8,128)S(1)}, u32[]{:S(2)}, u32[]{:S(2)}) collective-permute-start(f32[5,64,128]{2,1,0:T(8,128)S(1)} %copy-done.17), channel_id=1, source_target_pairs={{0,8},{8,16},{16,24},{24,32},{32,40},{40,48},{48,56},{56,64},{64,7... | collective-permute-start | bytes 491528 | tf_op jit(solution)/shard_map/ppermute | solution.py:474
  16.4 11.5 %all-to-all-done.rest_0_ = f32[16,128,128]{2,1,0:T(8,128)S(1)} async-done(((f32[16,128,128]{2,1,0:T(8,128)}), f32[16,128,128]{2,1,0:T(8,128)S(1)}, u32[]{:S(2)}, u32[]{:S(2)}) %all-to-all-start) | async-done | bytes 1048608 | tf_op jit(solution)/shard_map/all_to_all | solution.py:48
  27.9 1.1 fusion
  29.0 1.0 collective-permute-start.4
  30.0 0.4 collective-permute-start.5
  30.5 2.1 %collective-permute-start.6 = (f32[8,128,128]{2,1,0:T(8,128)}, f32[8,128,128]{2,1,0:T(8,128)}, u32[]{:S(2)}, u32[]{:S(2)}) collective-permute-start(f32[8,128,128]{2,1,0:T(8,128)} %get-tuple-element.34), channel_id=1, source_target_pairs={{0,8},{1,9},{2,10},{3,11},{4,12},{5,13},{6,14},{7,15},{8,16},{9,17... | collective-permute-start | bytes 1572872 | tf_op jit(solution)/shard_map/ppermute | solution.py:53
  32.6 0.0 collective-permute-start.7
  32.6 0.0 collective-permute-done.top
  32.6 0.0 copy-done.16
  32.6 1.9 %collective-permute-start.1 = (f32[5,64,128]{2,1,0:T(8,128)S(1)}, f32[5,64,128]{2,1,0:T(8,128)S(1)}, u32[]{:S(2)}, u32[]{:S(2)}) collective-permute-start(f32[5,64,128]{2,1,0:T(8,128)S(1)} %copy-done.16), channel_id=1, source_target_pairs={{8,0},{16,8},{24,16},{32,24},{40,32},{48,40},{56,48},{64,56},{72,6... | collective-permute-start | bytes 491528 | tf_op jit(solution)/shard_map/ppermute | solution.py:475
  34.5 12.5 %collective-permute-done.1.bottom = f32[5,64,128]{2,1,0:T(8,128)S(1)} collective-permute-done((f32[5,64,128]{2,1,0:T(8,128)S(1)}, f32[5,64,128]{2,1,0:T(8,128)S(1)}, u32[]{:S(2)}, u32[]{:S(2)}) %collective-permute-start.1) | collective-permute-done | bytes 163872 | tf_op jit(solution)/shard_map/ppermute | solution.py:475
  47.0 0.0 copy-done.12
  47.0 0.7 copy-done.13
  47.7 2.5 %pack_cols.1 = (f32[40,8,128]{2,1,0:T(8,128)}, f32[40,8,128]{2,1,0:T(8,128)}, f32[40,64]{1,0:T(8,128)}, f32[16,128]{1,0:T(8,128)}, f32[16,128]{1,0:T(8,128)}) custom-call(f32[32,64,128]{2,1,0:T(8,128)} %state.5, f32[5,64,128]{2,1,0:T(8,128)} %copy-done.12, f32[5,64,128]{2,1,0:T(8,128)} %copy-done.13, s32[2,32,64]{2,1,0:T(8,128)} %syndromes.5, ...), custom_call_target="tpu_custom_call" | custom-call | tf_op jit(solution)/shard_map/pack_cols/pallas_call | solution.py:477
  50.1 6.0 %collective-permute-start.2 = (f32[40,8,128]{2,1,0:T(8,128)}, f32[40,8,128]{2,1,0:T(8,128)S(1)}, u32[]{:S(2)}, u32[]{:S(2)}) collective-permute-start(f32[40,8,128]{2,1,0:T(8,128)} %get-tuple-element.21), channel_id=1, source_target_pairs={{1,0},{2,1},{3,2},{4,3},{5,4},{6,5},{7,6},{9,8},{10,9},{11,10},{12... | collective-permute-start | bytes 491528 | tf_op jit(solution)/shard_map/ppermute | solution.py:495
  56.1 4.5 %collective-permute-done.2.right = f32[40,8,128]{2,1,0:T(8,128)S(1)} collective-permute-done((f32[40,8,128]{2,1,0:T(8,128)}, f32[40,8,128]{2,1,0:T(8,128)S(1)}, u32[]{:S(2)}, u32[]{:S(2)}) %collective-permute-start.2) | collective-permute-done | bytes 163872 | tf_op jit(solution)/shard_map/ppermute | solution.py:495
  60.6 1.9 %collective-permute-start.3 = (f32[40,8,128]{2,1,0:T(8,128)}, f32[40,8,128]{2,1,0:T(8,128)S(1)}, u32[]{:S(2)}, u32[]{:S(2)}) collective-permute-start(f32[40,8,128]{2,1,0:T(8,128)} %get-tuple-element.22), channel_id=1, source_target_pairs={{0,1},{1,2},{2,3},{3,4},{4,5},{5,6},{6,7},{8,9},{9,10},{10,11},{11... | collective-permute-start | bytes 491528 | tf_op jit(solution)/shard_map/ppermute | solution.py:494
  62.5 2.6 %collective-permute-done.3.left = f32[40,8,128]{2,1,0:T(8,128)S(1)} collective-permute-done((f32[40,8,128]{2,1,0:T(8,128)}, f32[40,8,128]{2,1,0:T(8,128)S(1)}, u32[]{:S(2)}, u32[]{:S(2)}) %collective-permute-start.3) | collective-permute-done | bytes 163872 | tf_op jit(solution)/shard_map/ppermute | solution.py:494
  65.0 0.8 collective-permute-start.8
  65.8 0.0 collective-permute-done.4.rest_1_
  65.8 1.9 %collective-permute-start.9 = (f32[8,128,128]{2,1,0:T(8,128)}, f32[8,128,128]{2,1,0:T(8,128)}, u32[]{:S(2)}, u32[]{:S(2)}) collective-permute-start(f32[8,128,128]{2,1,0:T(8,128)} %get-tuple-element.33), channel_id=1, source_target_pairs={{0,96},{1,97},{2,98},{3,99},{4,100},{5,101},{6,102},{7,103},{8,104... | collective-permute-start | bytes 1572872 | tf_op jit(solution)/shard_map/ppermute | solution.py:54
  67.7 0.0 collective-permute-done.5.rest_2_
  67.7 1.7 %collective-permute-start.11 = (f32[8,128,128]{2,1,0:T(8,128)S(1)}, f32[8,128,128]{2,1,0:T(8,128)S(1)}, u32[]{:S(2)}, u32[]{:S(2)}) collective-permute-start(f32[8,128,128]{2,1,0:T(8,128)S(1)} %collective-permute-done.4.rest_1_), channel_id=1, source_target_pairs={{0,1},{1,0},{2,3},{3,2},{4,5},{5,4},{6,7},{7,6},{8,9},{9,8},{10,11... | collective-permute-start | bytes 1572872 | tf_op jit(solution)/shard_map/ppermute | solution.py:56
  69.4 0.0 collective-permute-done.6.rest_3_
  69.4 0.1 collective-permute-start.12
  69.5 0.8 copy-done.3
  70.3 0.0 collective-permute-done.7.rest_4_
  70.3 0.4 collective-permute-start.10
  70.7 8.2 %collective-permute-done.8.rest_5_ = f32[8,128,128]{2,1,0:T(8,128)} collective-permute-done((f32[8,128,128]{2,1,0:T(8,128)}, f32[8,128,128]{2,1,0:T(8,128)}, u32[]{:S(2)}, u32[]{:S(2)}) %collective-permute-start.8) | collective-permute-done | bytes 524320 | tf_op jit(solution)/shard_map/ppermute | solution.py:53
  78.9 2.0 %collective-permute-start.13 = (f32[8,128,128]{2,1,0:T(8,128)}, f32[8,128,128]{2,1,0:T(8,128)}, u32[]{:S(2)}, u32[]{:S(2)}) collective-permute-start(f32[8,128,128]{2,1,0:T(8,128)} %collective-permute-done.6.rest_3_), channel_id=1, source_target_pairs={{0,1},{1,0},{2,3},{3,2},{4,5},{5,4},{6,7},{7,6},{8,9},{9,8},{10,11... | collective-permute-start | bytes 1572872 | tf_op jit(solution)/shard_map/ppermute | solution.py:56
  80.9 0.0 collective-permute-done.9.rest_6_
  80.9 0.0 collective-permute-start.14
  80.9 0.0 collective-permute-done.11.rest_8_
  80.9 0.0 copy-start.5
  80.9 0.8 copy-done.5
  81.7 0.5 collective-permute-start.15
  82.2 0.0 collective-permute-done.12.rest_9_
  82.2 0.8 copy-done.7
  83.0 0.0 collective-permute-start.16
  83.0 0.7 pad_add_fusion.me
  83.7 3.8 %prepare.1 = (f32[34,64,128]{2,1,0:T(8,128)}, f32[32,64,128]{2,1,0:T(8,128)}, bf16[1024,768]{1,0:T(8,128)(2,1)}) custom-call(s32[4]{0:T(128)} %pad_add_fusion.me, f32[9,128,128]{2,1,0:T(8,128)} %taps.1, f32[40,64]{1,0:T(8,128)} %get-tuple-element.23.code, s32[2,32,64]{2,1,0:T(8,128)} %syndromes.5, s32[2,8,16]{2,1,0:T(8,128)} %erased.7, f32[2,128]{1,0:T(2,128)} %table.3, ...), custom_call_target="tpu_custom_call" | custom-call | tf_op jit(solution)/shard_map/prepare/pallas_call | solution.py:498
  87.5 0.0 copy-done.1
  87.5 0.0 copy-done.14
  87.5 0.0 copy-done.15
  87.5 0.0 copy-start
  87.5 0.0 copy-start.2
  87.6 0.0 copy-start.10
  87.6 0.0 copy-start.11
  87.6 6.3 %conv_first.1 = (f32[40,72,128]{2,1,0:T(8,128)}, f32[36,72,128]{2,1,0:T(8,128)}, s32[16,128]{1,0:T(8,128)}) custom-call(s32[4]{0:T(128)} %pad_add_fusion.me, f32[32,64,128]{2,1,0:T(8,128)} %state.5, f32[5,64,128]{2,1,0:T(8,128)} %copy-done.12, f32[5,64,128]{2,1,0:T(8,128)} %copy-done.13, f32[40,8,128]{2,1,0:T(8,128)} %copy-done.14, ...), custom_call_target="tpu_custom_call" | custom-call | flops 2000000000 | bytes 6000000 | tf_op jit(solution)/shard_map/conv_first/pallas_call | solution.py:508
  93.9 0.0 collective-permute-done.13.rest_10_
  93.9 0.0 collective-permute-done.14.rest_11_
  93.9 0.0 collective-permute-done.15.rest_12_
  93.9 0.0 collective-permute-done.16.rest_13_
  93.9 0.0 collective-permute-done.10.rest_7_
  93.9 0.0 copy-done
  94.0 1.0 copy-done.4
  95.0 1.0 copy-done.6
  96.0 1.0 copy-done.8
  97.1 0.7 copy-done.9
  97.8 10.8 %read_and_finish.1 = f32[32,64,128]{2,1,0:T(8,128)} custom-call(s32[16,128]{1,0:T(8,128)S(1)} %copy-done.9, s32[4]{0:T(128)S(1)} %copy-done.10, f32[1,128]{1,0:T(1,128)S(1)} %bitcast.5, f32[40,72,128]{2,1,0:T(8,128)} %get-tuple-element.29.ext_hbm, f32[36,72,128]{2,1,0:T(8,128)} %get-tuple-element.30.pre_hbm, f32[32,64,128]{2,1,0:T(8,128)S(1)} %copy-done, ...), custom_call_target="tpu_custom_call" | custom-call | flops 4000000000 | bytes 12000000 | tf_op jit(solution)/shard_map/read_and_finish/pallas_call | solution.py:521
  (15 shorter events, 0.0 us)
Async XLA Ops:
  3.0 9.3 %copy-start.17 = (f32[5,64,128]{2,1,0:T(8,128)S(1)}, f32[5,64,128]{2,1,0:T(8,128)}, u32[]{:S(2)}) copy-start(f32[5,64,128]{2,1,0:T(8,128)} %get-tuple-element.19) | copy-start | bytes 491524
  3.1 24.9 %all-to-all-start = ((f32[16,128,128]{2,1,0:T(8,128)}), f32[16,128,128]{2,1,0:T(8,128)S(1)}, u32[]{:S(2)}, u32[]{:S(2)}) async-start(f32[16,128,128]{2,1,0:T(8,128)} %get-tuple-element.32), calls=%async_computation | async-start | bytes 2097152 | tf_op jit(solution)/shard_map/all_to_all | solution.py:48
  12.3 20.3 %copy-start.16 = (f32[5,64,128]{2,1,0:T(8,128)S(1)}, f32[5,64,128]{2,1,0:T(8,128)}, u32[]{:S(2)}) copy-start(f32[5,64,128]{2,1,0:T(8,128)} %get-tuple-element.20) | copy-start | bytes 491524
  12.3 20.3 %collective-permute-start = (f32[5,64,128]{2,1,0:T(8,128)S(1)}, f32[5,64,128]{2,1,0:T(8,128)S(1)}, u32[]{:S(2)}, u32[]{:S(2)}) collective-permute-start(f32[5,64,128]{2,1,0:T(8,128)S(1)} %copy-done.17), channel_id=1, source_target_pairs={{0,8},{8,16},{16,24},{24,32},{32,40},{40,48},{48,56},{56,64},{64,7... | collective-permute-start | bytes 491528 | tf_op jit(solution)/shard_map/ppermute | solution.py:474
  29.0 36.8 %collective-permute-start.4 = (f32[8,128,128]{2,1,0:T(8,128)}, f32[8,128,128]{2,1,0:T(8,128)S(1)}, u32[]{:S(2)}, u32[]{:S(2)}) collective-permute-start(f32[8,128,128]{2,1,0:T(8,128)} %get-tuple-element.34), channel_id=1, source_target_pairs={{0,2},{1,3},{2,4},{3,5},{4,6},{5,7},{6,0},{7,1},{8,10},{9,11},{10,... | collective-permute-start | bytes 1572872 | tf_op jit(solution)/shard_map/ppermute | solution.py:53
  30.0 37.7 %collective-permute-start.5 = (f32[8,128,128]{2,1,0:T(8,128)}, f32[8,128,128]{2,1,0:T(8,128)S(1)}, u32[]{:S(2)}, u32[]{:S(2)}) collective-permute-start(f32[8,128,128]{2,1,0:T(8,128)} %get-tuple-element.33), channel_id=1, source_target_pairs={{0,6},{1,7},{2,0},{3,1},{4,2},{5,3},{6,4},{7,5},{8,14},{9,15},{10,... | collective-permute-start | bytes 1572872 | tf_op jit(solution)/shard_map/ppermute | solution.py:54
  30.5 38.9 %collective-permute-start.6 = (f32[8,128,128]{2,1,0:T(8,128)}, f32[8,128,128]{2,1,0:T(8,128)}, u32[]{:S(2)}, u32[]{:S(2)}) collective-permute-start(f32[8,128,128]{2,1,0:T(8,128)} %get-tuple-element.34), channel_id=1, source_target_pairs={{0,8},{1,9},{2,10},{3,11},{4,12},{5,13},{6,14},{7,15},{8,16},{9,17... | collective-permute-start | bytes 1572872 | tf_op jit(solution)/shard_map/ppermute | solution.py:53
  32.6 37.7 %collective-permute-start.7 = (f32[8,128,128]{2,1,0:T(8,128)}, f32[8,128,128]{2,1,0:T(8,128)}, u32[]{:S(2)}, u32[]{:S(2)}) collective-permute-start(f32[8,128,128]{2,1,0:T(8,128)} %get-tuple-element.33), channel_id=1, source_target_pairs={{0,24},{1,25},{2,26},{3,27},{4,28},{5,29},{6,30},{7,31},{8,0},{9,1... | collective-permute-start | bytes 1572872 | tf_op jit(solution)/shard_map/ppermute | solution.py:54
  32.6 14.4 %copy-start.12 = (f32[5,64,128]{2,1,0:T(8,128)}, f32[5,64,128]{2,1,0:T(8,128)S(1)}, u32[]{:S(2)}) copy-start(f32[5,64,128]{2,1,0:T(8,128)S(1)} %collective-permute-done.top) | copy-start | bytes 491524
  32.6 14.4 %collective-permute-start.1 = (f32[5,64,128]{2,1,0:T(8,128)S(1)}, f32[5,64,128]{2,1,0:T(8,128)S(1)}, u32[]{:S(2)}, u32[]{:S(2)}) collective-permute-start(f32[5,64,128]{2,1,0:T(8,128)S(1)} %copy-done.16), channel_id=1, source_target_pairs={{8,0},{16,8},{24,16},{32,24},{40,32},{48,40},{56,48},{64,56},{72,6... | collective-permute-start | bytes 491528 | tf_op jit(solution)/shard_map/ppermute | solution.py:475
  47.0 0.7 copy-start.13
  50.1 10.4 %collective-permute-start.2 = (f32[40,8,128]{2,1,0:T(8,128)}, f32[40,8,128]{2,1,0:T(8,128)S(1)}, u32[]{:S(2)}, u32[]{:S(2)}) collective-permute-start(f32[40,8,128]{2,1,0:T(8,128)} %get-tuple-element.21), channel_id=1, source_target_pairs={{1,0},{2,1},{3,2},{4,3},{5,4},{6,5},{7,6},{9,8},{10,9},{11,10},{12... | collective-permute-start | bytes 491528 | tf_op jit(solution)/shard_map/ppermute | solution.py:495
  60.6 27.0 %copy-start.14 = (f32[40,8,128]{2,1,0:T(8,128)}, f32[40,8,128]{2,1,0:T(8,128)S(1)}, u32[]{:S(2)}) copy-start(f32[40,8,128]{2,1,0:T(8,128)S(1)} %collective-permute-done.2.right) | copy-start | bytes 491524
  60.6 4.5 %collective-permute-start.3 = (f32[40,8,128]{2,1,0:T(8,128)}, f32[40,8,128]{2,1,0:T(8,128)S(1)}, u32[]{:S(2)}, u32[]{:S(2)}) collective-permute-start(f32[40,8,128]{2,1,0:T(8,128)} %get-tuple-element.22), channel_id=1, source_target_pairs={{0,1},{1,2},{2,3},{3,4},{4,5},{5,6},{6,7},{8,9},{9,10},{10,11},{11... | collective-permute-start | bytes 491528 | tf_op jit(solution)/shard_map/ppermute | solution.py:494
  65.0 22.5 %copy-start.15 = (f32[40,8,128]{2,1,0:T(8,128)}, f32[40,8,128]{2,1,0:T(8,128)S(1)}, u32[]{:S(2)}) copy-start(f32[40,8,128]{2,1,0:T(8,128)S(1)} %collective-permute-done.3.left) | copy-start | bytes 491524
  65.0 13.9 %collective-permute-start.8 = (f32[8,128,128]{2,1,0:T(8,128)}, f32[8,128,128]{2,1,0:T(8,128)}, u32[]{:S(2)}, u32[]{:S(2)}) collective-permute-start(f32[8,128,128]{2,1,0:T(8,128)} %get-tuple-element.34), channel_id=1, source_target_pairs={{0,32},{1,33},{2,34},{3,35},{4,36},{5,37},{6,38},{7,39},{8,40},{9,... | collective-permute-start | bytes 1572872 | tf_op jit(solution)/shard_map/ppermute | solution.py:53
  65.8 21.7 %copy-start.1 = (f32[8,128,128]{2,1,0:T(8,128)}, f32[8,128,128]{2,1,0:T(8,128)S(1)}, u32[]{:S(2)}) copy-start(f32[8,128,128]{2,1,0:T(8,128)S(1)} %collective-permute-done.4.rest_1_) | copy-start | bytes 1572868
  65.8 15.1 %collective-permute-start.9 = (f32[8,128,128]{2,1,0:T(8,128)}, f32[8,128,128]{2,1,0:T(8,128)}, u32[]{:S(2)}, u32[]{:S(2)}) collective-permute-start(f32[8,128,128]{2,1,0:T(8,128)} %get-tuple-element.33), channel_id=1, source_target_pairs={{0,96},{1,97},{2,98},{3,99},{4,100},{5,101},{6,102},{7,103},{8,104... | collective-permute-start | bytes 1572872 | tf_op jit(solution)/shard_map/ppermute | solution.py:54
  67.7 13.2 %collective-permute-start.11 = (f32[8,128,128]{2,1,0:T(8,128)S(1)}, f32[8,128,128]{2,1,0:T(8,128)S(1)}, u32[]{:S(2)}, u32[]{:S(2)}) collective-permute-start(f32[8,128,128]{2,1,0:T(8,128)S(1)} %collective-permute-done.4.rest_1_), channel_id=1, source_target_pairs={{0,1},{1,0},{2,3},{3,2},{4,5},{5,4},{6,7},{7,6},{8,9},{9,8},{10,11... | collective-permute-start | bytes 1572872 | tf_op jit(solution)/shard_map/ppermute | solution.py:56
  69.4 12.8 %collective-permute-start.12 = (f32[8,128,128]{2,1,0:T(8,128)S(1)}, f32[8,128,128]{2,1,0:T(8,128)S(1)}, u32[]{:S(2)}, u32[]{:S(2)}) collective-permute-start(f32[8,128,128]{2,1,0:T(8,128)S(1)} %collective-permute-done.5.rest_2_), channel_id=1, source_target_pairs={{0,1},{1,0},{2,3},{3,2},{4,5},{5,4},{6,7},{7,6},{8,9},{9,8},{10,11... | collective-permute-start | bytes 1572872 | tf_op jit(solution)/shard_map/ppermute | solution.py:56
  69.5 0.8 copy-start.3
  70.3 23.6 %collective-permute-start.10 = (f32[16,128,128]{2,1,0:T(8,128)S(1)}, f32[16,128,128]{2,1,0:T(8,128)S(1)}, u32[]{:S(2)}, u32[]{:S(2)}) collective-permute-start(f32[16,128,128]{2,1,0:T(8,128)S(1)} %all-to-all-done.rest_0_), channel_id=1, source_target_pairs={{0,1},{1,0},{2,3},{3,2},{4,5},{5,4},{6,7},{7,6},{8,9},{9,8},{10,11... | collective-permute-start | bytes 3145736 | tf_op jit(solution)/shard_map/ppermute | solution.py:55
  78.9 14.9 %collective-permute-start.13 = (f32[8,128,128]{2,1,0:T(8,128)}, f32[8,128,128]{2,1,0:T(8,128)}, u32[]{:S(2)}, u32[]{:S(2)}) collective-permute-start(f32[8,128,128]{2,1,0:T(8,128)} %collective-permute-done.6.rest_3_), channel_id=1, source_target_pairs={{0,1},{1,0},{2,3},{3,2},{4,5},{5,4},{6,7},{7,6},{8,9},{9,8},{10,11... | collective-permute-start | bytes 1572872 | tf_op jit(solution)/shard_map/ppermute | solution.py:56
  80.9 13.0 %collective-permute-start.14 = (f32[8,128,128]{2,1,0:T(8,128)}, f32[8,128,128]{2,1,0:T(8,128)}, u32[]{:S(2)}, u32[]{:S(2)}) collective-permute-start(f32[8,128,128]{2,1,0:T(8,128)} %collective-permute-done.7.rest_4_), channel_id=1, source_target_pairs={{0,1},{1,0},{2,3},{3,2},{4,5},{5,4},{6,7},{7,6},{8,9},{9,8},{10,11... | collective-permute-start | bytes 1572872 | tf_op jit(solution)/shard_map/ppermute | solution.py:56
  80.9 0.8 copy-start.5
  81.7 12.2 %collective-permute-start.15 = (f32[8,128,128]{2,1,0:T(8,128)}, f32[8,128,128]{2,1,0:T(8,128)}, u32[]{:S(2)}, u32[]{:S(2)}) collective-permute-start(f32[8,128,128]{2,1,0:T(8,128)} %collective-permute-done.8.rest_5_), channel_id=1, source_target_pairs={{0,1},{1,0},{2,3},{3,2},{4,5},{5,4},{6,7},{7,6},{8,9},{9,8},{10,11... | collective-permute-start | bytes 1572872 | tf_op jit(solution)/shard_map/ppermute | solution.py:56
  82.2 0.8 copy-start.7
  83.0 10.9 %collective-permute-start.16 = (f32[8,128,128]{2,1,0:T(8,128)}, f32[8,128,128]{2,1,0:T(8,128)}, u32[]{:S(2)}, u32[]{:S(2)}) collective-permute-start(f32[8,128,128]{2,1,0:T(8,128)} %collective-permute-done.9.rest_6_), channel_id=1, source_target_pairs={{0,1},{1,0},{2,3},{3,2},{4,5},{5,4},{6,7},{7,6},{8,9},{9,8},{10,11... | collective-permute-start | bytes 1572872 | tf_op jit(solution)/shard_map/ppermute | solution.py:56
  87.5 6.4 %copy-start = (f32[32,64,128]{2,1,0:T(8,128)S(1)}, f32[32,64,128]{2,1,0:T(8,128)}, u32[]{:S(2)}) copy-start(f32[32,64,128]{2,1,0:T(8,128)} %get-tuple-element.31.inputs_hbm) | copy-start | bytes 3145732
  87.5 6.4 %copy-start.2 = (f32[8,128,128]{2,1,0:T(8,128)S(1)}, f32[8,128,128]{2,1,0:T(8,128)}, u32[]{:S(2)}) copy-start(f32[8,128,128]{2,1,0:T(8,128)} %copy-done.1) | copy-start | bytes 1572868
  87.6 6.4 %copy-start.10 = (s32[4]{0:T(128)S(1)}, s32[4]{0:T(128)}, u32[]{:S(2)}) copy-start(s32[4]{0:T(128)} %pad_add_fusion.me) | copy-start | bytes 52
  87.6 6.4 %copy-start.11 = (f32[128]{0:T(128)S(1)}, f32[128]{0:T(128)}, u32[]{:S(2)}) copy-start(f32[128]{0:T(128)} %param.17) | copy-start | bytes 1540
  94.0 1.0 copy-start.4
  95.0 1.0 copy-start.6
  96.0 1.0 copy-start.8
  97.1 0.7 copy-start.9
